TPU v7x, 32 devices: a whole 2x2x4 slice. The times are simulated.
32 devices in a mesh: dp: 4 (over y, x), seq: 8 (over z, core).
Axes of the slice: x: 2, y: 2, z: 4, core: 2. Of those that a mesh axis runs over, the one named last changes fastest.
Arguments:
- hidden: bfloat16 [8192, 1024], P(('dp', 'seq')), may hold values from -6 to 6
- encoder: bfloat16 [4096, 1024], P(('dp', 'seq')), may hold values from -6 to 6
- piece_starts: int32 [4, 2], P('dp'), may hold values from 0 to 1792, as said below
- grad_out: bfloat16 [8192, 1024], P(('dp', 'seq')), may hold values from -6 to 6
- attn_in: float32 [6, 1024, 1024], P(None, 'seq'), may hold values from -0.1875 to 0.1875
- attn_out: float32 [2, 1024, 1024], P(None, 'seq'), may hold values from -4 to 4
- ffn_in: float32 [1024, 8192], P('seq'), may hold values from -0.1875 to 0.1875
- ffn_out: float32 [8192, 1024], P('seq'), may hold values from -0.0625 to 0.0625
- norms: float32 [6, 1024], replicated, may hold values from -0.2 to 1.5, as said below
- first_attn_in: float32 [6, 1024, 1024], P(None, 'seq'), may hold values from -0.036 to 0.036
- first_attn_out: float32 [2, 1024, 1024], P(None, 'seq'), may hold values from -0.036 to 0.036
- first_ffn_in: float32 [1024, 8192], P('seq'), may hold values from -0.036 to 0.036
- first_ffn_out: float32 [8192, 1024], P('seq'), may hold values from -0.036 to 0.036
- first_norms: float32 [6, 1024], replicated, may hold values from -0.036 to 0.036
- second_attn_in: float32 [6, 1024, 1024], P(None, 'seq'), may hold values from 1e-05 to 0.001
- second_attn_out: float32 [2, 1024, 1024], P(None, 'seq'), may hold values from 1e-05 to 0.001
- second_ffn_in: float32 [1024, 8192], P('seq'), may hold values from 1e-05 to 0.001
- second_ffn_out: float32 [8192, 1024], P('seq'), may hold values from 1e-05 to 0.001
- second_norms: float32 [6, 1024], replicated, may hold values from 1e-05 to 0.001
Outputs:
- out_hidden: float32 [8192, 1024], P(('dp', 'seq'))
- grad_hidden: float32 [8192, 1024], P(('dp', 'seq'))
- grad_encoder: float32 [4096, 1024], P(('dp', 'seq'))
- grad_attn_in: float32 [6, 1024, 1024], P(None, 'seq')
- grad_attn_out: float32 [2, 1024, 1024], P(None, 'seq')
- grad_ffn_in: float32 [1024, 8192], P('seq')
- grad_ffn_out: float32 [8192, 1024], P('seq')
- grad_norms: float32 [6, 1024], replicated
- new_first_attn_in: float32 [6, 1024, 1024], P(None, 'seq')
- new_first_attn_out: float32 [2, 1024, 1024], P(None, 'seq')
- new_first_ffn_in: float32 [1024, 8192], P('seq')
- new_first_ffn_out: float32 [8192, 1024], P('seq')
- new_first_norms: float32 [6, 1024], replicated
- new_second_attn_in: float32 [6, 1024, 1024], P(None, 'seq')
- new_second_attn_out: float32 [2, 1024, 1024], P(None, 'seq')
- new_second_ffn_in: float32 [1024, 8192], P('seq')
- new_second_ffn_out: float32 [8192, 1024], P('seq')
- new_second_norms: float32 [6, 1024], replicated
- change_attn_in: float32 [6, 1024, 1024], P(None, 'seq')
- change_attn_out: float32 [2, 1024, 1024], P(None, 'seq')
- change_ffn_in: float32 [1024, 8192], P('seq')
- change_ffn_out: float32 [8192, 1024], P('seq')
- change_norms: float32 [6, 1024], replicated
Inputs may be any that keep to these rules, and one draw needn't show every extreme that they name: `piece_starts`: in each sequence the 2 starts rise, each piece of 256 tokens ends before the next one starts, and every piece lies inside the sequence. `norms`: rows 0, 2, 4 are gains, rows 1, 3, 5 biases.
All inputs are finite; a program needn't handle non-finite values.
Results may differ from a plain program's by a relative error of at most 0.025.
Values may be sent and summed in bfloat16 or wider, within the bound.
No kernel may reach another device: no remote copies, remote signals or barrier semaphores. Data moves between devices by JAX's collectives and lax.ppermute only.
A program may use at most 448 MiB of HBM per device.

v0:
```python
import math

import jax
import jax.numpy as jnp
from jax import lax
from jax.sharding import PartitionSpec as P

HEAD_DIM = 64
PIECE_LEN = 256


NORM_EPS = 1e-05
SCALE = 0.125
BETA_ONE = 0.9
BETA_TWO = 0.95
CORRECT_ONE = 1.0 - 0.9**8
CORRECT_TWO = 1.0 - 0.95**8
ADAM_EPS = 1e-08
RATE = 0.01
DECAY = 0.1
CLIP_RMS = 0.05
CLIP_EPS = 1e-06


def layer_norm(values_in, gain, shift):
    mean_val = jnp.mean(values_in, axis=-1, keepdims=True)
    centred = values_in - mean_val
    variance = jnp.mean(centred * centred, axis=-1, keepdims=True)
    return centred * lax.rsqrt(variance + NORM_EPS) * gain + shift


def piece_numbers(positions, starts):
    inside = (positions[:, None] >= starts[None, :]) & (
        positions[:, None] < starts[None, :] + PIECE_LEN
    )
    labels = jnp.arange(1, starts.shape[0] + 1, dtype=jnp.int32)
    return jnp.sum(jnp.where(inside, labels[None, :], 0), axis=1)


def soft_rows(query_head, key_head, visible):
    scores = (
        jnp.einsum("nd,kd->nk", query_head, key_head, preferred_element_type=jnp.float32) * SCALE
    )
    masked = jnp.where(visible, scores, -1e30)
    row_peak = jnp.max(masked, axis=1, keepdims=True)
    exp_terms = jnp.where(visible, jnp.exp(masked - row_peak), 0.0)
    row_total = jnp.sum(exp_terms, axis=1, keepdims=True)
    return (exp_terms / row_total, row_peak, row_total)


def soft_again(query_head, key_head, visible, row_peak, row_total):
    scores = (
        jnp.einsum("nd,kd->nk", query_head, key_head, preferred_element_type=jnp.float32) * SCALE
    )
    masked = jnp.where(visible, scores, -1e30)
    exp_terms = jnp.where(visible, jnp.exp(masked - row_peak), 0.0)
    return exp_terms / row_total


def attend_all(query_rows, key_rows, value_rows, visible):
    row_count = query_rows.shape[0]
    head_count = query_rows.shape[1] // HEAD_DIM

    def per_head(head_index, carry):
        outputs, peaks, totals = carry
        col_start = head_index * HEAD_DIM
        query_head = lax.dynamic_slice_in_dim(query_rows, col_start, HEAD_DIM, 1)
        key_head = lax.dynamic_slice_in_dim(key_rows, col_start, HEAD_DIM, 1)
        value_head = lax.dynamic_slice_in_dim(value_rows, col_start, HEAD_DIM, 1)
        soft_weights, row_peak, row_total = soft_rows(query_head, key_head, visible)
        head_out = jnp.dot(
            soft_weights.astype(jnp.bfloat16), value_head, preferred_element_type=jnp.float32
        )
        outputs = lax.dynamic_update_slice_in_dim(outputs, head_out, col_start, 1)
        peaks = lax.dynamic_update_slice_in_dim(peaks, row_peak[None], head_index, 0)
        totals = lax.dynamic_update_slice_in_dim(totals, row_total[None], head_index, 0)
        return (outputs, peaks, totals)

    start_state = (
        jnp.zeros((row_count, query_rows.shape[1]), jnp.float32),
        jnp.zeros((head_count, row_count, 1), jnp.float32),
        jnp.zeros((head_count, row_count, 1), jnp.float32),
    )
    return lax.fori_loop(0, head_count, per_head, start_state)


def attend_back(query_rows, key_rows, value_rows, visible, peaks, totals, grad_rows):
    head_count = query_rows.shape[1] // HEAD_DIM

    def per_head(head_index, carry):
        grad_query, grad_key, grad_value = carry
        col_start = head_index * HEAD_DIM
        query_head = lax.dynamic_slice_in_dim(query_rows, col_start, HEAD_DIM, 1)
        key_head = lax.dynamic_slice_in_dim(key_rows, col_start, HEAD_DIM, 1)
        value_head = lax.dynamic_slice_in_dim(value_rows, col_start, HEAD_DIM, 1)
        grad_head = lax.dynamic_slice_in_dim(grad_rows, col_start, HEAD_DIM, 1)
        soft_weights = soft_again(
            query_head, key_head, visible, peaks[head_index], totals[head_index]
        )
        grad_soft = jnp.einsum(
            "nd,kd->nk", grad_head, value_head, preferred_element_type=jnp.float32
        )
        value_part = jnp.einsum(
            "nk,nd->kd",
            soft_weights.astype(jnp.bfloat16),
            grad_head,
            preferred_element_type=jnp.float32,
        )
        grad_score = soft_weights * (
            grad_soft - jnp.sum(soft_weights * grad_soft, axis=1, keepdims=True)
        )
        grad_score = grad_score.astype(jnp.bfloat16)
        query_part = jnp.dot(grad_score, key_head, preferred_element_type=jnp.float32) * SCALE
        key_part = (
            jnp.einsum("nk,nd->kd", grad_score, query_head, preferred_element_type=jnp.float32)
            * SCALE
        )
        grad_query = lax.dynamic_update_slice_in_dim(grad_query, query_part, col_start, 1)
        grad_key = lax.dynamic_update_slice_in_dim(grad_key, key_part, col_start, 1)
        grad_value = lax.dynamic_update_slice_in_dim(grad_value, value_part, col_start, 1)
        return (grad_query, grad_key, grad_value)

    start_state = (
        jnp.zeros(query_rows.shape, jnp.float32),
        jnp.zeros(key_rows.shape, jnp.float32),
        jnp.zeros(value_rows.shape, jnp.float32),
    )
    return lax.fori_loop(0, head_count, per_head, start_state)


def left_product(left, right):
    return jnp.einsum("nd,ne->de", left, right, preferred_element_type=jnp.float32)


def right_product(left, weight):
    return jnp.einsum("ne,de->nd", left, weight, preferred_element_type=jnp.float32)


def clip_units(grad):
    mean_sq = jnp.mean(grad * grad, axis=-1, keepdims=True)
    return grad * jnp.minimum(1.0, CLIP_RMS * lax.rsqrt(mean_sq + CLIP_EPS))


def adam_update(weight, grad_sum, first_moment, second_moment):
    clipped = clip_units(grad_sum)
    first_new = BETA_ONE * first_moment + (1.0 - BETA_ONE) * clipped
    second_new = BETA_TWO * second_moment + (1.0 - BETA_TWO) * clipped * clipped
    step_size = first_new / CORRECT_ONE / (jnp.sqrt(second_new / CORRECT_TWO) + ADAM_EPS)
    return (first_new, second_new, -RATE * (step_size + DECAY * weight))


def gelu_tanh(values_in):
    return jax.nn.gelu(values_in, approximate=True)


def on_device(
    hidden,
    encoder,
    piece_starts,
    grad_out,
    attn_in,
    attn_out,
    ffn_in,
    ffn_out,
    norms,
    first_attn_in,
    first_attn_out,
    first_ffn_in,
    first_ffn_out,
    first_norms,
    second_attn_in,
    second_attn_out,
    second_ffn_in,
    second_ffn_out,
    second_norms,
):
    full = (
        lax.all_gather(attn_in.astype(jnp.bfloat16), "seq", axis=1, tiled=True),
        lax.all_gather(attn_out.astype(jnp.bfloat16), "seq", axis=1, tiled=True),
        lax.all_gather(ffn_in.astype(jnp.bfloat16), "seq", axis=0, tiled=True),
        lax.all_gather(ffn_out.astype(jnp.bfloat16), "seq", axis=0, tiled=True),
    )
    w_in, w_out, w_up, w_down = full
    gains = lax.optimization_barrier(norms.astype(jnp.bfloat16)).astype(jnp.float32)
    row_count = hidden.shape[0]
    seq_count = lax.axis_size("seq")
    group_count = lax.axis_size("dp")
    seq_total = row_count * seq_count
    query_pos = lax.axis_index("seq") * row_count + jnp.arange(row_count, dtype=jnp.int32)
    key_pos = jnp.arange(seq_total, dtype=jnp.int32)
    query_ids = piece_numbers(query_pos, piece_starts[0])
    key_ids = piece_numbers(key_pos, piece_starts[0])
    visible = (key_pos[None, :] <= query_pos[:, None]) | (
        key_ids[None, :] == query_ids[:, None]
    ) & (query_ids[:, None] > 0)
    resid_in = hidden.astype(jnp.float32)
    normed_one, norm_one_back = jax.vjp(layer_norm, resid_in, gains[0], gains[1])
    normed_one = normed_one.astype(jnp.bfloat16)
    query_rows = jnp.dot(normed_one, w_in[0], preferred_element_type=jnp.float32).astype(
        jnp.bfloat16
    )
    key_local = jnp.dot(normed_one, w_in[1], preferred_element_type=jnp.float32).astype(
        jnp.bfloat16
    )
    value_local = jnp.dot(normed_one, w_in[2], preferred_element_type=jnp.float32).astype(
        jnp.bfloat16
    )
    key_rows, value_rows = (
        lax.all_gather(key_local, "seq", axis=0, tiled=True),
        lax.all_gather(value_local, "seq", axis=0, tiled=True),
    )
    attended, self_peaks, self_totals = attend_all(query_rows, key_rows, value_rows, visible)
    attended = attended.astype(jnp.bfloat16)
    first_sum = resid_in + jnp.dot(attended, w_out[0], preferred_element_type=jnp.float32)
    normed_two, norm_two_back = jax.vjp(layer_norm, first_sum, gains[2], gains[3])
    normed_two = normed_two.astype(jnp.bfloat16)
    cross_queries = jnp.dot(normed_two, w_in[3], preferred_element_type=jnp.float32).astype(
        jnp.bfloat16
    )
    cross_key_local = jnp.dot(encoder, w_in[4], preferred_element_type=jnp.float32).astype(
        jnp.bfloat16
    )
    cross_value_local = jnp.dot(encoder, w_in[5], preferred_element_type=jnp.float32).astype(
        jnp.bfloat16
    )
    cross_keys, cross_values = (
        lax.all_gather(cross_key_local, "seq", axis=0, tiled=True),
        lax.all_gather(cross_value_local, "seq", axis=0, tiled=True),
    )
    everywhere = jnp.ones((row_count, cross_keys.shape[0]), dtype=jnp.bool_)
    crossed, cross_peaks, cross_totals = attend_all(
        cross_queries, cross_keys, cross_values, everywhere
    )
    crossed = crossed.astype(jnp.bfloat16)
    second_sum = first_sum + jnp.dot(crossed, w_out[1], preferred_element_type=jnp.float32)
    normed_three, norm_three_back = jax.vjp(layer_norm, second_sum, gains[4], gains[5])
    normed_three = normed_three.astype(jnp.bfloat16)
    pre_act = jnp.dot(normed_three, w_up, preferred_element_type=jnp.float32)
    activated, gelu_back = jax.vjp(gelu_tanh, pre_act)
    activated = activated.astype(jnp.bfloat16)
    out_hidden = second_sum + jnp.dot(activated, w_down, preferred_element_type=jnp.float32)
    top_grad = grad_out.astype(jnp.float32)
    grad_down = left_product(activated, grad_out)
    grad_act = right_product(grad_out, w_down)
    grad_pre = gelu_back(grad_act)[0].astype(jnp.bfloat16)
    grad_up = left_product(normed_three, grad_pre)
    grad_normed_three = right_product(grad_pre, w_up)
    norm_part, grad_gain_three, grad_shift_three = norm_three_back(grad_normed_three)
    grad_second = top_grad + norm_part
    grad_cross_branch = grad_second.astype(jnp.bfloat16)
    grad_cross_out = left_product(crossed, grad_cross_branch)
    grad_crossed = right_product(grad_cross_branch, w_out[1]).astype(jnp.bfloat16)
    grad_cq, grad_ck_all, grad_cv_all = attend_back(
        cross_queries, cross_keys, cross_values, everywhere, cross_peaks, cross_totals, grad_crossed
    )
    grad_cq = grad_cq.astype(jnp.bfloat16)
    grad_ck, grad_cv = (
        lax.psum_scatter(
            grad_ck_all.astype(jnp.bfloat16), "seq", scatter_dimension=0, tiled=True
        ).astype(jnp.float32),
        lax.psum_scatter(
            grad_cv_all.astype(jnp.bfloat16), "seq", scatter_dimension=0, tiled=True
        ).astype(jnp.float32),
    )
    grad_ck = grad_ck.astype(jnp.bfloat16)
    grad_cv = grad_cv.astype(jnp.bfloat16)
    grad_w_cq = left_product(normed_two, grad_cq)
    grad_w_ck = left_product(encoder, grad_ck)
    grad_w_cv = left_product(encoder, grad_cv)
    grad_encoder = right_product(grad_ck, w_in[4]) + right_product(grad_cv, w_in[5])
    grad_normed_two = right_product(grad_cq, w_in[3])
    norm_part, grad_gain_two, grad_shift_two = norm_two_back(grad_normed_two)
    grad_first = grad_second + norm_part
    grad_self_branch = grad_first.astype(jnp.bfloat16)
    grad_self_out = left_product(attended, grad_self_branch)
    grad_attended = right_product(grad_self_branch, w_out[0]).astype(jnp.bfloat16)
    back_keys, back_values = (
        lax.all_gather(key_local, "seq", axis=0, tiled=True),
        lax.all_gather(value_local, "seq", axis=0, tiled=True),
    )
    grad_query, grad_key_all, grad_value_all = attend_back(
        query_rows, back_keys, back_values, visible, self_peaks, self_totals, grad_attended
    )
    grad_query = grad_query.astype(jnp.bfloat16)
    grad_key, grad_value = (
        lax.psum_scatter(
            grad_key_all.astype(jnp.bfloat16), "seq", scatter_dimension=0, tiled=True
        ).astype(jnp.float32),
        lax.psum_scatter(
            grad_value_all.astype(jnp.bfloat16), "seq", scatter_dimension=0, tiled=True
        ).astype(jnp.float32),
    )
    grad_key = grad_key.astype(jnp.bfloat16)
    grad_value = grad_value.astype(jnp.bfloat16)
    grad_w_q = left_product(normed_one, grad_query)
    grad_w_k = left_product(normed_one, grad_key)
    grad_w_v = left_product(normed_one, grad_value)
    grad_normed_one = (
        right_product(grad_query, w_in[0])
        + right_product(grad_key, w_in[1])
        + right_product(grad_value, w_in[2])
    )
    norm_part, grad_gain_one, grad_shift_one = norm_one_back(grad_normed_one)
    grad_hidden = grad_first + norm_part
    grad_scale = 1.0 / math.sqrt(seq_total * group_count)
    sum_in = jnp.stack([grad_w_q, grad_w_k, grad_w_v, grad_w_cq, grad_w_ck, grad_w_cv]) * grad_scale
    sum_out = jnp.stack([grad_self_out, grad_cross_out]) * grad_scale
    sum_up = grad_up * grad_scale
    sum_down = grad_down * grad_scale
    sum_norms = (
        jnp.stack(
            [
                grad_gain_one,
                grad_shift_one,
                grad_gain_two,
                grad_shift_two,
                grad_gain_three,
                grad_shift_three,
            ]
        )
        * grad_scale
    )
    norm_total = lax.psum(sum_norms, ("dp", "seq"))
    owned = (
        lax.psum_scatter(
            sum_in.astype(jnp.bfloat16), "seq", scatter_dimension=1, tiled=True
        ).astype(jnp.float32),
        lax.psum_scatter(
            sum_out.astype(jnp.bfloat16), "seq", scatter_dimension=1, tiled=True
        ).astype(jnp.float32),
        lax.psum_scatter(
            sum_up.astype(jnp.bfloat16), "seq", scatter_dimension=0, tiled=True
        ).astype(jnp.float32),
        lax.psum_scatter(
            sum_down.astype(jnp.bfloat16), "seq", scatter_dimension=0, tiled=True
        ).astype(jnp.float32),
    )
    owned = (
        lax.psum(owned[0].astype(jnp.bfloat16), "dp").astype(jnp.float32),
        lax.psum(owned[1].astype(jnp.bfloat16), "dp").astype(jnp.float32),
        lax.psum(owned[2].astype(jnp.bfloat16), "dp").astype(jnp.float32),
        lax.psum(owned[3].astype(jnp.bfloat16), "dp").astype(jnp.float32),
    )
    upd_in = adam_update(attn_in, owned[0], first_attn_in, second_attn_in)
    upd_out = adam_update(attn_out, owned[1], first_attn_out, second_attn_out)
    upd_up = adam_update(ffn_in, owned[2], first_ffn_in, second_ffn_in)
    upd_down = adam_update(ffn_out, owned[3], first_ffn_out, second_ffn_out)
    upd_norms = adam_update(norms, norm_total, first_norms, second_norms)
    return (
        out_hidden,
        grad_hidden,
        grad_encoder,
        owned[0],
        owned[1],
        owned[2],
        owned[3],
        norm_total,
        upd_in[0],
        upd_out[0],
        upd_up[0],
        upd_down[0],
        upd_norms[0],
        upd_in[1],
        upd_out[1],
        upd_up[1],
        upd_down[1],
        upd_norms[1],
        upd_in[2],
        upd_out[2],
        upd_up[2],
        upd_down[2],
        upd_norms[2],
    )


def solution(mesh):
    placed = (
        P(("dp", "seq"), None),
        P(("dp", "seq"), None),
        P("dp", None),
        P(("dp", "seq"), None),
        P(None, "seq", None),
        P(None, "seq", None),
        P("seq", None),
        P("seq", None),
        P(),
        P(None, "seq", None),
        P(None, "seq", None),
        P("seq", None),
        P("seq", None),
        P(),
        P(None, "seq", None),
        P(None, "seq", None),
        P("seq", None),
        P("seq", None),
        P(),
    )
    return jax.shard_map(
        on_device,
        mesh=mesh,
        in_specs=placed,
        out_specs=(
            P(("dp", "seq"), None),
            P(("dp", "seq"), None),
            P(("dp", "seq"), None),
            P(None, "seq", None),
            P(None, "seq", None),
            P("seq", None),
            P("seq", None),
            P(),
            P(None, "seq", None),
            P(None, "seq", None),
            P("seq", None),
            P("seq", None),
            P(),
            P(None, "seq", None),
            P(None, "seq", None),
            P("seq", None),
            P("seq", None),
            P(),
            P(None, "seq", None),
            P(None, "seq", None),
            P("seq", None),
            P("seq", None),
            P(),
        ),
        check_vma=False,
    )
```

profile of v0, /device:TPU:0, one launch (start us, length us, event | category | flops | bytes accessed | tf_op | source)
XLA Modules:
  0.0 1882.8 jit_solution(12469954555190141828)
XLA Ops:
  11.3 119.0 %all-gather.9.cloned.1.call-done = bf16[6,1024,1024]{2,1,0:T(8,128)(2,1)} async-done(((bf16[6,128,1024]{2,1,0:T(8,128)(2,1)}), bf16[6,1024,1024]{2,1,0:T(8,128)(2,1)}) %all-gather.9.cloned.1.call-update) | async-done | bytes 12582928 | tf_op jit(solution)/shard_map/all_gather | solution.py:178
  154.1 25.0 %all-gather.11.cloned.1.call-done = bf16[2048,1024]{1,0:T(8,128)(2,1)} async-done(((bf16[256,1024]{1,0:T(8,128)(2,1)}), bf16[2048,1024]{1,0:T(8,128)(2,1)}) %all-gather.11.cloned.1.call-update) | async-done | bytes 4194320 | tf_op jit(solution)/shard_map/all_gather | solution.py:209
  179.1 47.9 %all-gather.13.cloned.1.call-done = bf16[2048,1024]{1,0:T(8,128)(2,1)} async-done(((bf16[256,1024]{1,0:T(8,128)(2,1)}), bf16[2048,1024]{1,0:T(8,128)(2,1)}) %all-gather.13.cloned.1.call-update) | async-done | bytes 4194320 | tf_op jit(solution)/shard_map/all_gather | solution.py:210
  227.1 88.7 %while.72 = (s32[]{:T(128)}, bf16[256,1024]{0,1:T(8,128)(2,1)S(1)}, f32[16,256,1]{1,2,0:T(1,128)S(1)}, f32[16,256,1]{1,2,0:T(1,128)S(1)}, bf16[256,1024]{1,0:T(8...) while((s32[]{:T(128)}, bf16[256,1024]{0,1:T(8,128)(2,1)S(1)}, ...), condition=%wide.region_7.8_spmd.clone, body=%wide.region_4.7_spmd.clone.sunk | while | flops 145751552 | bytes 7514567 | solution.py:84
  321.7 13.8 all-gather.19.cloned.1.call-done
  335.6 51.6 %while.70 = (s32[]{:T(128)}, bf16[256,1024]{0,1:T(8,128)(2,1)S(1)}, f32[16,256,1]{1,2,0:T(1,128)S(1)}, f32[16,256,1]{1,2,0:T(1,128)S(1)}, bf16[256,1024]{1,0:T(8...) while((s32[]{:T(128)}, bf16[256,1024]{0,1:T(8,128)(2,1)S(1)}, ...), condition=%wide.region_13.14_spmd, body=%wide.region_10.13_spmd.sunk | while | flops 68943360 | bytes 3812519 | solution.py:84
  390.7 97.7 %all-gather.23.cloned.1.call-done = bf16[8192,1024]{1,0:T(8,128)(2,1)} async-done(((bf16[1024,1024]{1,0:T(8,128)(2,1)}), bf16[8192,1024]{1,0:T(8,128)(2,1)}) %all-gather.23.cloned.1.call-update) | async-done | bytes 16777232 | tf_op jit(solution)/shard_map/all_gather | solution.py:181
  488.4 14.6 fusion.152
  502.9 137.0 %all-gather.21.cloned.1.call-done = bf16[1024,8192]{1,0:T(8,128)(2,1)} async-done(((bf16[128,8192]{1,0:T(8,128)(2,1)}), bf16[1024,8192]{1,0:T(8,128)(2,1)}) %all-gather.21.cloned.1.call-update) | async-done | bytes 16777232 | tf_op jit(solution)/shard_map/all_gather | solution.py:180
  639.9 17.4 fusion.69
  657.4 13.3 multiply_reduce_fusion.6
  680.2 140.8 %while.71 = (s32[]{:T(128)}, bf16[256,1024]{0,1:T(8,128)(2,1)}, bf16[1024,1024]{0,1:T(8,128)(2,1)}, bf16[1024,1024]{0,1:T(8,128)(2,1)}, bf16[256,1024]{1,0:T(8,1...) while((s32[]{:T(128)}, bf16[256,1024]{0,1:T(8,128)(2,1)}, ...), condition=%wide.region_20.21_spmd, body=%wide.region_18.20_spmd.sunk | while | flops 170213120 | bytes 9516223 | solution.py:128
  834.0 171.4 %while.73 = (s32[]{:T(128)}, bf16[256,1024]{0,1:T(8,128)(2,1)}, bf16[2048,1024]{0,1:T(8,128)(2,1)}, bf16[2048,1024]{0,1:T(8,128)(2,1)}, bf16[256,1024]{1,0:T(8,1...) while((s32[]{:T(128)}, bf16[256,1024]{0,1:T(8,128)(2,1)}, ...), condition=%wide.region_25.26_spmd.clone, body=%wide.region_23.25_spmd.clone.sunk | while | flops 343555840 | bytes 18701792 | solution.py:128
  1023.3 30.5 %reduce-scatter.13.cloned.1.call-done = bf16[256,1024]{0,1:T(8,128)(2,1)} async-done(((bf16[2048,1024]{0,1:T(8,128)(2,1)}), bf16[256,1024]{0,1:T(8,128)(2,1)}) %reduce-scatter.13.cloned.1.call-update) | async-done | bytes 524304 | tf_op jit(solution)/shard_map/reduce_scatter | solution.py:286
  1057.8 46.9 %reduce-scatter.15.cloned.1.call-done = bf16[256,1024]{0,1:T(8,128)(2,1)} async-done(((bf16[2048,1024]{0,1:T(8,128)(2,1)}), bf16[256,1024]{0,1:T(8,128)(2,1)}) %reduce-scatter.15.cloned.1.call-update) | async-done | bytes 524304 | tf_op jit(solution)/shard_map/reduce_scatter | solution.py:289
  1111.4 30.1 %reduce-scatter.25.cloned.1.call-done = bf16[128,1024]{1,0:T(8,128)(2,1)} async-done(((bf16[1024,1024]{1,0:T(8,128)(2,1)}), bf16[128,1024]{1,0:T(8,128)(2,1)}) %reduce-scatter.25.cloned.1.call-update) | async-done | bytes 262160
  1145.2 33.6 %reduce-scatter.27.cloned.1.call-done = bf16[128,1024]{1,0:T(8,128)(2,1)} async-done(((bf16[1024,1024]{1,0:T(8,128)(2,1)}), bf16[128,1024]{1,0:T(8,128)(2,1)}) %reduce-scatter.27.cloned.1.call-update) | async-done | bytes 262160
  1182.6 14.3 multiply_convert_fusion.4
  1230.4 129.5 %reduce-scatter.17.cloned.1.call-done = bf16[6,128,1024]{2,1,0:T(8,128)(2,1)} async-done(((bf16[6,1024,1024]{2,1,0:T(8,128)(2,1)}), bf16[6,128,1024]{2,1,0:T(8,128)(2,1)}) %reduce-scatter.17.cloned.1.call-update) | async-done | bytes 1572880 | tf_op jit(solution)/shard_map/reduce_scatter | solution.py:325
  1359.9 168.9 %reduce-scatter.21.cloned.1.call-done = bf16[128,8192]{1,0:T(8,128)(2,1)} async-done(((bf16[1024,8192]{1,0:T(8,128)(2,1)}), bf16[128,8192]{1,0:T(8,128)(2,1)}) %reduce-scatter.21.cloned.1.call-update) | async-done | bytes 2097168 | tf_op jit(solution)/shard_map/reduce_scatter | solution.py:331
  1528.8 168.8 %reduce-scatter.23.cloned.1.call-done = bf16[1024,1024]{1,0:T(8,128)(2,1)} async-done(((bf16[8192,1024]{1,0:T(8,128)(2,1)}), bf16[1024,1024]{1,0:T(8,128)(2,1)}) %reduce-scatter.23.cloned.1.call-update) | async-done | bytes 2097168 | tf_op jit(solution)/shard_map/reduce_scatter | solution.py:334
  1700.0 15.5 convolution_add_fusion
  1727.3 39.0 %psum.39 = f32[6,1024]{1,0:T(8,128)S(1)} all-reduce(f32[6,1024]{1,0:T(8,128)S(1)} %broadcast_multiply_fusion), channel_id=1, replica_groups=mesh['dp'=4,'seq'=8] {'dp','seq'}, use_global_device_ids=true, to_apply=%region_46.47 | all-reduce | flops 6144 | bytes 49152 | tf_op jit(solution)/shard_map/psum | solution.py:323
  1768.6 71.9 %all-reduce.3.cloned.1.call-done = (bf16[6,128,1024]{2,1,0:T(8,128)(2,1)}, bf16[2,128,1024]{2,1,0:T(8,128)(2,1)}, bf16[128,8192]{1,0:T(8,128)(2,1)}, bf16[1024,1024]{1,0:T(8,128)(2,1)}) async-done(((bf16[6,128,1024]{2,1,0:T(8,128)(2,1)}, bf16[2,128,1024]{2,1,0:T(8,128)(2,1)}, bf16[128,8192]{1,0:T(8,128)(2,1)}, bf16[1024,1024]{1,0:T(8,128)(2,1)}), (bf16[6,128,1024]{2,1,0:T(8,128)(2,1)}, ...) | async-done | bytes 6291472 | tf_op jit(solution)/shard_map/psum | solution.py:339
  (597 shorter events, 631.0 us)
Async XLA Ops:
  7.2 130.5 %copy-start = (bf16[128,1024]{1,0:T(8,128)(2,1)S(1)}, bf16[128,1024]{1,0:T(8,128)(2,1)}, u32[]{:S(2)}) copy-start(bf16[128,1024]{1,0:T(8,128)(2,1)} %param.28) | copy-start | bytes 786436
  7.2 123.0 %all-gather.9.cloned.1.call-start = ((), (), s32[]{:S(2)}) async-start(), calls=%async_computation.8 | async-start | bytes 14155776 | tf_op jit(solution)/shard_map/all_gather | solution.py:178
  10.7 168.5 %all-gather.11.cloned.1.call-start = ((), (), s32[]{:S(2)}) async-start(), calls=%async_computation.9 | async-start | bytes 4718592 | tf_op jit(solution)/shard_map/all_gather | solution.py:209
  10.9 140.8 %copy-start.47 = (f32[256]{0:T(256)}, f32[256]{0:T(256)S(1)}, u32[]{:S(2)}) copy-start(f32[256]{0:T(256)S(1)} %broadcast_multiply_fusion.3) | copy-start | bytes 3076
  11.2 119.1 %copy-start.53 = (f32[256]{0:T(256)}, f32[256]{0:T(256)S(1)}, u32[]{:S(2)}) copy-start(f32[256]{0:T(256)S(1)} %fusion.111) | copy-start | bytes 3076
  11.2 140.5 %copy-start.49 = (f32[256]{0:T(256)}, f32[256]{0:T(256)S(1)}, u32[]{:S(2)}) copy-start(f32[256]{0:T(256)S(1)} %fusion.128) | copy-start | bytes 3076
  11.3 140.5 %copy-start.41 = (f32[1,1024]{1,0:T(1,128)}, f32[1,1024]{1,0:T(1,128)S(1)}, u32[]{:S(2)}) copy-start(f32[1,1024]{1,0:T(1,128)S(1)} %get-tuple-element.866) | copy-start | bytes 12292
  11.3 140.5 %copy-start.45 = (f32[1,1024]{1,0:T(1,128)}, f32[1,1024]{1,0:T(1,128)S(1)}, u32[]{:S(2)}) copy-start(f32[1,1024]{1,0:T(1,128)S(1)} %get-tuple-element.867) | copy-start | bytes 12292
  133.4 93.6 %all-gather.13.cloned.1.call-start = ((), (), s32[]{:S(2)}) async-start(), calls=%async_computation.10 | async-start | bytes 4718592 | tf_op jit(solution)/shard_map/all_gather | solution.py:210
  136.7 179.1 %all-gather.15.cloned.1.call-start = ((), (), s32[]{:S(2)}) async-start(), calls=%async_computation.11 | async-start | bytes 4718592 | tf_op jit(solution)/shard_map/all_gather | solution.py:179
  137.7 184.0 %all-gather.17.cloned.1.call-start = ((), (), s32[]{:S(2)}) async-start(), calls=%async_computation.12 | async-start | bytes 2359296 | tf_op jit(solution)/shard_map/all_gather | solution.py:227
  140.6 194.9 %all-gather.19.cloned.1.call-start = ((), (), s32[]{:S(2)}) async-start(), calls=%async_computation.13 | async-start | bytes 2359296 | tf_op jit(solution)/shard_map/all_gather | solution.py:228
  143.4 344.9 %all-gather.23.cloned.1.call-start = ((), (), s32[]{:S(2)}) async-start(), calls=%async_computation.15 | async-start | bytes 18874368 | tf_op jit(solution)/shard_map/all_gather | solution.py:181
  147.4 492.6 %all-gather.21.cloned.1.call-start = ((), (), s32[]{:S(2)}) async-start(), calls=%async_computation.14 | async-start | bytes 18874368 | tf_op jit(solution)/shard_map/all_gather | solution.py:180
  151.2 902.5 %reduce-scatter.13.cloned.1.call-start = ((), (), s32[]{:S(2)}) async-start(), calls=%async_computation.16 | async-start | bytes 4718592 | tf_op jit(solution)/shard_map/reduce_scatter | solution.py:286
  1005.4 99.3 %reduce-scatter.15.cloned.1.call-start = ((), (), s32[]{:S(2)}) async-start(), calls=%async_computation.17 | async-start | bytes 4718592 | tf_op jit(solution)/shard_map/reduce_scatter | solution.py:289
  1006.0 135.5 %reduce-scatter.25.cloned.1.call-start = ((), (), s32[]{:S(2)}) async-start(), calls=%async_computation.22 | async-start | bytes 2359296
  1010.0 168.8 %reduce-scatter.27.cloned.1.call-start = ((), (), s32[]{:S(2)}) async-start(), calls=%async_computation.23 | async-start | bytes 2359296
  1014.0 216.4 %reduce-scatter.19.cloned.1.call-start = ((), (), s32[]{:S(2)}) async-start(), calls=%async_computation.19 | async-start | bytes 4718592 | tf_op jit(solution)/shard_map/reduce_scatter | solution.py:328
  1019.4 340.5 %reduce-scatter.17.cloned.1.call-start = ((), (), s32[]{:S(2)}) async-start(), calls=%async_computation.18 | async-start | bytes 14155776 | tf_op jit(solution)/shard_map/reduce_scatter | solution.py:325
  1196.9 331.9 %reduce-scatter.21.cloned.1.call-start = ((), (), s32[]{:S(2)}) async-start(), calls=%async_computation.20 | async-start | bytes 18874368 | tf_op jit(solution)/shard_map/reduce_scatter | solution.py:331
  1207.6 490.0 %reduce-scatter.23.cloned.1.call-start = ((), (), s32[]{:S(2)}) async-start(), calls=%async_computation.21 | async-start | bytes 18874368 | tf_op jit(solution)/shard_map/reduce_scatter | solution.py:334
  1221.6 618.9 %all-reduce.3.cloned.1.call-start = ((), (), s32[]{:S(2)}) async-start(), calls=%async_computation.24 | async-start | bytes 12582912 | tf_op jit(solution)/shard_map/psum | solution.py:339
  1766.3 76.1 %copy-start.38 = (f32[6,1024]{1,0:T(8,128)}, f32[6,1024]{1,0:T(8,128)S(1)}, u32[]{:S(2)}) copy-start(f32[6,1024]{1,0:T(8,128)S(1)} %psum.39) | copy-start | bytes 73732
  (51 other events, 410.5 us)
Sparse Core Ops, SparseCore 0:
  10.8 119.4 all-gather.8
  133.5 45.5 all-gather.10
  181.3 45.6 all-gather.12
  229.0 45.8 all-gather.14
  276.9 27.8 all-gather.16
  306.8 28.6 all-gather.18
  337.7 150.6 all-gather.22
  490.5 149.3 all-gather.20
  1005.5 48.2 reduce-scatter.12
  1056.5 48.1 reduce-scatter.14
  1107.5 33.9 reduce-scatter.24
  1144.2 34.5 reduce-scatter.26
  1181.6 48.6 reduce-scatter.18
  1232.5 127.3 reduce-scatter.16
  1362.1 166.6 reduce-scatter.20
  1531.0 166.5 reduce-scatter.22
  1701.2 139.2 all-reduce.2
where the time goes:
time: 1900 us; the launch traced here: 1880 us
  waiting for transfers between devices  1130 us (59%)
  matrix products  571 us (30%)
  other arithmetic  91.3 us (5%)
  blocking collectives  39 us (2%)
  local copies, waits for them, and re-layouts  33.5 us (2%)
    reduce_scatter x1, waiting for transfers between devices, on_device(): lax.psum_scatter(sum_up.astype(jnp.bfloat16), 'seq', scatter_dimension=0,...  169 us
    reduce_scatter x1, waiting for transfers between devices, on_device(): lax.psum_scatter(sum_down.astype(jnp.bfloat16), 'seq', scatter_dimension=...  169 us
    all_gather x1, waiting for transfers between devices, on_device(): lax.all_gather(ffn_in.astype(jnp.bfloat16), 'seq', axis=0, tiled=True)  137 us
    reduce_scatter x1, waiting for transfers between devices, on_device(): lax.psum_scatter(sum_in.astype(jnp.bfloat16), 'seq', scatter_dimension=1,...  130 us
    all_gather x1, waiting for transfers between devices, on_device(): lax.all_gather(attn_in.astype(jnp.bfloat16), 'seq', axis=1, tiled=True)  119 us
    all_gather x1, waiting for transfers between devices, on_device(): lax.all_gather(ffn_out.astype(jnp.bfloat16), 'seq', axis=0, tiled=True)  97.7 us
    psum x1, waiting for transfers between devices, on_device(): lax.psum(owned[0].astype(jnp.bfloat16), 'dp').astype(jnp.float32)  71.9 us
    dot_general x32, matrix products, per_head(): jnp.dot(grad_score, key_head, preferred_element_type=jnp.float32) * SCALE  69.1 us
  transfers between devices with their start and end apart: 17, of which 15 were waited for; matrix products, arithmetic and copies ran while one was open for 15% of the time, Pallas kernels for 0%

commit v1 on v0

v1 whole, which is shorter than its diff:
```python
import functools
import math

import jax
import jax.numpy as jnp
from jax import lax
from jax.experimental import pallas as pl
from jax.experimental.pallas import tpu as pltpu
from jax.sharding import Mesh
from jax.sharding import PartitionSpec as P

HEAD_DIM = 64
PIECE_LEN = 256

NORM_EPS = 1e-05
SCALE = 0.125
BETA_ONE = 0.9
BETA_TWO = 0.95
CORRECT_ONE = 1.0 - 0.9**8
CORRECT_TWO = 1.0 - 0.95**8
ADAM_EPS = 1e-08
RATE = 0.01
DECAY = 0.1
CLIP_RMS = 0.05
CLIP_EPS = 1e-06
MASKED = -1e30

SEQ = ("chip", "core")
BF16 = jnp.bfloat16
F32 = jnp.float32
VMEM_LIMIT = 48 * 1024 * 1024
NT = (((1,), (1,)), ((), ()))
TN = (((0,), (0,)), ((), ()))


def layer_norm(values_in, gain, shift):
    mean_val = jnp.mean(values_in, axis=-1, keepdims=True)
    centred = values_in - mean_val
    variance = jnp.mean(centred * centred, axis=-1, keepdims=True)
    return centred * lax.rsqrt(variance + NORM_EPS) * gain + shift


def dot_f32(left, right):
    return jnp.dot(left, right, preferred_element_type=F32)


def dot_nt(left, right):
    return lax.dot_general(left, right, NT, preferred_element_type=F32)


def dot_tn(left, right):
    return lax.dot_general(left, right, TN, preferred_element_type=F32)


def key_limit(positions, starts_ref, pieces):
    limit = positions + 1
    for piece in range(pieces):
        start = starts_ref[0, piece]
        inside = (positions >= start) & (positions < start + PIECE_LEN)
        limit = jnp.where(inside, jnp.maximum(limit, start + PIECE_LEN), limit)
    return limit


def spills_over(boundary, starts_ref, pieces):
    over = jnp.bool_(False)
    for piece in range(pieces):
        start = starts_ref[0, piece]
        over = over | ((start < boundary) & (start + PIECE_LEN > boundary))
    return over


def self_fwd_kernel(heads, pieces, block, starts_ref, q_ref, k_ref, v_ref, o_ref, lse_ref, s_ref):
    step = pl.program_id(0)
    last = pl.num_programs(0) - 1
    row_pos = step * block + lax.broadcasted_iota(jnp.int32, (block, 1), 0)
    limit = key_limit(row_pos, starts_ref, pieces)
    over = spills_over((step + 1) * block, starts_ref, pieces) & (step < last)
    blocks = step + 1 + over.astype(jnp.int32)
    for head in range(heads):
        cols = slice(head * HEAD_DIM, (head + 1) * HEAD_DIM)
        query = q_ref[:, cols] * BF16(SCALE)

        def scores(index):
            rows = pl.ds(pl.multiple_of(index * block, block), block)
            return dot_nt(query, k_ref[rows, cols])

        def masked_scores(index):
            key_pos = index * block + lax.broadcasted_iota(jnp.int32, (1, block), 1)
            return jnp.where(key_pos < limit, scores(index), MASKED)

        def lane_max(peak, values):
            for at in range(0, block, 128):
                peak = jnp.maximum(peak, values[:, at : at + 128])
            return peak

        def first_pass(index, peak):
            values = scores(index)
            s_ref[index] = values
            return lane_max(peak, values)

        def edge_pass(index, peak):
            values = masked_scores(index)
            s_ref[index] = values
            return lane_max(peak, values)

        peak = jnp.full((block, 128), MASKED, F32)
        peak = lax.fori_loop(0, step, first_pass, peak)
        peak = lax.fori_loop(step, blocks, edge_pass, peak)
        peak = jnp.max(peak, axis=1, keepdims=True)

        def second_pass(index, carry):
            total, out = carry
            terms = jnp.exp(s_ref[index] - peak)
            for at in range(0, block, 128):
                total = total + terms[:, at : at + 128]
            rows = pl.ds(pl.multiple_of(index * block, block), block)
            return total, out + dot_f32(terms.astype(BF16), v_ref[rows, cols])

        total, out = lax.fori_loop(
            0,
            blocks,
            second_pass,
            (jnp.zeros((block, 128), F32), jnp.zeros((block, HEAD_DIM), F32)),
        )
        total = jnp.sum(total, axis=1, keepdims=True)
        o_ref[:, cols] = (out / total).astype(BF16)
        lse = jnp.broadcast_to(peak + jnp.log(total), (block, 128))
        lse_ref[head] = jnp.transpose(lse)[:8]


def self_forward(starts, query, key, value, block):
    tokens, width = query.shape
    heads = width // HEAD_DIM
    pieces = starts.shape[1]
    whole = pl.BlockSpec((tokens, width), lambda i, s: (0, 0))
    flops = 2 * 2 * heads * tokens * tokens * HEAD_DIM
    return pl.pallas_call(
        functools.partial(self_fwd_kernel, heads, pieces, block),
        out_shape=(
            jax.ShapeDtypeStruct((tokens, width), BF16),
            jax.ShapeDtypeStruct((heads, 8, tokens), F32),
        ),
        grid_spec=pltpu.PrefetchScalarGridSpec(
            num_scalar_prefetch=1,
            grid=(tokens // block,),
            in_specs=[pl.BlockSpec((block, width), lambda i, s: (i, 0)), whole, whole],
            out_specs=(
                pl.BlockSpec((block, width), lambda i, s: (i, 0)),
                pl.BlockSpec((heads, 8, block), lambda i, s: (0, 0, i)),
            ),
            scratch_shapes=[pltpu.VMEM((tokens // block, block, block), F32)],
        ),
        compiler_params=pltpu.CompilerParams(
            dimension_semantics=("arbitrary",), vmem_limit_bytes=VMEM_LIMIT
        ),
        cost_estimate=pl.CostEstimate(
            flops=flops, bytes_accessed=8 * tokens * width, transcendentals=heads * tokens * tokens
        ),
        name="self_forward",
    )(starts, query, key, value)


def self_bwd_kernel(
    heads,
    pieces,
    block,
    starts_ref,
    q_ref,
    k_ref,
    v_ref,
    o_ref,
    do_ref,
    lse_ref,
    dq_ref,
    dk_ref,
    dv_ref,
    dk_acc,
    dv_acc,
):
    step = pl.program_id(0)
    last = pl.num_programs(0) - 1

    @pl.when(step == 0)
    def _():
        dk_acc[...] = jnp.zeros_like(dk_acc)
        dv_acc[...] = jnp.zeros_like(dv_acc)

    col_pos = step * block + lax.broadcasted_iota(jnp.int32, (1, block), 1)
    limit = key_limit(col_pos, starts_ref, pieces)
    over = spills_over((step + 1) * block, starts_ref, pieces) & (step < last)
    blocks = step + 1 + over.astype(jnp.int32)
    for head in range(heads):
        cols = slice(head * HEAD_DIM, (head + 1) * HEAD_DIM)
        query = q_ref[:, cols] * BF16(SCALE)
        grad = do_ref[:, cols]
        product = grad.astype(F32) * o_ref[:, cols].astype(F32)
        delta = lax.dot_general(
            jnp.ones((8, HEAD_DIM), F32),
            product,
            NT,
            precision=lax.Precision.HIGHEST,
            preferred_element_type=F32,
        )[:1]
        lse = lse_ref[head][:1]

        def one_block(masked, index, dq):
            rows = pl.ds(pl.multiple_of(index * block, block), block)
            key = k_ref[rows, cols]
            scores = dot_nt(key, query)
            if masked:
                key_pos = index * block + lax.broadcasted_iota(jnp.int32, (block, 1), 0)
                scores = jnp.where(key_pos < limit, scores, MASKED)
            weights = jnp.exp(scores - lse)
            grad_weights = dot_nt(v_ref[rows, cols], grad)
            dv_acc[rows, cols] += dot_f32(weights.astype(BF16), grad)
            grad_scores = (weights * (grad_weights - delta)).astype(BF16)
            dk_acc[rows, cols] += dot_f32(grad_scores, query)
            return dq + dot_tn(grad_scores, key)

        dq = jnp.zeros((block, HEAD_DIM), F32)
        dq = lax.fori_loop(0, step, functools.partial(one_block, False), dq)
        dq = lax.fori_loop(step, blocks, functools.partial(one_block, True), dq)
        dq_ref[:, cols] = (dq * SCALE).astype(BF16)

    @pl.when(step == last)
    def _():
        dk_ref[...] = dk_acc[...].astype(BF16)
        dv_ref[...] = dv_acc[...].astype(BF16)


def self_backward(starts, query, key, value, out, grad, lse, block):
    tokens, width = query.shape
    heads = width // HEAD_DIM
    pieces = starts.shape[1]
    whole = pl.BlockSpec((tokens, width), lambda i, s: (0, 0))
    rows = pl.BlockSpec((block, width), lambda i, s: (i, 0))
    flops = 5 * 2 * heads * tokens * tokens * HEAD_DIM
    shape = jax.ShapeDtypeStruct((tokens, width), BF16)
    return pl.pallas_call(
        functools.partial(self_bwd_kernel, heads, pieces, block),
        out_shape=(shape, shape, shape),
        grid_spec=pltpu.PrefetchScalarGridSpec(
            num_scalar_prefetch=1,
            grid=(tokens // block,),
            in_specs=[
                rows,
                whole,
                whole,
                rows,
                rows,
                pl.BlockSpec((heads, 8, block), lambda i, s: (0, 0, i)),
            ],
            out_specs=(rows, whole, whole),
            scratch_shapes=[pltpu.VMEM((tokens, width), F32), pltpu.VMEM((tokens, width), F32)],
        ),
        compiler_params=pltpu.CompilerParams(
            dimension_semantics=("arbitrary",), vmem_limit_bytes=VMEM_LIMIT
        ),
        cost_estimate=pl.CostEstimate(
            flops=flops, bytes_accessed=16 * tokens * width, transcendentals=heads * tokens * tokens
        ),
        name="self_backward",
    )(starts, query, key, value, out, grad, lse)


def cross_fwd_kernel(q_ref, k_ref, v_ref, o_ref, lse_ref):
    rows = q_ref.shape[0]
    for head in range(q_ref.shape[1] // HEAD_DIM):
        cols = slice(head * HEAD_DIM, (head + 1) * HEAD_DIM)
        scores = dot_nt(q_ref[:, cols] * BF16(SCALE), k_ref[:, cols])
        peak = jnp.max(scores, axis=1, keepdims=True)
        terms = jnp.exp(scores - peak)
        total = jnp.sum(terms, axis=1, keepdims=True)
        o_ref[:, cols] = (dot_f32(terms.astype(BF16), v_ref[:, cols]) / total).astype(BF16)
        lse = jnp.broadcast_to(peak + jnp.log(total), (rows, 128))
        lse_ref[head] = jnp.transpose(lse)[:8]


def cross_forward(query, key_value):
    rows, width = query.shape
    keys = key_value.shape[1]
    heads = width // HEAD_DIM
    return pl.pallas_call(
        lambda q, k, v, o, lse: cross_fwd_kernel(q, k, v, o, lse),
        out_shape=(
            jax.ShapeDtypeStruct((rows, width), BF16),
            jax.ShapeDtypeStruct((heads, 8, rows), F32),
        ),
        grid=(width // 128,),
        in_specs=[
            pl.BlockSpec((rows, 128), lambda i: (0, i)),
            pl.BlockSpec((None, keys, 128), lambda i: (0, 0, i)),
            pl.BlockSpec((None, keys, 128), lambda i: (1, 0, i)),
        ],
        out_specs=(
            pl.BlockSpec((rows, 128), lambda i: (0, i)),
            pl.BlockSpec((2, 8, rows), lambda i: (i, 0, 0)),
        ),
        compiler_params=pltpu.CompilerParams(
            dimension_semantics=("arbitrary",), vmem_limit_bytes=VMEM_LIMIT
        ),
        cost_estimate=pl.CostEstimate(
            flops=4 * rows * keys * width,
            bytes_accessed=4 * rows * width + 4 * keys * width,
            transcendentals=heads * rows * keys,
        ),
        name="cross_forward",
    )(query, key_value, key_value)


def cross_bwd_kernel(q_ref, k_ref, v_ref, o_ref, do_ref, lse_ref, dq_ref, dkv_ref):
    for head in range(q_ref.shape[1] // HEAD_DIM):
        cols = slice(head * HEAD_DIM, (head + 1) * HEAD_DIM)
        query = q_ref[:, cols] * BF16(SCALE)
        grad = do_ref[:, cols]
        product = grad.astype(F32) * o_ref[:, cols].astype(F32)
        delta = lax.dot_general(
            jnp.ones((8, HEAD_DIM), F32),
            product,
            NT,
            precision=lax.Precision.HIGHEST,
            preferred_element_type=F32,
        )[:1]
        key = k_ref[:, cols]
        weights = jnp.exp(dot_nt(key, query) - lse_ref[head][:1])
        grad_weights = dot_nt(v_ref[:, cols], grad)
        dkv_ref[1, :, cols] = dot_f32(weights.astype(BF16), grad).astype(BF16)
        grad_scores = (weights * (grad_weights - delta)).astype(BF16)
        dkv_ref[0, :, cols] = dot_f32(grad_scores, query).astype(BF16)
        dq_ref[:, cols] = (dot_tn(grad_scores, key) * SCALE).astype(BF16)


def cross_backward(query, key_value, out, grad, lse):
    rows, width = query.shape
    keys = key_value.shape[1]
    heads = width // HEAD_DIM
    rows_spec = pl.BlockSpec((rows, 128), lambda i: (0, i))
    return pl.pallas_call(
        lambda *refs: cross_bwd_kernel(*refs),
        out_shape=(
            jax.ShapeDtypeStruct((rows, width), BF16),
            jax.ShapeDtypeStruct((2, keys, width), BF16),
        ),
        grid=(width // 128,),
        in_specs=[
            rows_spec,
            pl.BlockSpec((None, keys, 128), lambda i: (0, 0, i)),
            pl.BlockSpec((None, keys, 128), lambda i: (1, 0, i)),
            rows_spec,
            rows_spec,
            pl.BlockSpec((2, 8, rows), lambda i: (i, 0, 0)),
        ],
        out_specs=(rows_spec, pl.BlockSpec((2, keys, 128), lambda i: (0, 0, i))),
        compiler_params=pltpu.CompilerParams(
            dimension_semantics=("arbitrary",), vmem_limit_bytes=VMEM_LIMIT
        ),
        cost_estimate=pl.CostEstimate(
            flops=10 * rows * keys * width,
            bytes_accessed=8 * rows * width + 8 * keys * width,
            transcendentals=heads * rows * keys,
        ),
        name="cross_backward",
    )(query, key_value, key_value, out, grad, lse)


def dp_swap(values, offset):
    count = lax.axis_size("dp")
    return lax.ppermute(values, "dp", [(index, index ^ offset) for index in range(count)])


def dp_gather(values):
    return [values] + [dp_swap(values, k) for k in range(1, lax.axis_size("dp"))]


def dp_scatter(blocks):
    total = blocks[0]
    for k in range(1, len(blocks)):
        total = total + dp_swap(blocks[k].astype(BF16), k).astype(F32)
    return total


def dp_join(values):
    copies = jnp.broadcast_to(values[None], (lax.axis_size("dp"),) + values.shape)
    return lax.all_to_all(copies, "dp", split_axis=0, concat_axis=0, tiled=True)


def own_part(values, axis):
    return lax.dynamic_index_in_dim(values, lax.axis_index("dp"), axis, keepdims=False)


def clip_units(grad):
    mean_sq = jnp.mean(grad * grad, axis=-1, keepdims=True)
    return grad * jnp.minimum(1.0, CLIP_RMS * lax.rsqrt(mean_sq + CLIP_EPS))


def adam_update(weight, grad_sum, first_moment, second_moment):
    clipped = clip_units(grad_sum)
    first_new = BETA_ONE * first_moment + (1.0 - BETA_ONE) * clipped
    second_new = BETA_TWO * second_moment + (1.0 - BETA_TWO) * clipped * clipped
    step_size = first_new / CORRECT_ONE / (jnp.sqrt(second_new / CORRECT_TWO) + ADAM_EPS)
    return (first_new, second_new, -RATE * (step_size + DECAY * weight))


def gelu_both(values_in):
    root = math.sqrt(2.0 / math.pi)
    square = values_in * values_in
    bent = jnp.tanh(root * (values_in + 0.044715 * values_in * square))
    half = 0.5 * (1.0 + bent)
    slope = half + 0.5 * values_in * (1.0 - bent * bent) * root * (1.0 + 3.0 * 0.044715 * square)
    return values_in * half, slope


def on_device(
    hidden,
    encoder,
    piece_starts,
    grad_out,
    attn_in,
    attn_out,
    ffn_in,
    ffn_out,
    norms,
    first_attn_in,
    first_attn_out,
    first_ffn_in,
    first_ffn_out,
    first_norms,
    second_attn_in,
    second_attn_out,
    second_ffn_in,
    second_ffn_out,
    second_norms,
):
    groups = lax.axis_size("dp")
    shards = lax.axis_size("chip") * lax.axis_size("core")
    rows, model = hidden.shape
    tokens = rows * shards
    width = model // shards
    shard_rows = attn_in.shape[1]
    part_rows = shard_rows // groups
    hidden_units = ffn_in.shape[1]
    unit_cut = hidden_units // (shards * groups)
    block = min(512, tokens)

    gains = lax.optimization_barrier(norms.astype(BF16)).astype(F32)
    resid_in = hidden.astype(F32)
    normed_one, norm_one_back = jax.vjp(layer_norm, resid_in, gains[0], gains[1])
    normed_one = normed_one.astype(BF16)
    normed_all = lax.all_gather(normed_one, SEQ, axis=0, tiled=True)

    to_heads = attn_in[:3].astype(BF16).reshape(3, shard_rows, shards, width)
    to_heads = lax.all_to_all(to_heads, SEQ, split_axis=2, concat_axis=1, tiled=True)
    to_heads = to_heads.reshape(3, model, width)

    def row_part(weights):
        cut = weights.reshape(weights.shape[0], groups, part_rows, model)
        return own_part(cut, 1).astype(BF16)

    early = jnp.concatenate([row_part(attn_out), row_part(attn_in[3:])], axis=0)
    early = lax.all_gather(early, SEQ + ("dp",), axis=1, tiled=True)
    w_o, w_co, w_cq, w_ck, w_cv = [early[index] for index in range(5)]
    encoder_all = lax.all_gather(encoder, SEQ, axis=0, tiled=True)

    up = own_part(ffn_in.reshape(shard_rows, shards, groups, unit_cut), 2)
    up = up.reshape(shard_rows, shards * unit_cut).astype(BF16)
    w_up = lax.all_gather(up, SEQ, axis=0, tiled=True)
    down = own_part(ffn_out.reshape(groups, unit_cut, model), 0).astype(BF16)
    w_down = lax.all_gather(down, SEQ, axis=0, tiled=True)
    late = row_part(attn_in[:3])
    late = lax.all_gather(late, SEQ + ("dp",), axis=1, tiled=True)

    qkv = dot_f32(normed_all, jnp.concatenate([to_heads[i] for i in range(3)], axis=1))
    qkv = qkv.astype(BF16)
    query, key, value = [qkv[:, i * width : (i + 1) * width] for i in range(3)]
    out_heads, self_lse = self_forward(piece_starts, query, key, value, block)
    attended = lax.all_to_all(
        out_heads.reshape(shards, rows, width), SEQ, split_axis=0, concat_axis=0, tiled=True
    )
    attended = attended.transpose(1, 0, 2).reshape(rows, model)
    first_sum = resid_in + dot_f32(attended, w_o)

    normed_two, norm_two_back = jax.vjp(layer_norm, first_sum, gains[2], gains[3])
    normed_two = normed_two.astype(BF16)
    cross_queries = dot_f32(normed_two, w_cq).astype(BF16)
    cross_kv = jnp.stack([dot_f32(encoder_all, w_ck), dot_f32(encoder_all, w_cv)]).astype(BF16)
    crossed, cross_lse = cross_forward(cross_queries, cross_kv)
    second_sum = first_sum + dot_f32(crossed, w_co)

    normed_three, norm_three_back = jax.vjp(layer_norm, second_sum, gains[4], gains[5])
    normed_three = normed_three.astype(BF16)
    grad_tokens = jnp.concatenate(dp_gather(grad_out), axis=0)
    ffn_tokens = jnp.concatenate(dp_gather(normed_three), axis=0)
    activated, slope = gelu_both(dot_f32(ffn_tokens, w_up))
    activated = activated.astype(BF16)
    grad_pre = (dot_nt(grad_tokens, w_down) * slope).astype(BF16)
    partial = dot_nt(grad_pre, w_up)
    grad_normed_three = dp_scatter(
        [partial[k * rows : (k + 1) * rows] for k in range(groups)]
    )
    partial = dot_f32(activated, w_down)
    out_hidden = second_sum + dp_scatter(
        [partial[k * rows : (k + 1) * rows] for k in range(groups)]
    )
    grad_down = dot_tn(activated, grad_tokens).astype(BF16)
    grad_up = dot_tn(ffn_tokens, grad_pre).astype(BF16)
    grad_down = lax.psum_scatter(grad_down, SEQ, scatter_dimension=0, tiled=True)
    grad_up = lax.psum_scatter(grad_up, SEQ, scatter_dimension=0, tiled=True)

    norm_part, grad_gain_three, grad_shift_three = norm_three_back(grad_normed_three)
    grad_second = grad_out.astype(F32) + norm_part
    grad_cross_branch = grad_second.astype(BF16)
    grad_w_co = dot_tn(crossed, grad_cross_branch)
    grad_crossed = dot_nt(grad_cross_branch, w_co).astype(BF16)
    grad_cq, grad_ckv = cross_backward(
        cross_queries, cross_kv, crossed, grad_crossed, cross_lse
    )
    grad_ckv = lax.psum_scatter(grad_ckv, SEQ, scatter_dimension=1, tiled=True)
    grad_w_cq = dot_tn(normed_two, grad_cq)
    norm_part, grad_gain_two, grad_shift_two = norm_two_back(dot_nt(grad_cq, w_cq))
    grad_first = grad_second + norm_part
    grad_self_branch = grad_first.astype(BF16)
    grad_attended = dot_nt(grad_self_branch, w_o).astype(BF16)
    grad_heads = lax.all_to_all(
        grad_attended.reshape(rows, shards, width).transpose(1, 0, 2),
        SEQ,
        split_axis=0,
        concat_axis=0,
        tiled=True,
    ).reshape(tokens, width)
    grad_w_o = dot_tn(attended, grad_self_branch)
    grad_q, grad_k, grad_v = self_backward(
        piece_starts, query, key, value, out_heads, grad_heads, self_lse, block
    )
    grad_qkv = jnp.stack([grad_q, grad_k, grad_v])
    grad_rows = lax.all_to_all(
        grad_qkv.reshape(3, shards, rows, width), SEQ, split_axis=1, concat_axis=1, tiled=True
    )
    grad_rows = grad_rows.transpose(0, 2, 1, 3).reshape(3, rows, model)
    grad_normed_one = (
        dot_nt(grad_rows[0], late[0]) + dot_nt(grad_rows[1], late[1]) + dot_nt(grad_rows[2], late[2])
    )
    norm_part, grad_gain_one, grad_shift_one = norm_one_back(grad_normed_one)
    grad_hidden = grad_first + norm_part

    grad_w_ck = dot_tn(encoder, grad_ckv[0])
    grad_w_cv = dot_tn(encoder, grad_ckv[1])
    grad_encoder = dot_nt(grad_ckv[0], w_ck) + dot_nt(grad_ckv[1], w_cv)

    index = lax.axis_index("dp")

    def dp_parts(grad):
        axis = grad.ndim - 3
        blocks = [
            lax.dynamic_index_in_dim(grad, index ^ k, axis, keepdims=False) for k in range(groups)
        ]
        return dp_scatter(blocks)

    local = jnp.stack([grad_w_o, grad_w_co, grad_w_cq, grad_w_ck, grad_w_cv])
    local = dp_parts(local.reshape(5, shards, groups, part_rows, model)).astype(BF16)
    local = local.reshape(5, shards * part_rows, model)
    local = lax.psum_scatter(local, SEQ, scatter_dimension=1, tiled=True)
    headed = dot_tn(normed_all, jnp.concatenate([grad_q, grad_k, grad_v], axis=1))
    headed = dp_parts(headed.reshape(shards, groups, part_rows, 3 * width)).astype(BF16)
    headed = lax.all_to_all(headed, SEQ, split_axis=0, concat_axis=0, tiled=True)
    headed = headed.reshape(shards, part_rows, 3, width).transpose(2, 1, 0, 3)
    headed = headed.reshape(3, part_rows, model)

    scale = 1.0 / math.sqrt(tokens * groups)
    local = dp_join(local)
    headed = dp_join(headed)

    def whole_rows(parts):
        return parts.transpose(1, 0, 2, 3).reshape(parts.shape[1], shard_rows, model)

    sum_out = whole_rows(local[:, :2]).astype(F32) * scale
    sum_in = (
        jnp.concatenate([whole_rows(headed), whole_rows(local[:, 2:])], axis=0).astype(F32) * scale
    )
    sum_down = dp_join(grad_down).reshape(groups * unit_cut, model).astype(F32) * scale
    sum_up = dp_join(grad_up.reshape(shard_rows, shards, unit_cut))
    sum_up = sum_up.transpose(1, 2, 0, 3).reshape(shard_rows, hidden_units).astype(F32) * scale
    sum_norms = jnp.stack(
        [
            grad_gain_one,
            grad_shift_one,
            grad_gain_two,
            grad_shift_two,
            grad_gain_three,
            grad_shift_three,
        ]
    )
    norm_total = lax.psum(sum_norms * scale, ("dp",) + SEQ)

    upd_in = adam_update(attn_in, sum_in, first_attn_in, second_attn_in)
    upd_out = adam_update(attn_out, sum_out, first_attn_out, second_attn_out)
    upd_up = adam_update(ffn_in, sum_up, first_ffn_in, second_ffn_in)
    upd_down = adam_update(ffn_out, sum_down, first_ffn_out, second_ffn_out)
    upd_norms = adam_update(norms, norm_total, first_norms, second_norms)
    return (
        out_hidden,
        grad_hidden,
        grad_encoder,
        sum_in,
        sum_out,
        sum_up,
        sum_down,
        norm_total,
        upd_in[0],
        upd_out[0],
        upd_up[0],
        upd_down[0],
        upd_norms[0],
        upd_in[1],
        upd_out[1],
        upd_up[1],
        upd_down[1],
        upd_norms[1],
        upd_in[2],
        upd_out[2],
        upd_up[2],
        upd_down[2],
        upd_norms[2],
    )


def solution(mesh):
    groups, shards = mesh.shape["dp"], mesh.shape["seq"]
    split = Mesh(mesh.devices.reshape(groups, shards // 2, 2), ("dp",) + SEQ)
    token = P(("dp",) + SEQ, None)
    stacked = P(None, SEQ, None)
    flat = P(SEQ, None)
    params = (stacked, stacked, flat, flat, P())
    return jax.shard_map(
        on_device,
        mesh=split,
        in_specs=(token, token, P("dp", None), token) + params * 3,
        out_specs=(token, token, token) + params * 4,
        check_vma=False,
    )
```

time: 1900 us -> 839 us (0.44)
  waiting for transfers between devices: 1130 us -> 286 us
  matrix products: 571 us -> 112 us
  blocking collectives: 39 us -> 127 us
  Pallas kernels: 0 us -> 72.2 us
  local copies, waits for them, and re-layouts: 33.5 us -> 102 us
  starting transfers between devices: 1.26 us -> 55.8 us
  other arithmetic: 91.3 us -> 60.5 us
    reduce_scatter x6 -> x4, waiting for transfers between devices: 553 us -> 0.02 us  [the longest x1 0.01 us: on_device(): grad_up = lax.psum_scatter(grad_up, SEQ, scatter_dimension=0, tiled=True)]
    dot_general x254 -> x26, matrix products: 571 us -> 112 us  [the longest x8 40.9 us: dot_f32(): return jnp.dot(left, right, preferred_element_type=F32)]
    all_gather x8 -> x6, waiting for transfers between devices: 440 us -> 114 us  [the longest x1 43 us: on_device(): early = lax.all_gather(early, SEQ + ('dp',), axis=1, tiled=True)]
    all_to_all x0 -> x8, waiting for transfers between devices: none -> 123 us  [the longest x1 39.1 us: on_device(): lax.all_to_all(to_heads, SEQ, split_axis=2, concat_axis=1, tiled=True)]
    psum x1, blocking collectives: 39 us -> 112 us  [on_device(): norm_total = lax.psum(sum_norms * scale, ('dp',) + SEQ)]
    pallas_call x0 -> x4, Pallas kernels: none -> 72.2 us  [the longest x1 23.6 us: self_backward(): pl.pallas_call(functools.partial(self_bwd_kernel, heads, pieces, block),...]
    psum x1 -> x0, waiting for transfers between devices: 71.9 us -> none  [on_device(): lax.psum(owned[0].astype(jnp.bfloat16), 'dp').astype(jnp.float32)]
    unnamed x19 -> x10, waiting for transfers between devices: 64.4 us -> 0.83 us
  transfers between devices with their start and end apart: 17 -> 36, of which waited for: 15 -> 22; matrix products, arithmetic and copies ran while one was open for 15% -> 27% of each run, Pallas kernels for 0% -> 7%
where the time goes in v1:
time: 839 us; the launch traced here: 830 us
  waiting for transfers between devices  286 us (34%)
  blocking collectives  127 us (15%)
  matrix products  112 us (13%)
  local copies, waits for them, and re-layouts  102 us (12%)
  Pallas kernels  72.2 us (9%)
  other arithmetic  60.5 us (7%)
  starting transfers between devices  55.8 us (7%)
  between operations  15.9 us (2%)
    psum x1, blocking collectives, on_device(): norm_total = lax.psum(sum_norms * scale, ('dp',) + SEQ)  112 us
    unnamed x139, local copies, waits for them, and re-layouts  61 us
    ppermute x18, waiting for transfers between devices, dp_swap(): lax.ppermute(values, 'dp', [(index, index ^ offset) for index in range(co...  47.4 us
    all_gather x1, waiting for transfers between devices, on_device(): early = lax.all_gather(early, SEQ + ('dp',), axis=1, tiled=True)  43 us
    dot_general x8, matrix products, dot_f32(): return jnp.dot(left, right, preferred_element_type=F32)  40.9 us
    all_to_all x1, waiting for transfers between devices, on_device(): lax.all_to_all(to_heads, SEQ, split_axis=2, concat_axis=1, tiled=True)  39.1 us
    dot_general x10, matrix products, dot_nt(): return lax.dot_general(left, right, NT, preferred_element_type=F32)  38.1 us
    all_to_all x4, waiting for transfers between devices, dp_join(): return lax.all_to_all(copies, 'dp', split_axis=0, concat_axis=0, tiled=True)  35.7 us
  transfers between devices with their start and end apart: 36, of which 22 were waited for; matrix products, arithmetic and copies ran while one was open for 27% of the time, Pallas kernels for 7%

profile of v1, /device:TPU:0, one launch (start us, length us, event | category | flops | bytes accessed | tf_op | source)
XLA Modules:
  0.0 830.1 jit_solution(4527699431792678563)
XLA Ops:
  35.2 39.1 %all-to-all-done = bf16[3,128,8,128]{1,3,0,2:T(8,128)(2,1)S(1)} async-done(((bf16[3,128,8,128]{1,3,0,2:T(8,128)(2,1)}), bf16[3,128,8,128]{1,3,0,2:T(8,128)(2,1)S(1)}, u32[]{:S(2)}, u32[]{:S(2)}) %all-to-all-start) | async-done | bytes 786464 | tf_op jit(solution)/shard_map/all_to_all | solution.py:452
  84.3 19.9 %self_forward.1 = (bf16[2048,128]{1,0:T(8,128)(2,1)S(1)}, f32[2,8,2048]{2,1,0:T(8,128)S(1)}) custom-call(s32[1,2]{1,0:T(1,128)S(1)} %copy-done.9, bf16[2048,128]{1,0:T(8,128)(2,1)S(1)} %get-tuple-element.117.q_ref, bf16[2048,128]{1,0:T(8,128)(2,1)S(1)} %get-tuple-element.116.k_ref, bf16[2048,128]{1,0:T(8,128)(2,1)S(1)} %get-tuple-element.115.v_ref), custom_call_target="tpu_custom_call" | custom-call | flops 2147483648 | bytes 2097152 | tf_op jit(solution)/shard_map/self_forward/pallas_call | solution.py:137
  112.7 21.7 %all-to-all-done.1 = bf16[8,256,128]{1,2,0:T(8,128)(2,1)S(1)} async-done(((bf16[8,256,128]{1,2,0:T(8,128)(2,1)}), bf16[8,256,128]{1,2,0:T(8,128)(2,1)S(1)}, u32[]{:S(2)}, u32[]{:S(2)}) %all-to-all-start.1) | async-done | bytes 524320 | tf_op jit(solution)/shard_map/all_to_all | solution.py:476
  134.4 43.0 %all-gather.11.cloned.1.call-done = bf16[5,1024,1024]{2,1,0:T(8,128)(2,1)} async-done(((bf16[5,32,1024]{2,1,0:T(8,128)(2,1)}), bf16[5,1024,1024]{2,1,0:T(8,128)(2,1)}) %all-gather.11.cloned.1.call-update) | async-done | bytes 10485776 | tf_op jit(solution)/shard_map/all_gather | solution.py:460
  180.1 26.6 %all-gather.13.cloned.1.call-done = bf16[1024,1024]{1,0:T(8,128)(2,1)} async-done(((bf16[128,1024]{1,0:T(8,128)(2,1)}), bf16[1024,1024]{1,0:T(8,128)(2,1)}) %all-gather.13.cloned.1.call-update) | async-done | bytes 2097168 | tf_op jit(solution)/shard_map/all_gather | solution.py:462
  219.7 11.5 %cross_forward.1 = (bf16[256,1024]{1,0:T(8,128)(2,1)S(1)}, f32[16,8,256]{2,1,0:T(8,128)S(1)}) custom-call(bf16[256,1024]{1,0:T(8,128)(2,1)S(1)} %fusion.47.q.refs_0_, bf16[2,1024,1024]{2,1,0:T(8,128)(2,1)S(1)} %pad_maximum_fusion.k.v.refs_1_.refs_2_, bf16[2,1024,1024]{2,1,0:T(8,128)(2,1)S(1)} %pad_maximum_fusion.k.v.refs_1_.refs_2_), custom_call_target="tpu_custom_call" | custom-call | flops 1073741824 | bytes 5242880 | tf_op jit(solution)/shard_map/cross_forward/pallas_call | solution.py:283
  245.8 10.3 %all-gather.15.cloned.1.call-done = bf16[1024,2048]{0,1:T(8,128)(2,1)} async-done(((bf16[128,2048]{0,1:T(8,128)(2,1)}), bf16[1024,2048]{0,1:T(8,128)(2,1)}) %all-gather.15.cloned.1.call-update) | async-done | bytes 4194320 | tf_op jit(solution)/shard_map/all_gather | solution.py:466
  262.4 11.3 %fusion.78 = f32[1024,2048]{1,0:T(8,128)} fusion(bf16[1024,2048]{0,1:T(8,128)(2,1)} %all-gather.15.cloned.1.call-done, bf16[256,1024]{1,0:T(8,128)(2,1)} %collective-permute-done.2, bf16[256,1024]{1,0:T(8,128)(2,1)} %collective-permute-done.1, bf16[256,1024]{1,0:T(8,128)(2,1)} %collective-permute-done, bf16[256,1024]{1,0:T(8,128)(2,1)} %add_convert_fusion), kind=kOutput, calls=%fused_computation.154 | convolution fusion | flops 4303355904 | bytes 14680064 | tf_op jit(solution)/shard_map/dot_general | solution.py:44
  273.7 29.8 %all-gather.17.cloned.1.call-done = bf16[1,2048,1024]{2,1,0:T(8,128)(2,1)} async-done(((bf16[1,256,1024]{2,1,0:T(8,128)(2,1)}), bf16[1,2048,1024]{2,1,0:T(8,128)(2,1)}) %all-gather.17.cloned.1.call-update) | async-done | bytes 4194320 | tf_op jit(solution)/shard_map/all_gather | solution.py:468
  303.5 12.1 %multiply_convert_fusion = bf16[1024,2048]{1,0:T(8,128)(2,1)S(1)} fusion(f32[1024,2048]{1,0:T(8,128)} %fusion.78, bf16[1024,1024]{1,0:T(8,128)(2,1)} %constant_dynamic-update-slice_fusion, bf16[1,2048,1024]{2,1,0:T(8,128)(2,1)} %all-gather.17.cloned.1.call-done), kind=kOutput, calls=%fused_computation | convolution fusion | flops 4332716032 | bytes 18874368 | tf_op jit(solution)/shard_map/dot_general | solution.py:48
  337.6 9.8 %collective-permute-done.10 = bf16[256,1024]{1,0:T(8,128)(2,1)S(1)} collective-permute-done((bf16[256,1024]{1,0:T(8,128)(2,1)S(1)}, bf16[256,1024]{1,0:T(8,128)(2,1)S(1)}, u32[]{:S(2)}, u32[]{:S(2)}) %collective-permute-start.10) | collective-permute-done | bytes 524320 | tf_op jit(solution)/shard_map/ppermute | solution.py:368
  348.0 10.6 %collective-permute-done.5 = bf16[256,1024]{1,0:T(8,128)(2,1)S(1)} collective-permute-done((bf16[256,1024]{1,0:T(8,128)(2,1)S(1)}, bf16[256,1024]{1,0:T(8,128)(2,1)S(1)}, u32[]{:S(2)}, u32[]{:S(2)}) %collective-permute-start.5) | collective-permute-done | bytes 524320 | tf_op jit(solution)/shard_map/ppermute | solution.py:368
  358.6 10.4 %collective-permute-done.4 = bf16[256,1024]{1,0:T(8,128)(2,1)S(1)} collective-permute-done((bf16[256,1024]{1,0:T(8,128)(2,1)S(1)}, bf16[256,1024]{1,0:T(8,128)(2,1)S(1)}, u32[]{:S(2)}, u32[]{:S(2)}) %collective-permute-start.4) | collective-permute-done | bytes 524320 | tf_op jit(solution)/shard_map/ppermute | solution.py:368
  373.6 17.1 %cross_backward.1 = (bf16[256,1024]{1,0:T(8,128)(2,1)S(1)}, bf16[2,1024,1024]{2,1,0:T(8,128)(2,1)}) custom-call(bf16[256,1024]{1,0:T(8,128)(2,1)S(1)} %fusion.47.q.refs_0_, bf16[2,1024,1024]{2,1,0:T(8,128)(2,1)} %copy-done, bf16[2,1024,1024]{2,1,0:T(8,128)(2,1)} %copy-done, bf16[256,1024]{1,0:T(8,128)(2,1)S(1)} %get-tuple-element.33.refs_3_, ...), custom_call_target="tpu_custom_call" | custom-call | flops 2684354560 | bytes 10485760 | tf_op jit(solution)/shard_map/cross_backward/pallas_call | solution.py:338
  415.0 12.0 %convolution_convert_fusion = bf16[2048,1024]{1,0:T(8,128)(2,1)} fusion(bf16[1024,1024]{1,0:T(8,128)(2,1)} %constant_dynamic-update-slice_fusion, f32[1024,2048]{1,0:T(8,128)} %fusion.78), kind=kOutput, calls=%fused_computation.40 | convolution fusion | flops 4315938816 | bytes 14680064 | tf_op jit(solution)/shard_map/dot_general | solution.py:52
  427.1 11.6 %all-to-all-done.2 = bf16[8,256,128]{2,1,0:T(8,128)(2,1)S(1)} async-done(((bf16[8,256,128]{2,1,0:T(8,128)(2,1)}), bf16[8,256,128]{2,1,0:T(8,128)(2,1)S(1)}, u32[]{:S(2)}, u32[]{:S(2)}) %all-to-all-start.2) | async-done | bytes 524320 | tf_op jit(solution)/shard_map/all_to_all | solution.py:523
  441.8 23.6 %self_backward.1 = (bf16[2048,128]{1,0:T(8,128)(2,1)S(1)}, bf16[2048,128]{1,0:T(8,128)(2,1)S(1)}, bf16[2048,128]{1,0:T(8,128)(2,1)S(1)}) custom-call(s32[1,2]{1,0:T(1,128)S(1)} %copy-done.9, bf16[2048,128]{1,0:T(8,128)(2,1)S(1)} %copy-done.6, bf16[2048,128]{1,0:T(8,128)(2,1)S(1)} %copy-done.4, bf16[2048,128]{1,0:T(8,128)(2,1)S(1)} %copy-done.2, ...), custom_call_target="tpu_custom_call" | custom-call | flops 5368709120 | bytes 4194304 | tf_op jit(solution)/shard_map/self_backward/pallas_call | solution.py:239
  480.2 14.6 %all_to_all.55 = bf16[8,32,384]{2,1,0:T(8,128)(2,1)S(1)} all-to-all(bf16[8,32,384]{2,1,0:T(8,128)(2,1)S(1)} %fusion.77), channel_id=1, replica_groups=mesh['dp'=4,'chip'=4,'core'=2] {'chip','core'}, dimensions={0} | all-to-all | bytes 393216 | tf_op jit(solution)/shard_map/all_to_all | solution.py:564
  507.1 12.7 %all-to-all-done.5 = bf16[4,3,32,1024]{3,2,1,0:T(8,128)(2,1)S(1)} async-done(((bf16[4,3,32,1024]{3,2,1,0:T(8,128)(2,1)}), bf16[4,3,32,1024]{3,2,1,0:T(8,128)(2,1)S(1)}, u32[]{:S(2)}, u32[]{:S(2)}) %all-to-all-start.5) | async-done | bytes 786464 | tf_op jit(solution)/shard_map/all_to_all | solution.py:384
  563.6 14.9 %all-to-all-done.3 = bf16[3,8,256,128]{2,3,0,1:T(8,128)(2,1)S(1)} async-done(((bf16[3,8,256,128]{2,3,0,1:T(8,128)(2,1)}), bf16[3,8,256,128]{2,3,0,1:T(8,128)(2,1)S(1)}, u32[]{:S(2)}, u32[]{:S(2)}) %all-to-all-start.3) | async-done | bytes 1572896 | tf_op jit(solution)/shard_map/all_to_all | solution.py:535
  587.0 111.9 %psum.7 = f32[6,1024]{1,0:T(8,128)S(1)} all-reduce(f32[6,1024]{1,0:T(8,128)S(1)} %broadcast_multiply_fusion), channel_id=1, replica_groups=mesh['dp'=4,'chip'=4,'core'=2] {'dp','chip','core'}, use_global_device_ids=true, to_apply=%region_22.23 | all-reduce | flops 6144 | bytes 49152 | tf_op jit(solution)/shard_map/psum | solution.py:592
  722.9 16.6 %all-to-all-done.7 = bf16[4,128,8,256]{3,2,1,0:T(8,128)(2,1)} async-done(((bf16[4,128,8,256]{3,2,1,0:T(8,128)(2,1)}), bf16[4,128,8,256]{3,2,1,0:T(8,128)(2,1)}, u32[]{:S(2)}, u32[]{:S(2)}) %all-to-all-start.7) | async-done | bytes 2097184 | tf_op jit(solution)/shard_map/all_to_all | solution.py:384
  753.0 10.5 %add_multiply_fusion.2 = (f32[128,8192]{0,1:T(8,128)}, f32[128,8192]{0,1:T(8,128)}, f32[128,8192]{0,1:T(8,128)}, f32[128,8192]{0,1:T(8,128)}) fusion(f32[128,8192]{0,1:T(8,128)} %copy.124, f32[128]{0:T(128)S(1)} %minimum_multiply_fusion.1, bf16[4,128,8,256]{1,3,0,2:T(8,128)(2,1)} %copy.140, f32[128,8192]{0,1:T(8,128)} %copy.142, f32[128,8192]{0,1:T(8,128)} %copy.141), kind=kLoop, calls=%fused_computation.37 | loop fusion | flops 17825792 | bytes 31457792 | tf_op jit(solution)/shard_map/mul | solution.py:401
  793.5 10.4 %add_multiply_fusion.1 = (f32[1024,1024]{1,0:T(8,128)}, f32[1024,1024]{1,0:T(8,128)}, f32[1024,1024]{1,0:T(8,128)}, f32[1024,1024]{1,0:T(8,128)}) fusion(f32[1024,1024]{1,0:T(8,128)} %param.26, f32[1024]{0:T(1024)S(1)} %bitcast.324, bf16[4,256,1024]{2,1,0:T(8,128)(2,1)S(1)} %all-to-all-done.8, f32[1024,1024]{1,0:T(8,128)} %param.36, f32[1024,1024]{1,0:T(8,128)} %param.31), kind=kLoop, calls=%fused_computation.36 | loop fusion | flops 17825792 | bytes 31461376 | tf_op jit(solution)/shard_map/mul | solution.py:401
  (312 shorter events, 302.1 us)
Async XLA Ops:
  7.2 72.2 %all-gather.9.cloned.1.call-start = ((), (), s32[]{:S(2)}) async-start(), calls=%async_computation.13 | async-start | bytes 4718592 | tf_op jit(solution)/shard_map/all_gather | solution.py:449
  12.8 164.7 %all-gather.11.cloned.1.call-start = ((), (), s32[]{:S(2)}) async-start(), calls=%async_computation.14 | async-start | bytes 10813440 | tf_op jit(solution)/shard_map/all_gather | solution.py:460
  16.8 189.9 %all-gather.13.cloned.1.call-start = ((), (), s32[]{:S(2)}) async-start(), calls=%async_computation.15 | async-start | bytes 2359296 | tf_op jit(solution)/shard_map/all_gather | solution.py:462
  17.6 238.5 %all-gather.15.cloned.1.call-start = ((), (), s32[]{:S(2)}) async-start(), calls=%async_computation.16 | async-start | bytes 4718592 | tf_op jit(solution)/shard_map/all_gather | solution.py:466
  26.7 47.6 %all-to-all-start = ((bf16[3,128,8,128]{1,3,0,2:T(8,128)(2,1)}), bf16[3,128,8,128]{1,3,0,2:T(8,128)(2,1)S(1)}, u32[]{:S(2)}, u32[]{:S(2)}) async-start(bf16[3,128,8,128]{1,3,0,2:T(8,128)(2,1)} %copy.119), calls=%async_computation | async-start | bytes 1572864 | tf_op jit(solution)/shard_map/all_to_all | solution.py:452
  33.0 270.5 %all-gather.17.cloned.1.call-start = ((), (), s32[]{:S(2)}) async-start(), calls=%async_computation.21 | async-start | bytes 4718592 | tf_op jit(solution)/shard_map/all_gather | solution.py:468
  105.3 29.1 %all-to-all-start.1 = ((bf16[8,256,128]{1,2,0:T(8,128)(2,1)}), bf16[8,256,128]{1,2,0:T(8,128)(2,1)S(1)}, u32[]{:S(2)}, u32[]{:S(2)}) async-start(bf16[8,256,128]{1,2,0:T(8,128)(2,1)} %copy.121), calls=%async_computation.1 | async-start | bytes 1048576 | tf_op jit(solution)/shard_map/all_to_all | solution.py:476
  108.8 422.9 %reduce-scatter.5.cloned.1.call-start = ((), (), s32[]{:S(2)}) async-start(), calls=%async_computation.17 | async-start | bytes 4718592 | tf_op jit(solution)/shard_map/reduce_scatter | solution.py:517
  109.2 129.6 %collective-permute-start.6 = (bf16[256,1024]{1,0:T(8,128)(2,1)S(1)}, bf16[256,1024]{1,0:T(8,128)(2,1)}, u32[]{:S(2)}, u32[]{:S(2)}) collective-permute-start(bf16[256,1024]{1,0:T(8,128)(2,1)S(1)} %copy-done.23), channel_id=1, source_target_pairs={{0,8},{8,0},{16,24},{24,16},{1,9},{9,1},{17,25},{25,17},{2,10},{10... | collective-permute-start | bytes 1572872 | tf_op jit(solution)/shard_map/ppermute | solution.py:368
  110.7 131.3 %collective-permute-start.7 = (bf16[256,1024]{1,0:T(8,128)(2,1)S(1)}, bf16[256,1024]{1,0:T(8,128)(2,1)}, u32[]{:S(2)}, u32[]{:S(2)}) collective-permute-start(bf16[256,1024]{1,0:T(8,128)(2,1)S(1)} %copy-done.23), channel_id=1, source_target_pairs={{0,16},{8,24},{16,0},{24,8},{1,17},{9,25},{17,1},{25,9},{2,18},{10... | collective-permute-start | bytes 1572872 | tf_op jit(solution)/shard_map/ppermute | solution.py:368
  112.2 131.7 %collective-permute-start.8 = (bf16[256,1024]{1,0:T(8,128)(2,1)S(1)}, bf16[256,1024]{1,0:T(8,128)(2,1)}, u32[]{:S(2)}, u32[]{:S(2)}) collective-permute-start(bf16[256,1024]{1,0:T(8,128)(2,1)S(1)} %copy-done.23), channel_id=1, source_target_pairs={{0,24},{8,16},{16,8},{24,0},{1,25},{9,17},{17,9},{25,1},{2,26},{10... | collective-permute-start | bytes 1572872 | tf_op jit(solution)/shard_map/ppermute | solution.py:368
  334.0 35.0 %collective-permute-start.4 = (bf16[256,1024]{1,0:T(8,128)(2,1)S(1)}, bf16[256,1024]{1,0:T(8,128)(2,1)S(1)}, u32[]{:S(2)}, u32[]{:S(2)}) collective-permute-start(bf16[256,1024]{1,0:T(8,128)(2,1)S(1)} %get-tuple-element.108), channel_id=1, source_target_pairs={{0,16},{8,24},{16,0},{24,8},{1,17},{9,25},{17,1},{25,9},{2,18},{10... | collective-permute-start | bytes 1572872 | tf_op jit(solution)/shard_map/ppermute | solution.py:368
  336.1 33.1 %collective-permute-start.3 = (bf16[256,1024]{1,0:T(8,128)(2,1)S(1)}, bf16[256,1024]{1,0:T(8,128)(2,1)S(1)}, u32[]{:S(2)}, u32[]{:S(2)}) collective-permute-start(bf16[256,1024]{1,0:T(8,128)(2,1)S(1)} %get-tuple-element.106), channel_id=1, source_target_pairs={{0,8},{8,0},{16,24},{24,16},{1,9},{9,1},{17,25},{25,17},{2,10},{10... | collective-permute-start | bytes 1572872 | tf_op jit(solution)/shard_map/ppermute | solution.py:368
  390.7 188.2 %all-gather.19.cloned.1.call-start = ((), (), s32[]{:S(2)}) async-start(), calls=%async_computation.22 | async-start | bytes 6488064 | tf_op jit(solution)/shard_map/all_gather | solution.py:470
  392.6 315.2 %reduce-scatter.9.cloned.1.call-start = ((), (), s32[]{:S(2)}) async-start(), calls=%async_computation.19 | async-start | bytes 4718592 | tf_op jit(solution)/shard_map/reduce_scatter | solution.py:507
  411.1 27.6 %all-to-all-start.2 = ((bf16[8,256,128]{2,1,0:T(8,128)(2,1)}), bf16[8,256,128]{2,1,0:T(8,128)(2,1)S(1)}, u32[]{:S(2)}, u32[]{:S(2)}) async-start(bf16[8,256,128]{2,1,0:T(8,128)(2,1)} %bitcast.273), calls=%async_computation.2 | async-start | bytes 1048576 | tf_op jit(solution)/shard_map/all_to_all | solution.py:523
  414.6 308.4 %reduce-scatter.11.cloned.1.call-start = ((), (), s32[]{:S(2)}) async-start(), calls=%async_computation.20 | async-start | bytes 4718592 | tf_op jit(solution)/shard_map/reduce_scatter | solution.py:506
  519.9 58.7 %all-to-all-start.3 = ((bf16[3,8,256,128]{2,3,0,1:T(8,128)(2,1)}), bf16[3,8,256,128]{2,3,0,1:T(8,128)(2,1)S(1)}, u32[]{:S(2)}, u32[]{:S(2)}) async-start(bf16[3,8,256,128]{2,3,0,1:T(8,128)(2,1)} %pad_maximum_fusion.2), calls=%async_computation.3 | async-start | bytes 3145728 | tf_op jit(solution)/shard_map/all_to_all | solution.py:535
  523.5 264.0 %reduce-scatter.7.cloned.1.call-start = ((), (), s32[]{:S(2)}) async-start(), calls=%async_computation.18 | async-start | bytes 2949120 | tf_op jit(solution)/shard_map/reduce_scatter | solution.py:561
  548.0 150.9 %collective-permute-start.17 = (bf16[5,8,32,1024]{3,2,1,0:T(8,128)(2,1)}, bf16[5,8,32,1024]{3,2,1,0:T(8,128)(2,1)}, u32[]{:S(2)}, u32[]{:S(2)}) collective-permute-start(bf16[5,8,32,1024]{3,2,1,0:T(8,128)(2,1)} %get-tuple-element.97), channel_id=1, source_target_pairs={{0,24},{8,16},{16,8},{24,0},{1,25},{9,17},{17,9},{25,1},{2,26},{10... | collective-permute-start | bytes 7864328 | tf_op jit(solution)/shard_map/ppermute | solution.py:368
  549.0 149.9 %collective-permute-start.16 = (bf16[5,8,32,1024]{3,2,1,0:T(8,128)(2,1)}, bf16[5,8,32,1024]{3,2,1,0:T(8,128)(2,1)}, u32[]{:S(2)}, u32[]{:S(2)}) collective-permute-start(bf16[5,8,32,1024]{3,2,1,0:T(8,128)(2,1)} %get-tuple-element.98), channel_id=1, source_target_pairs={{0,16},{8,24},{16,0},{24,8},{1,17},{9,25},{17,1},{25,9},{2,18},{10... | collective-permute-start | bytes 7864328 | tf_op jit(solution)/shard_map/ppermute | solution.py:368
  550.9 148.0 %collective-permute-start.15 = (bf16[5,8,32,1024]{3,2,1,0:T(8,128)(2,1)}, bf16[5,8,32,1024]{3,2,1,0:T(8,128)(2,1)}, u32[]{:S(2)}, u32[]{:S(2)}) collective-permute-start(bf16[5,8,32,1024]{3,2,1,0:T(8,128)(2,1)} %get-tuple-element.96), channel_id=1, source_target_pairs={{0,8},{8,0},{16,24},{24,16},{1,9},{9,1},{17,25},{25,17},{2,10},{10... | collective-permute-start | bytes 7864328 | tf_op jit(solution)/shard_map/ppermute | solution.py:368
  710.5 29.0 %all-to-all-start.7 = ((bf16[4,128,8,256]{3,2,1,0:T(8,128)(2,1)}), bf16[4,128,8,256]{3,2,1,0:T(8,128)(2,1)}, u32[]{:S(2)}, u32[]{:S(2)}) async-start(bf16[4,128,8,256]{3,2,1,0:T(8,128)(2,1)} %broadcast_in_dim.65), calls=%async_computation.10 | async-start | bytes 4194304 | tf_op jit(solution)/shard_map/all_to_all | solution.py:384
  742.2 27.9 %all-to-all-start.8 = ((bf16[4,256,1024]{2,1,0:T(8,128)(2,1)}), bf16[4,256,1024]{2,1,0:T(8,128)(2,1)S(1)}, u32[]{:S(2)}, u32[]{:S(2)}) async-start(bf16[4,256,1024]{2,1,0:T(8,128)(2,1)} %broadcast_in_dim.66), calls=%async_computation.12 | async-start | bytes 4194304 | tf_op jit(solution)/shard_map/all_to_all | solution.py:384
  (73 other events, 1686.0 us)
Sparse Core Ops, SparseCore 0:
  12.9 66.4 all-gather.8
  82.9 94.4 all-gather.10
  179.0 27.6 all-gather.12
  208.8 47.2 all-gather.14
  258.1 45.3 all-gather.16
  390.9 56.4 reduce-scatter.4
  450.8 82.4 all-gather.18
  536.2 63.6 reduce-scatter.8
  602.8 51.5 reduce-scatter.10
  707.7 36.5 reduce-scatter.6

commit v2 on v1

--- a/solution.py
+++ b/solution.py
@@ -171,14 +171,13 @@
     o_ref,
     do_ref,
     lse_ref,
-    dq_ref,
-    dk_ref,
-    dv_ref,
+    flat_ref,
     dk_acc,
     dv_acc,
 ):
     step = pl.program_id(0)
     last = pl.num_programs(0) - 1
+    width = dk_acc.shape[1]
 
     @pl.when(step == 0)
     def _():
@@ -220,12 +219,13 @@
         dq = jnp.zeros((block, HEAD_DIM), F32)
         dq = lax.fori_loop(0, step, functools.partial(one_block, False), dq)
         dq = lax.fori_loop(step, blocks, functools.partial(one_block, True), dq)
-        dq_ref[:, cols] = (dq * SCALE).astype(BF16)
+        dq = (dq * SCALE).astype(BF16)
+        flat_ref[pl.ds(pl.multiple_of(step * block, block), block), cols] = dq
 
     @pl.when(step == last)
     def _():
-        dk_ref[...] = dk_acc[...].astype(BF16)
-        dv_ref[...] = dv_acc[...].astype(BF16)
+        for which, acc in ((1, dk_acc), (2, dv_acc)):
+            flat_ref[:, which * width : (which + 1) * width] = acc[...].astype(BF16)
 
 
 def self_backward(starts, query, key, value, out, grad, lse, block):
@@ -235,10 +235,9 @@
     whole = pl.BlockSpec((tokens, width), lambda i, s: (0, 0))
     rows = pl.BlockSpec((block, width), lambda i, s: (i, 0))
     flops = 5 * 2 * heads * tokens * tokens * HEAD_DIM
-    shape = jax.ShapeDtypeStruct((tokens, width), BF16)
     return pl.pallas_call(
         functools.partial(self_bwd_kernel, heads, pieces, block),
-        out_shape=(shape, shape, shape),
+        out_shape=jax.ShapeDtypeStruct((tokens, 3 * width), BF16),
         grid_spec=pltpu.PrefetchScalarGridSpec(
             num_scalar_prefetch=1,
             grid=(tokens // block,),
@@ -250,7 +249,7 @@
                 rows,
                 pl.BlockSpec((heads, 8, block), lambda i, s: (0, 0, i)),
             ],
-            out_specs=(rows, whole, whole),
+            out_specs=pl.BlockSpec((tokens, 3 * width), lambda i, s: (0, 0)),
             scratch_shapes=[pltpu.VMEM((tokens, width), F32), pltpu.VMEM((tokens, width), F32)],
         ),
         compiler_params=pltpu.CompilerParams(
@@ -308,9 +307,11 @@
     )(query, key_value, key_value)
 
 
-def cross_bwd_kernel(q_ref, k_ref, v_ref, o_ref, do_ref, lse_ref, dq_ref, dkv_ref):
+def cross_bwd_kernel(width, q_ref, k_ref, v_ref, o_ref, do_ref, lse_ref, dq_ref, dkv_ref):
     for head in range(q_ref.shape[1] // HEAD_DIM):
         cols = slice(head * HEAD_DIM, (head + 1) * HEAD_DIM)
+        owner = head * HEAD_DIM // width
+        own_cols = slice(head * HEAD_DIM % width, head * HEAD_DIM % width + HEAD_DIM)
         query = q_ref[:, cols] * BF16(SCALE)
         grad = do_ref[:, cols]
         product = grad.astype(F32) * o_ref[:, cols].astype(F32)
@@ -324,22 +325,23 @@
         key = k_ref[:, cols]
         weights = jnp.exp(dot_nt(key, query) - lse_ref[head][:1])
         grad_weights = dot_nt(v_ref[:, cols], grad)
-        dkv_ref[1, :, cols] = dot_f32(weights.astype(BF16), grad).astype(BF16)
+        dkv_ref[owner, 1, :, own_cols] = dot_f32(weights.astype(BF16), grad).astype(BF16)
         grad_scores = (weights * (grad_weights - delta)).astype(BF16)
-        dkv_ref[0, :, cols] = dot_f32(grad_scores, query).astype(BF16)
+        dkv_ref[owner, 0, :, own_cols] = dot_f32(grad_scores, query).astype(BF16)
         dq_ref[:, cols] = (dot_tn(grad_scores, key) * SCALE).astype(BF16)
 
 
-def cross_backward(query, key_value, out, grad, lse):
+def cross_backward(query, key_value, out, grad, lse, owner_width):
     rows, width = query.shape
     keys = key_value.shape[1]
     heads = width // HEAD_DIM
     rows_spec = pl.BlockSpec((rows, 128), lambda i: (0, i))
+    dkv_block = (128 // owner_width, 2, keys, owner_width)
     return pl.pallas_call(
-        lambda *refs: cross_bwd_kernel(*refs),
+        functools.partial(cross_bwd_kernel, owner_width),
         out_shape=(
             jax.ShapeDtypeStruct((rows, width), BF16),
-            jax.ShapeDtypeStruct((2, keys, width), BF16),
+            jax.ShapeDtypeStruct((width // owner_width, 2, keys, owner_width), BF16),
         ),
         grid=(width // 128,),
         in_specs=[
@@ -350,7 +352,7 @@
             rows_spec,
             pl.BlockSpec((2, 8, rows), lambda i: (i, 0, 0)),
         ],
-        out_specs=(rows_spec, pl.BlockSpec((2, keys, 128), lambda i: (0, 0, i))),
+        out_specs=(rows_spec, pl.BlockSpec(dkv_block, lambda i: (i, 0, 0, 0))),
         compiler_params=pltpu.CompilerParams(
             dimension_semantics=("arbitrary",), vmem_limit_bytes=VMEM_LIMIT
         ),
@@ -363,29 +365,189 @@
     )(query, key_value, key_value, out, grad, lse)
 
 
-def dp_swap(values, offset):
-    count = lax.axis_size("dp")
-    return lax.ppermute(values, "dp", [(index, index ^ offset) for index in range(count)])
+def swap(values, axis, offset):
+    count = lax.axis_size(axis)
+    return lax.ppermute(values, axis, [(index, index ^ offset) for index in range(count)])
 
 
 def dp_gather(values):
-    return [values] + [dp_swap(values, k) for k in range(1, lax.axis_size("dp"))]
-
-
-def dp_scatter(blocks):
-    total = blocks[0]
-    for k in range(1, len(blocks)):
-        total = total + dp_swap(blocks[k].astype(BF16), k).astype(F32)
-    return total
-
-
-def dp_join(values):
-    copies = jnp.broadcast_to(values[None], (lax.axis_size("dp"),) + values.shape)
-    return lax.all_to_all(copies, "dp", split_axis=0, concat_axis=0, tiled=True)
+    return [values] + [swap(values, "dp", k) for k in range(1, lax.axis_size("dp"))]
+
+
+def swap_blocks(blocks, axis):
+    return [blocks[0]] + [swap(blocks[k], axis, k) for k in range(1, len(blocks))]
+
+
+def pick_blocks(values, axis_name, axis):
+    index = lax.axis_index(axis_name)
+    return [
+        lax.dynamic_index_in_dim(values, index ^ k, axis, keepdims=False)
+        for k in range(values.shape[axis])
+    ]
+
+
+def tree_sum(parts):
+    parts = [part.astype(F32) for part in parts]
+    while len(parts) > 1:
+        parts = [parts[k] + parts[k + 1] for k in range(0, len(parts), 2)]
+    return parts[0]
+
+
+def sum_everywhere(values):
+    for axis in ("core", "chip", "dp"):
+        count = lax.axis_size(axis)
+        values = tree_sum([values] + [swap(values, axis, k) for k in range(1, count)])
+    return values
+
+
+def position():
+    return jnp.stack([lax.axis_index(axis) for axis in ("dp",) + SEQ]).astype(jnp.int32)
+
+
+def place_kernel(store, at_ref, *refs):
+    store(at_ref[0], at_ref[1], at_ref[2], refs[:-1], refs[-1])
+
+
+def place(parts, store, shape, block=None, part_blocks=None):
+    steps = 1 if block is None else shape[0]
+    block = shape if block is None else block
+    part_blocks = [part.shape for part in parts] if part_blocks is None else part_blocks
+
+    def spec(dims):
+        return pl.BlockSpec(dims, lambda i, at: (i,) + (0,) * (len(dims) - 1))
+
+    return pl.pallas_call(
+        functools.partial(place_kernel, store),
+        out_shape=jax.ShapeDtypeStruct(shape, parts[0].dtype),
+        grid_spec=pltpu.PrefetchScalarGridSpec(
+            num_scalar_prefetch=1,
+            grid=(steps,),
+            in_specs=[spec(dims) for dims in part_blocks],
+            out_specs=spec(block),
+        ),
+        compiler_params=pltpu.CompilerParams(
+            dimension_semantics=("arbitrary",), vmem_limit_bytes=VMEM_LIMIT
+        ),
+        cost_estimate=pl.CostEstimate(
+            flops=0, bytes_accessed=4 * math.prod(shape), transcendentals=0
+        ),
+        name="place",
+    )(position(), *parts)
+
+
+def join_parts(parts, axis):
+    shape = parts[0].shape
+    full = shape[:axis] + (len(parts),) + shape[axis:]
+
+    def store(dp_index, chip, core, refs, out):
+        for k, ref in enumerate(refs):
+            if axis == 0:
+                out[dp_index ^ k] = ref[...]
+            else:
+                for lead in range(shape[0]):
+                    where = (lead,) + (slice(None),) * (axis - 1) + (dp_index ^ k,)
+                    out[where] = ref[lead]
+
+    return place(parts, store, full)
+
+
+def join_columns(parts, cut):
+    groups = len(parts)
+    rows, columns = parts[0].shape
+    if cut % 128:
+        joined = jnp.zeros((groups, rows, columns // cut, cut), parts[0].dtype)
+        for k, part in enumerate(parts):
+            part = part.reshape(rows, columns // cut, cut)
+            index = lax.axis_index("dp") ^ k
+            joined = lax.dynamic_update_index_in_dim(joined, part, index, 0)
+        return joined.transpose(1, 2, 0, 3).reshape(rows, columns * groups)
+
+    def store(dp_index, chip, core, refs, out):
+        for k, ref in enumerate(refs):
+            for s in range(columns // cut):
+                start = pl.multiple_of((s * groups + (dp_index ^ k)) * cut, 128)
+                out[:, pl.ds(start, cut)] = ref[:, s * cut : (s + 1) * cut]
+
+    return place(parts, store, (rows, columns * groups))
 
 
 def own_part(values, axis):
     return lax.dynamic_index_in_dim(values, lax.axis_index("dp"), axis, keepdims=False)
+
+
+def fetch_columns(own):
+    half = own.shape[1] // 2
+    mine = lax.dynamic_slice_in_dim(own, lax.axis_index("core") * half, half, 1)
+    return [swap(mine, "dp", k) for k in range(1, lax.axis_size("dp"))]
+
+
+def share_columns(parts):
+    return [swap(part, "core", 1) for part in parts]
+
+
+def send_rows(parts):
+    own, given = pick_blocks(parts, "core", 1)
+    both = jnp.stack([own, swap(given, "core", 1)], axis=1)
+    return swap_blocks(pick_blocks(both, "chip", 0), "chip")
+
+
+def join_rows(parts):
+    def store(dp_index, chip, core, refs, out):
+        for k, ref in enumerate(refs):
+            for flip in range(2):
+                out[(chip ^ k) * 2 + (core ^ flip)] = ref[flip]
+
+    return place(parts, store, (2 * len(parts),) + parts[0].shape[1:])
+
+
+def join_fetched(parts):
+    count, model, cut = parts[0].shape
+    half = model // 2
+    others = (len(parts) - 1) // 2
+
+    def store(dp_index, chip, core, refs, out):
+        out[0, :, pl.ds(pl.multiple_of(dp_index * cut, 128), cut)] = refs[0][0]
+        for flip in range(2):
+            rows = pl.ds(pl.multiple_of((core ^ flip) * half, 128), half)
+            for k in range(1, others + 1):
+                columns = pl.ds(pl.multiple_of((dp_index ^ k) * cut, 128), cut)
+                out[0, rows, columns] = refs[flip * others + k][0]
+
+    blocks = [(1,) + part.shape[1:] for part in parts]
+    return place(parts, store, (count, model, model), (1, model, model), blocks)
+
+
+def after(values, marker):
+    return lax.optimization_barrier((values, marker))[0]
+
+
+def meet(*values):
+    return lax.optimization_barrier(values)
+
+
+def take_columns_kernel(at_ref, in_ref, out_ref):
+    out_ref[...] = in_ref[...].astype(BF16)
+
+
+def take_columns(weights, shards, groups, cut):
+    rows = weights.shape[0]
+    if cut % 128:
+        cut_up = own_part(weights.reshape(rows, shards, groups, cut), 2)
+        return cut_up.reshape(rows, shards * cut).astype(BF16)
+    return pl.pallas_call(
+        take_columns_kernel,
+        out_shape=jax.ShapeDtypeStruct((rows, shards * cut), BF16),
+        grid_spec=pltpu.PrefetchScalarGridSpec(
+            num_scalar_prefetch=1,
+            grid=(shards,),
+            in_specs=[pl.BlockSpec((rows, cut), lambda s, at: (0, s * groups + at[0]))],
+            out_specs=pl.BlockSpec((rows, cut), lambda s, at: (0, s)),
+        ),
+        cost_estimate=pl.CostEstimate(
+            flops=0, bytes_accessed=6 * rows * shards * cut, transcendentals=0
+        ),
+        name="take_columns",
+    )(lax.axis_index("dp").astype(jnp.int32)[None], weights)
 
 
 def clip_units(grad):
@@ -399,6 +561,38 @@
     second_new = BETA_TWO * second_moment + (1.0 - BETA_TWO) * clipped * clipped
     step_size = first_new / CORRECT_ONE / (jnp.sqrt(second_new / CORRECT_TWO) + ADAM_EPS)
     return (first_new, second_new, -RATE * (step_size + DECAY * weight))
+
+
+def adam_kernel(scale, g_ref, w_ref, m1_ref, m2_ref, g_out, m1_out, m2_out, change_out):
+    grad = g_ref[...].astype(F32) * scale
+    g_out[...] = grad
+    m1_out[...], m2_out[...], change_out[...] = adam_update(
+        w_ref[...], grad, m1_ref[...], m2_ref[...]
+    )
+
+
+def adam_call(grad, scale, weight, first, second):
+    shape = weight.shape
+    columns = shape[-1]
+    rows = math.prod(shape[:-1])
+    step = min(rows, 262144 // columns)
+    spec = pl.BlockSpec((step, columns), lambda i: (i, 0))
+    flat = jax.ShapeDtypeStruct((rows, columns), F32)
+    outs = pl.pallas_call(
+        functools.partial(adam_kernel, scale),
+        out_shape=(flat,) * 4,
+        grid=(rows // step,),
+        in_specs=[spec] * 4,
+        out_specs=(spec,) * 4,
+        compiler_params=pltpu.CompilerParams(
+            dimension_semantics=("arbitrary",), vmem_limit_bytes=VMEM_LIMIT
+        ),
+        cost_estimate=pl.CostEstimate(
+            flops=20 * rows * columns, bytes_accessed=30 * rows * columns, transcendentals=0
+        ),
+        name="adam",
+    )(*[array.reshape(rows, columns) for array in (grad, weight, first, second)])
+    return [array.reshape(shape) for array in outs]
 
 
 def gelu_both(values_in):
@@ -442,81 +636,101 @@
     unit_cut = hidden_units // (shards * groups)
     block = min(512, tokens)
 
+    core = lax.axis_index("core")
+    chips = shards // 2
     gains = lax.optimization_barrier(norms.astype(BF16)).astype(F32)
     resid_in = hidden.astype(F32)
     normed_one, norm_one_back = jax.vjp(layer_norm, resid_in, gains[0], gains[1])
     normed_one = normed_one.astype(BF16)
     normed_all = lax.all_gather(normed_one, SEQ, axis=0, tiled=True)
 
-    to_heads = attn_in[:3].astype(BF16).reshape(3, shard_rows, shards, width)
-    to_heads = lax.all_to_all(to_heads, SEQ, split_axis=2, concat_axis=1, tiled=True)
-    to_heads = to_heads.reshape(3, model, width)
-
-    def row_part(weights):
-        cut = weights.reshape(weights.shape[0], groups, part_rows, model)
-        return own_part(cut, 1).astype(BF16)
-
-    early = jnp.concatenate([row_part(attn_out), row_part(attn_in[3:])], axis=0)
-    early = lax.all_gather(early, SEQ + ("dp",), axis=1, tiled=True)
-    w_o, w_co, w_cq, w_ck, w_cv = [early[index] for index in range(5)]
-    encoder_all = lax.all_gather(encoder, SEQ, axis=0, tiled=True)
-
-    up = own_part(ffn_in.reshape(shard_rows, shards, groups, unit_cut), 2)
-    up = up.reshape(shard_rows, shards * unit_cut).astype(BF16)
-    w_up = lax.all_gather(up, SEQ, axis=0, tiled=True)
+    to_heads = own_part(attn_in[:3].reshape(3, groups, part_rows, shards, width), 1).astype(BF16)
+    to_heads = to_heads.transpose(2, 1, 0, 3).reshape(shards, part_rows, 3 * width)
+    to_heads = lax.all_to_all(to_heads, SEQ, split_axis=0, concat_axis=0, tiled=True)
+    to_heads = dp_gather(to_heads)
+    grad_parts = dp_gather(grad_out)
+
+    def column_part(weights):
+        cut = weights.reshape(weights.shape[0], shard_rows, groups, model // groups)
+        return own_part(cut, 2).astype(BF16)
+
+    first = column_part(jnp.concatenate([attn_out[:1], attn_in[3:4]], axis=0))
+    second = column_part(jnp.concatenate([attn_in[4:], attn_out[1:]], axis=0))
+    enc_rows = encoder.shape[0]
+    second = jnp.concatenate(
+        [second, encoder.reshape(enc_rows, groups, model // groups).transpose(1, 0, 2)], axis=0
+    )
+    up = take_columns(ffn_in, shards, groups, unit_cut)
     down = own_part(ffn_out.reshape(groups, unit_cut, model), 0).astype(BF16)
-    w_down = lax.all_gather(down, SEQ, axis=0, tiled=True)
-    late = row_part(attn_in[:3])
-    late = lax.all_gather(late, SEQ + ("dp",), axis=1, tiled=True)
-
-    qkv = dot_f32(normed_all, jnp.concatenate([to_heads[i] for i in range(3)], axis=1))
-    qkv = qkv.astype(BF16)
+    to_heads = join_parts(to_heads, 1).reshape(model, 3 * width)
+    normed_all, to_heads, grad_parts, first, second, up, down = meet(
+        normed_all, to_heads, grad_parts, first, second, up, down
+    )
+
+    first = lax.all_gather(first, SEQ, axis=1, tiled=True)
+    qkv = dot_f32(normed_all, to_heads).astype(BF16)
+    second = lax.all_gather(after(second, qkv), SEQ, axis=1, tiled=True)
     query, key, value = [qkv[:, i * width : (i + 1) * width] for i in range(3)]
     out_heads, self_lse = self_forward(piece_starts, query, key, value, block)
+    out_heads, first = meet(out_heads, first)
+    w_up = lax.all_gather(after(up, out_heads), SEQ, axis=0, tiled=True)
+    first_parts = fetch_columns(first)
     attended = lax.all_to_all(
         out_heads.reshape(shards, rows, width), SEQ, split_axis=0, concat_axis=0, tiled=True
     )
+    attended, first_parts = meet(attended, first_parts)
+    w_down = lax.all_gather(after(down, attended), SEQ, axis=0, tiled=True)
+    first_shared = share_columns(first_parts)
     attended = attended.transpose(1, 0, 2).reshape(rows, model)
+    attended, first_shared, second = meet(attended, first_shared, second)
+    second_parts = fetch_columns(second[:3])
+    encoder_all = second[3:].transpose(1, 0, 2).reshape(enc_rows * shards, model)
+    w_o, w_cq = join_fetched([first] + first_parts + first_shared)
     first_sum = resid_in + dot_f32(attended, w_o)
 
     normed_two, norm_two_back = jax.vjp(layer_norm, first_sum, gains[2], gains[3])
     normed_two = normed_two.astype(BF16)
     cross_queries = dot_f32(normed_two, w_cq).astype(BF16)
+    cross_queries, second_parts = meet(cross_queries, second_parts)
+    w_ck, w_cv, w_co = join_fetched([second[:3]] + second_parts + share_columns(second_parts))
     cross_kv = jnp.stack([dot_f32(encoder_all, w_ck), dot_f32(encoder_all, w_cv)]).astype(BF16)
     crossed, cross_lse = cross_forward(cross_queries, cross_kv)
     second_sum = first_sum + dot_f32(crossed, w_co)
 
     normed_three, norm_three_back = jax.vjp(layer_norm, second_sum, gains[4], gains[5])
     normed_three = normed_three.astype(BF16)
-    grad_tokens = jnp.concatenate(dp_gather(grad_out), axis=0)
     ffn_tokens = jnp.concatenate(dp_gather(normed_three), axis=0)
+    grad_tokens = jnp.concatenate(grad_parts, axis=0)
     activated, slope = gelu_both(dot_f32(ffn_tokens, w_up))
     activated = activated.astype(BF16)
     grad_pre = (dot_nt(grad_tokens, w_down) * slope).astype(BF16)
-    partial = dot_nt(grad_pre, w_up)
-    grad_normed_three = dp_scatter(
-        [partial[k * rows : (k + 1) * rows] for k in range(groups)]
-    )
-    partial = dot_f32(activated, w_down)
-    out_hidden = second_sum + dp_scatter(
-        [partial[k * rows : (k + 1) * rows] for k in range(groups)]
-    )
+    partial = dot_nt(grad_pre, w_up).astype(BF16)
+    grad_three = swap_blocks([partial[k * rows : (k + 1) * rows] for k in range(groups)], "dp")
+    activated, grad_pre = after((activated, grad_pre), partial)
     grad_down = dot_tn(activated, grad_tokens).astype(BF16)
     grad_up = dot_tn(ffn_tokens, grad_pre).astype(BF16)
     grad_down = lax.psum_scatter(grad_down, SEQ, scatter_dimension=0, tiled=True)
+    activated, grad_three = after((activated, grad_three), grad_up)
     grad_up = lax.psum_scatter(grad_up, SEQ, scatter_dimension=0, tiled=True)
-
-    norm_part, grad_gain_three, grad_shift_three = norm_three_back(grad_normed_three)
+    partial = dot_f32(activated, w_down)
+    hidden_parts = [partial[:rows]] + [
+        partial[k * rows : (k + 1) * rows].astype(BF16) for k in range(1, groups)
+    ]
+    grad_three, hidden_parts = meet(grad_three, hidden_parts)
+    hidden_parts = swap_blocks(hidden_parts, "dp")
+
+    norm_part, grad_gain_three, grad_shift_three = norm_three_back(tree_sum(grad_three))
     grad_second = grad_out.astype(F32) + norm_part
     grad_cross_branch = grad_second.astype(BF16)
-    grad_w_co = dot_tn(crossed, grad_cross_branch)
     grad_crossed = dot_nt(grad_cross_branch, w_co).astype(BF16)
     grad_cq, grad_ckv = cross_backward(
-        cross_queries, cross_kv, crossed, grad_crossed, cross_lse
-    )
-    grad_ckv = lax.psum_scatter(grad_ckv, SEQ, scatter_dimension=1, tiled=True)
-    grad_w_cq = dot_tn(normed_two, grad_cq)
-    norm_part, grad_gain_two, grad_shift_two = norm_two_back(dot_nt(grad_cq, w_cq))
+        cross_queries, cross_kv, crossed, grad_crossed, cross_lse, width
+    )
+    grad_cq, hidden_parts, grad_ckv = meet(grad_cq, hidden_parts, grad_ckv)
+    grad_ckv = lax.psum_scatter(grad_ckv, SEQ, scatter_dimension=0, tiled=True)
+    grad_ckv = grad_ckv.reshape(2, enc_rows * shards, width)
+    grad_normed_two = dot_nt(grad_cq, w_cq)
+    norm_part, grad_gain_two, grad_shift_two = norm_two_back(grad_normed_two)
     grad_first = grad_second + norm_part
     grad_self_branch = grad_first.astype(BF16)
     grad_attended = dot_nt(grad_self_branch, w_o).astype(BF16)
@@ -527,58 +741,73 @@
         concat_axis=0,
         tiled=True,
     ).reshape(tokens, width)
+
+    crossed, attended, grad_down = after((crossed, attended, grad_down), grad_attended)
+    down_parts = dp_gather(grad_down)
+    grad_w_co = dot_tn(crossed, grad_cross_branch)
+    grad_w_cq = dot_tn(normed_two, grad_cq)
     grad_w_o = dot_tn(attended, grad_self_branch)
-    grad_q, grad_k, grad_v = self_backward(
+    local = jnp.stack([grad.astype(BF16) for grad in (grad_w_o, grad_w_co, grad_w_cq)])
+    local = swap_blocks(pick_blocks(local.reshape(3, chips, 2, shard_rows, model), "core", 2), "core")
+    grad_heads, local, down_parts = meet(grad_heads, local, down_parts)
+
+    def reduce_headed(inputs, grads):
+        headed = dot_tn(inputs, grads).astype(BF16)
+        headed = headed.reshape(shards, groups, part_rows, grads.shape[1])
+        return swap_blocks(pick_blocks(headed, "dp", 1), "dp")
+
+    def send_headed(headed):
+        headed = tree_sum(headed).astype(BF16)
+        return send_rows(headed.reshape(chips, 2, part_rows, headed.shape[2]))
+
+    def headed_rows(headed):
+        count = headed[0].shape[2] // width
+        headed = join_rows(headed).reshape(shards, part_rows, count, width)
+        return headed.transpose(2, 1, 0, 3).reshape(count, part_rows, model)
+
+    local = tree_sum(local).astype(BF16).reshape(3, chips, groups, part_rows, model)
+    local = swap_blocks(pick_blocks(local, "dp", 2), "dp")
+    grad_flat = self_backward(
         piece_starts, query, key, value, out_heads, grad_heads, self_lse, block
     )
-    grad_qkv = jnp.stack([grad_q, grad_k, grad_v])
-    grad_rows = lax.all_to_all(
-        grad_qkv.reshape(3, shards, rows, width), SEQ, split_axis=1, concat_axis=1, tiled=True
-    )
-    grad_rows = grad_rows.transpose(0, 2, 1, 3).reshape(3, rows, model)
-    grad_normed_one = (
-        dot_nt(grad_rows[0], late[0]) + dot_nt(grad_rows[1], late[1]) + dot_nt(grad_rows[2], late[2])
-    )
+    grad_flat, local = meet(grad_flat, local)
+
+    scale = 1.0 / math.sqrt(tokens * groups)
+    partial = dot_nt(grad_flat, to_heads).astype(BF16)
+    grad_flat, local, down_parts = after((grad_flat, local, down_parts), partial)
+    grad_normed_one = lax.psum_scatter(partial, SEQ, scatter_dimension=0, tiled=True)
+    self_part = reduce_headed(normed_all, grad_flat)
+    whole_down = join_parts(down_parts, 0)
+    local = pick_blocks(tree_sum(local).astype(BF16), "chip", 1)
+    self_part, whole_down = meet(self_part, whole_down)
+    local = swap_blocks(local, "chip")
+    sum_down, *upd_down = adam_call(whole_down, scale, ffn_out, first_ffn_out, second_ffn_out)
+    local, sum_down, grad_ckv, grad_up = meet(local, sum_down, grad_ckv, grad_up)
+    cross_part = reduce_headed(encoder_all, jnp.concatenate([grad_ckv[0], grad_ckv[1]], axis=1))
+    headed = send_headed(
+        [jnp.concatenate([left, right], axis=2) for left, right in zip(self_part, cross_part)]
+    )
+    ckv_rows = lax.all_to_all(
+        grad_ckv.reshape(2, shards, enc_rows, width).transpose(1, 0, 2, 3),
+        SEQ,
+        split_axis=0,
+        concat_axis=0,
+        tiled=True,
+    )
+    up_parts = dp_gather(after(grad_up, cross_part[0]))
+    headed = headed_rows(headed)
+    local = tree_sum(local).astype(BF16)
+    up_parts, headed = meet(up_parts, headed)
+    attn_parts = dp_gather(jnp.concatenate([headed[:3], local[2:], headed[3:], local[:2]]))
+    whole_up = join_columns(up_parts, unit_cut)
+    sum_up, *upd_up = adam_call(whole_up, scale, ffn_in, first_ffn_in, second_ffn_in)
+    attn_parts, sum_up, ckv_rows = meet(attn_parts, sum_up, ckv_rows)
+    whole_attn = join_parts(attn_parts, 1).reshape(8, shard_rows, model)
+    ckv_rows = ckv_rows.transpose(1, 2, 0, 3).reshape(2, enc_rows, model)
+    grad_encoder = dot_nt(ckv_rows[0], w_ck) + dot_nt(ckv_rows[1], w_cv)
+    grad_normed_one = after(grad_normed_one, whole_attn).astype(F32)
     norm_part, grad_gain_one, grad_shift_one = norm_one_back(grad_normed_one)
     grad_hidden = grad_first + norm_part
-
-    grad_w_ck = dot_tn(encoder, grad_ckv[0])
-    grad_w_cv = dot_tn(encoder, grad_ckv[1])
-    grad_encoder = dot_nt(grad_ckv[0], w_ck) + dot_nt(grad_ckv[1], w_cv)
-
-    index = lax.axis_index("dp")
-
-    def dp_parts(grad):
-        axis = grad.ndim - 3
-        blocks = [
-            lax.dynamic_index_in_dim(grad, index ^ k, axis, keepdims=False) for k in range(groups)
-        ]
-        return dp_scatter(blocks)
-
-    local = jnp.stack([grad_w_o, grad_w_co, grad_w_cq, grad_w_ck, grad_w_cv])
-    local = dp_parts(local.reshape(5, shards, groups, part_rows, model)).astype(BF16)
-    local = local.reshape(5, shards * part_rows, model)
-    local = lax.psum_scatter(local, SEQ, scatter_dimension=1, tiled=True)
-    headed = dot_tn(normed_all, jnp.concatenate([grad_q, grad_k, grad_v], axis=1))
-    headed = dp_parts(headed.reshape(shards, groups, part_rows, 3 * width)).astype(BF16)
-    headed = lax.all_to_all(headed, SEQ, split_axis=0, concat_axis=0, tiled=True)
-    headed = headed.reshape(shards, part_rows, 3, width).transpose(2, 1, 0, 3)
-    headed = headed.reshape(3, part_rows, model)
-
-    scale = 1.0 / math.sqrt(tokens * groups)
-    local = dp_join(local)
-    headed = dp_join(headed)
-
-    def whole_rows(parts):
-        return parts.transpose(1, 0, 2, 3).reshape(parts.shape[1], shard_rows, model)
-
-    sum_out = whole_rows(local[:, :2]).astype(F32) * scale
-    sum_in = (
-        jnp.concatenate([whole_rows(headed), whole_rows(local[:, 2:])], axis=0).astype(F32) * scale
-    )
-    sum_down = dp_join(grad_down).reshape(groups * unit_cut, model).astype(F32) * scale
-    sum_up = dp_join(grad_up.reshape(shard_rows, shards, unit_cut))
-    sum_up = sum_up.transpose(1, 2, 0, 3).reshape(shard_rows, hidden_units).astype(F32) * scale
     sum_norms = jnp.stack(
         [
             grad_gain_one,
@@ -589,13 +818,11 @@
             grad_shift_three,
         ]
     )
-    norm_total = lax.psum(sum_norms * scale, ("dp",) + SEQ)
-
-    upd_in = adam_update(attn_in, sum_in, first_attn_in, second_attn_in)
-    upd_out = adam_update(attn_out, sum_out, first_attn_out, second_attn_out)
-    upd_up = adam_update(ffn_in, sum_up, first_ffn_in, second_ffn_in)
-    upd_down = adam_update(ffn_out, sum_down, first_ffn_out, second_ffn_out)
+    norm_total = sum_everywhere(sum_norms * scale)
+    sum_in, *upd_in = adam_call(whole_attn[:6], scale, attn_in, first_attn_in, second_attn_in)
+    sum_out, *upd_out = adam_call(whole_attn[6:], scale, attn_out, first_attn_out, second_attn_out)
     upd_norms = adam_update(norms, norm_total, first_norms, second_norms)
+    out_hidden = second_sum + tree_sum(hidden_parts)
     return (
         out_hidden,
         grad_hidden,

time: 839 us -> 645 us (0.77)
  blocking collectives: 127 us -> 0 us
  waiting for transfers between devices: 286 us -> 176 us
  Pallas kernels: 72.2 us -> 135 us
  starting transfers between devices: 55.8 us -> 90.2 us
  other arithmetic: 60.5 us -> 35.6 us
  local copies, waits for them, and re-layouts: 102 us -> 79.9 us
    psum x1 -> x0, blocking collectives: 112 us -> none  [on_device(): norm_total = lax.psum(sum_norms * scale, ('dp',) + SEQ)]
    ppermute x18 -> x60, waiting for transfers between devices: 47.4 us -> 153 us  [swap(): lax.ppermute(values, axis, [(index, index ^ offset) for index in range(co...]
    all_gather x5 -> x4, waiting for transfers between devices: 110 us -> 5.82 us  [the longest x1 5.81 us: on_device(): second = lax.all_gather(after(second, qkv), SEQ, axis=1, tiled=True)]
    all_to_all x6 -> x2, waiting for transfers between devices: 89.7 us -> 0.01 us  [the longest x1 0.01 us: on_device(): lax.all_to_all(to_heads, SEQ, split_axis=0, concat_axis=0, tiled=True)]
    pallas_call x1 -> x13, Pallas kernels: 17.1 us -> 79.7 us  [the longest x4 37.5 us: adam_call(): pl.pallas_call(functools.partial(adam_kernel, scale), out_shape=(flat,) *...]
    ppermute x18 -> x60, starting transfers between devices: 22.1 us -> 70.8 us  [swap(): lax.ppermute(values, axis, [(index, index ^ offset) for index in range(co...]
    mul x5 -> x1, other arithmetic: 31.6 us -> 0.73 us  [adam_update(): return (first_new, second_new, -RATE * (step_size + DECAY * weight))]
    unnamed x139 -> x192, local copies, waits for them, and re-layouts: 61 us -> 33.1 us
  transfers between devices with their start and end apart: 36 -> 73, of which waited for: 22 -> 30; matrix products, arithmetic and copies ran while one was open for 27% -> 26% of each run, Pallas kernels for 7% -> 21%
where the time goes in v2:
time: 645 us; the launch traced here: 636 us
  waiting for transfers between devices  176 us (27%)
  Pallas kernels  135 us (21%)
  matrix products  104 us (16%)
  starting transfers between devices  90.2 us (14%)
  local copies, waits for them, and re-layouts  79.9 us (12%)
  other arithmetic  35.6 us (6%)
  between operations  15.4 us (2%)
    ppermute x60, waiting for transfers between devices, swap(): lax.ppermute(values, axis, [(index, index ^ offset) for index in range(co...  153 us
    ppermute x60, starting transfers between devices, swap(): lax.ppermute(values, axis, [(index, index ^ offset) for index in range(co...  70.8 us
    pallas_call x4, Pallas kernels, adam_call(): pl.pallas_call(functools.partial(adam_kernel, scale), out_shape=(flat,) *...  37.5 us
    dot_general x8, matrix products, dot_f32(): return jnp.dot(left, right, preferred_element_type=F32)  37.3 us
    dot_general x8, matrix products, dot_nt(): return lax.dot_general(left, right, NT, preferred_element_type=F32)  36.6 us
    unnamed x192, local copies, waits for them, and re-layouts  33.1 us
    dot_general x7, matrix products, dot_tn(): return lax.dot_general(left, right, TN, preferred_element_type=F32)  29.5 us
    pallas_call x1, Pallas kernels, self_backward(): pl.pallas_call(functools.partial(self_bwd_kernel, heads, pieces, block),...  24.7 us
  transfers between devices with their start and end apart: 73, of which 30 were waited for; matrix products, arithmetic and copies ran while one was open for 26% of the time, Pallas kernels for 21%

profile of v2, /device:TPU:0, one launch (start us, length us, event | category | flops | bytes accessed | tf_op | source)
XLA Modules:
  0.0 636.3 jit_solution(11716002386412399940)
XLA Ops:
  63.6 7.1 %collective-permute-done.1.refs_2_ = bf16[8,32,384]{2,1,0:T(8,128)(2,1)} collective-permute-done((bf16[8,32,384]{2,1,0:T(8,128)(2,1)S(1)}, bf16[8,32,384]{2,1,0:T(8,128)(2,1)}, u32[]{:S(2)}, u32[]{:S(2)}) %collective-permute-start.1) | collective-permute-done | bytes 196640 | tf_op jit(solution)/shard_map/ppermute | solution.py:370
  80.8 19.9 %self_forward.1 = (bf16[2048,128]{1,0:T(8,128)(2,1)S(1)}, f32[2,8,2048]{2,1,0:T(8,128)S(1)}) custom-call(s32[1,2]{1,0:T(1,128)S(1)} %copy-done.34, bf16[2048,128]{1,0:T(8,128)(2,1)S(1)} %get-tuple-element.294.q_ref, bf16[2048,128]{1,0:T(8,128)(2,1)S(1)} %get-tuple-element.293.k_ref, bf16[2048,128]{1,0:T(8,128)(2,1)S(1)} %get-tuple-element.292.v_ref), custom_call_target="tpu_custom_call" | custom-call | flops 2147483648 | bytes 2097152 | tf_op jit(solution)/shard_map/self_forward/pallas_call | solution.py:137
  115.5 11.3 %collective-permute-done.6.refs_1_ = bf16[2,512,256]{2,1,0:T(8,128)(2,1)} collective-permute-done((bf16[2,512,256]{2,1,0:T(8,128)(2,1)S(1)}, bf16[2,512,256]{2,1,0:T(8,128)(2,1)}, u32[]{:S(2)}, u32[]{:S(2)}) %collective-permute-start.6) | collective-permute-done | bytes 524320 | tf_op jit(solution)/shard_map/ppermute | solution.py:370
  126.8 10.0 %collective-permute-done.7.refs_2_ = bf16[2,512,256]{2,1,0:T(8,128)(2,1)} collective-permute-done((bf16[2,512,256]{2,1,0:T(8,128)(2,1)S(1)}, bf16[2,512,256]{2,1,0:T(8,128)(2,1)}, u32[]{:S(2)}, u32[]{:S(2)}) %collective-permute-start.7) | collective-permute-done | bytes 524320 | tf_op jit(solution)/shard_map/ppermute | solution.py:370
  168.0 7.8 %collective-permute-done.12.refs_1_ = bf16[3,512,256]{2,1,0:T(8,128)(2,1)} collective-permute-done((bf16[3,512,256]{2,1,0:T(8,128)(2,1)}, bf16[3,512,256]{2,1,0:T(8,128)(2,1)}, u32[]{:S(2)}, u32[]{:S(2)}) %collective-permute-start.12) | collective-permute-done | bytes 786464 | tf_op jit(solution)/shard_map/ppermute | solution.py:370
  175.9 17.4 %collective-permute-done.13.refs_2_ = bf16[3,512,256]{2,1,0:T(8,128)(2,1)} collective-permute-done((bf16[3,512,256]{2,1,0:T(8,128)(2,1)}, bf16[3,512,256]{2,1,0:T(8,128)(2,1)}, u32[]{:S(2)}, u32[]{:S(2)}) %collective-permute-start.13) | collective-permute-done | bytes 786464 | tf_op jit(solution)/shard_map/ppermute | solution.py:370
  215.0 11.0 %cross_forward.1 = (bf16[256,1024]{1,0:T(8,128)(2,1)S(1)}, f32[16,8,256]{2,1,0:T(8,128)S(1)}) custom-call(bf16[256,1024]{1,0:T(8,128)(2,1)S(1)} %copy-done.6, bf16[2,1024,1024]{2,1,0:T(8,128)(2,1)S(1)} %pad_maximum_fusion.1.k.v.k_ref.v_ref, bf16[2,1024,1024]{2,1,0:T(8,128)(2,1)S(1)} %pad_maximum_fusion.1.k.v.k_ref.v_ref), custom_call_target="tpu_custom_call" | custom-call | flops 1073741824 | bytes 5242880 | tf_op jit(solution)/shard_map/cross_forward/pallas_call | solution.py:282
  234.3 8.9 %collective-permute-done.20 = bf16[256,1024]{1,0:T(8,128)(2,1)S(1)} collective-permute-done((bf16[256,1024]{1,0:T(8,128)(2,1)S(1)}, bf16[256,1024]{1,0:T(8,128)(2,1)S(1)}, u32[]{:S(2)}, u32[]{:S(2)}) %collective-permute-start.20) | collective-permute-done | bytes 524320 | tf_op jit(solution)/shard_map/ppermute | solution.py:370
  243.2 10.8 %collective-permute-done.19 = bf16[256,1024]{1,0:T(8,128)(2,1)S(1)} collective-permute-done((bf16[256,1024]{1,0:T(8,128)(2,1)S(1)}, bf16[256,1024]{1,0:T(8,128)(2,1)S(1)}, u32[]{:S(2)}, u32[]{:S(2)}) %collective-permute-start.19) | collective-permute-done | bytes 524320 | tf_op jit(solution)/shard_map/ppermute | solution.py:370
  254.7 12.2 %multiply_convert_fusion.1 = (bf16[1024,2048]{1,0:T(8,128)(2,1)}, f32[1024,2048]{1,0:T(8,128)}) fusion(bf16[1024,2048]{1,0:T(8,128)(2,1)} %all-gather.12.cloned.1.call-done, bf16[256,1024]{1,0:T(8,128)(2,1)} %copy-done.86, bf16[256,1024]{1,0:T(8,128)(2,1)} %copy-done.87, bf16[256,1024]{1,0:T(8,128)(2,1)} %collective-permute-done.18, ...), kind=kOutput, calls=%fused_computation.1 | convolution fusion | flops 4322230272 | bytes 18874368 | tf_op jit(solution)/shard_map/dot_general | solution.py:44
  266.9 11.9 %multiply_convert_fusion = bf16[1024,2048]{1,0:T(8,128)(2,1)S(1)} fusion(f32[1024,2048]{1,0:T(8,128)} %get-tuple-element.330, bf16[1024,1024]{1,0:T(8,128)(2,1)} %copy-done.67, bf16[2048,1024]{1,0:T(8,128)(2,1)} %all-gather.14.cloned.1.call-done), kind=kOutput, calls=%fused_computation | convolution fusion | flops 4332716032 | bytes 18874368 | tf_op jit(solution)/shard_map/dot_general | solution.py:48
  290.9 9.4 %convolution_convert_fusion.2 = bf16[1024,2048]{1,0:T(8,128)(2,1)} fusion(bf16[1024,2048]{1,0:T(8,128)(2,1)} %copy-done.88, bf16[256,1024]{1,0:T(8,128)(2,1)} %copy-done.86, bf16[256,1024]{1,0:T(8,128)(2,1)} %copy-done.87, bf16[256,1024]{1,0:T(8,128)(2,1)} %collective-permute-done.18, bf16[256,1024]{1,0:T(8,128)(2,1)} %copy-done.63), kind=kOutput, calls=%fused_computation.10 | convolution fusion | flops 4305453056 | bytes 10485760 | tf_op jit(solution)/shard_map/dot_general | solution.py:52
  305.9 11.3 %collective-permute-done.21 = bf16[256,1024]{1,0:T(8,128)(2,1)S(1)} collective-permute-done((bf16[256,1024]{1,0:T(8,128)(2,1)S(1)}, bf16[256,1024]{1,0:T(8,128)(2,1)S(1)}, u32[]{:S(2)}, u32[]{:S(2)}) %collective-permute-start.21) | collective-permute-done | bytes 524320 | tf_op jit(solution)/shard_map/ppermute | solution.py:370
  317.1 9.8 %collective-permute-done.22 = bf16[256,1024]{1,0:T(8,128)(2,1)S(1)} collective-permute-done((bf16[256,1024]{1,0:T(8,128)(2,1)S(1)}, bf16[256,1024]{1,0:T(8,128)(2,1)S(1)}, u32[]{:S(2)}, u32[]{:S(2)}) %collective-permute-start.22) | collective-permute-done | bytes 524320 | tf_op jit(solution)/shard_map/ppermute | solution.py:370
  344.5 17.1 %cross_backward.1 = (bf16[256,1024]{1,0:T(8,128)(2,1)S(1)}, bf16[8,2,1024,128]{3,2,1,0:T(8,128)(2,1)}) custom-call(bf16[256,1024]{1,0:T(8,128)(2,1)S(1)} %copy-done.7, bf16[2,1024,1024]{2,1,0:T(8,128)(2,1)} %copy-done, bf16[2,1024,1024]{2,1,0:T(8,128)(2,1)} %copy-done, bf16[256,1024]{1,0:T(8,128)(2,1)S(1)} %copy-done.3, ...), custom_call_target="tpu_custom_call" | custom-call | flops 2684354560 | bytes 10485760 | tf_op jit(solution)/shard_map/cross_backward/pallas_call | solution.py:340
  392.2 15.7 %all-to-all-done.2 = bf16[8,256,128]{2,1,0:T(8,128)(2,1)} async-done(((bf16[8,256,128]{2,1,0:T(8,128)(2,1)}), bf16[8,256,128]{2,1,0:T(8,128)(2,1)}, u32[]{:S(2)}, u32[]{:S(2)}) %all-to-all-start.2) | async-done | bytes 524320 | tf_op jit(solution)/shard_map/all_to_all | solution.py:737
  407.8 7.3 %collective-permute-done.29.refs_2_ = bf16[256,1024]{1,0:T(8,128)(2,1)} collective-permute-done((bf16[256,1024]{1,0:T(8,128)(2,1)}, bf16[256,1024]{1,0:T(8,128)(2,1)}, u32[]{:S(2)}, u32[]{:S(2)}) %collective-permute-start.29) | collective-permute-done | bytes 524320 | tf_op jit(solution)/shard_map/ppermute | solution.py:370
  424.7 24.7 %self_backward.1 = bf16[2048,384]{1,0:T(8,128)(2,1)S(1)} custom-call(s32[1,2]{1,0:T(1,128)S(1)} %copy-done.34, bf16[2048,128]{1,0:T(8,128)(2,1)S(1)} %copy-done.28, bf16[2048,128]{1,0:T(8,128)(2,1)S(1)} %copy-done.26, bf16[2048,128]{1,0:T(8,128)(2,1)S(1)} %copy-done.24, bf16[2048,128]{1,0:T(8,128)(2,1)S(1)} %copy-done.22, bf16[2048,128]{1,0:T(8,128)(2,1)} %bitcast.33.do_ref, ...), custom_call_target="tpu_custom_call" | custom-call | flops 5368709120 | bytes 4194304 | tf_op jit(solution)/shard_map/self_backward/pallas_call | solution.py:238
  449.4 8.6 %collective-permute-done.32 = bf16[3,4,32,1024]{3,2,1,0:T(8,128)(2,1)} collective-permute-done((bf16[3,4,32,1024]{3,2,1,0:T(8,128)(2,1)S(1)}, bf16[3,4,32,1024]{3,2,1,0:T(8,128)(2,1)}, u32[]{:S(2)}, u32[]{:S(2)}) %collective-permute-start.32) | collective-permute-done | bytes 786464 | tf_op jit(solution)/shard_map/ppermute | solution.py:370
  480.9 12.4 %adam.4 = (f32[1024,1024]{1,0:T(8,128)}, f32[1024,1024]{1,0:T(8,128)}, f32[1024,1024]{1,0:T(8,128)}, f32[1024,1024]{1,0:T(8,128)}) custom-call(bf16[1024,1024]{1,0:T(8,128)(2,1)S(1)} %bitcast.215, f32[1024,1024]{1,0:T(8,128)} %w_ref.2, f32[1024,1024]{1,0:T(8,128)} %m1_ref.2, f32[1024,1024]{1,0:T(8,128)} %m2_ref.2), custom_call_target="tpu_custom_call" | custom-call | flops 20971520 | bytes 31457280 | tf_op jit(solution)/shard_map/adam/pallas_call | solution.py:581
  495.7 8.1 %collective-permute-done.36 = bf16[3,32,1024]{2,1,0:T(8,128)(2,1)} collective-permute-done((bf16[3,32,1024]{2,1,0:T(8,128)(2,1)}, bf16[3,32,1024]{2,1,0:T(8,128)(2,1)}, u32[]{:S(2)}, u32[]{:S(2)}) %collective-permute-start.36) | collective-permute-done | bytes 196640 | tf_op jit(solution)/shard_map/ppermute | solution.py:370
  539.7 13.9 %collective-permute-done.48.refs_2_ = bf16[2,32,640]{2,1,0:T(8,128)(2,1)S(1)} collective-permute-done((bf16[2,32,640]{2,1,0:T(8,128)(2,1)}, bf16[2,32,640]{2,1,0:T(8,128)(2,1)S(1)}, u32[]{:S(2)}, u32[]{:S(2)}) %collective-permute-start.48) | collective-permute-done | bytes 81952 | tf_op jit(solution)/shard_map/ppermute | solution.py:370
  571.1 12.7 %adam.5 = (f32[128,8192]{1,0:T(8,128)}, f32[128,8192]{1,0:T(8,128)}, f32[128,8192]{1,0:T(8,128)}, f32[128,8192]{1,0:T(8,128)}) custom-call(bf16[128,8192]{1,0:T(8,128)(2,1)S(1)} %place.12.g_ref, f32[128,8192]{1,0:T(8,128)} %w_ref.3, f32[128,8192]{1,0:T(8,128)} %m1_ref.3, f32[128,8192]{1,0:T(8,128)} %m2_ref.3), custom_call_target="tpu_custom_call" | custom-call | flops 20971520 | bytes 31457280 | tf_op jit(solution)/shard_map/adam/pallas_call | solution.py:581
  603.9 9.4 %adam.6 = (f32[768,1024]{1,0:T(8,128)}, f32[768,1024]{1,0:T(8,128)}, f32[768,1024]{1,0:T(8,128)}, f32[768,1024]{1,0:T(8,128)}) custom-call(bf16[768,1024]{1,0:T(8,128)(2,1)S(1)} %bitcast.217, f32[768,1024]{1,0:T(8,128)S(1)} %bitcast.216, f32[768,1024]{1,0:T(8,128)} %bitcast.231, f32[768,1024]{1,0:T(8,128)} %bitcast.232), custom_call_target="tpu_custom_call" | custom-call | flops 15728640 | bytes 23592960 | tf_op jit(solution)/shard_map/adam/pallas_call | solution.py:581
  (451 shorter events, 332.1 us)
Async XLA Ops:
  7.2 66.1 %all-gather.6.cloned.1.call-start = ((), (), s32[]{:S(2)}) async-start(), calls=%async_computation.8 | async-start | bytes 4718592 | tf_op jit(solution)/shard_map/all_gather | solution.py:645
  14.6 58.7 %collective-permute-start.3 = (bf16[256,1024]{1,0:T(8,128)(2,1)}, bf16[256,1024]{1,0:T(8,128)(2,1)}, u32[]{:S(2)}, u32[]{:S(2)}) collective-permute-start(bf16[256,1024]{1,0:T(8,128)(2,1)} %param.22), channel_id=1, source_target_pairs={{0,8},{8,0},{16,24},{24,16},{1,9},{9,1},{17,25},{25,17},{2,10},{10... | collective-permute-start | bytes 1572872 | tf_op jit(solution)/shard_map/ppermute | solution.py:370
  17.6 55.7 %collective-permute-start.4 = (bf16[256,1024]{1,0:T(8,128)(2,1)}, bf16[256,1024]{1,0:T(8,128)(2,1)}, u32[]{:S(2)}, u32[]{:S(2)}) collective-permute-start(bf16[256,1024]{1,0:T(8,128)(2,1)} %param.22), channel_id=1, source_target_pairs={{0,16},{8,24},{16,0},{24,8},{1,17},{9,25},{17,1},{25,9},{2,18},{10... | collective-permute-start | bytes 1572872 | tf_op jit(solution)/shard_map/ppermute | solution.py:370
  19.1 54.2 %collective-permute-start.5 = (bf16[256,1024]{1,0:T(8,128)(2,1)}, bf16[256,1024]{1,0:T(8,128)(2,1)}, u32[]{:S(2)}, u32[]{:S(2)}) collective-permute-start(bf16[256,1024]{1,0:T(8,128)(2,1)} %param.22), channel_id=1, source_target_pairs={{0,24},{8,16},{16,8},{24,0},{1,25},{9,17},{17,9},{25,1},{2,26},{10... | collective-permute-start | bytes 1572872 | tf_op jit(solution)/shard_map/ppermute | solution.py:370
  29.0 74.9 %all-gather.8.cloned.1.call-start = ((), (), s32[]{:S(2)}) async-start(), calls=%async_computation.9 | async-start | bytes 1179648 | tf_op jit(solution)/shard_map/all_gather | solution.py:670
  73.3 78.1 %all-gather.10.cloned.1.call-start = ((), (), s32[]{:S(2)}) async-start(), calls=%async_computation.10 | async-start | bytes 4128768 | tf_op jit(solution)/shard_map/all_gather | solution.py:672
  79.3 175.4 %all-gather.12.cloned.1.call-start = ((), (), s32[]{:S(2)}) async-start(), calls=%async_computation.11 | async-start | bytes 4718592 | tf_op jit(solution)/shard_map/all_gather | solution.py:676
  106.1 34.4 %all-to-all-start.1 = ((bf16[8,256,128]{1,2,0:T(8,128)(2,1)}), bf16[8,256,128]{1,2,0:T(8,128)(2,1)}, u32[]{:S(2)}, u32[]{:S(2)}) async-start(bf16[8,256,128]{1,2,0:T(8,128)(2,1)} %copy.82), calls=%async_computation.1 | async-start | bytes 1048576 | tf_op jit(solution)/shard_map/all_to_all | solution.py:678
  110.8 156.1 %all-gather.14.cloned.1.call-start = ((), (), s32[]{:S(2)}) async-start(), calls=%async_computation.12 | async-start | bytes 4718592 | tf_op jit(solution)/shard_map/all_gather | solution.py:682
  140.5 234.6 %reduce-scatter.5.cloned.1.call-start = ((), (), s32[]{:S(2)}) async-start(), calls=%async_computation.13 | async-start | bytes 4718592 | tf_op jit(solution)/shard_map/reduce_scatter | solution.py:712
  156.7 36.6 %collective-permute-start.13 = (bf16[3,512,256]{2,1,0:T(8,128)(2,1)}, bf16[3,512,256]{2,1,0:T(8,128)(2,1)}, u32[]{:S(2)}, u32[]{:S(2)}) collective-permute-start(bf16[3,512,256]{2,1,0:T(8,128)(2,1)} %constant_dynamic-slice_fusion.2), channel_id=1, source_target_pairs={{0,16},{8,24},{16,0},{24,8},{1,17},{9,25},{17,1},{25,9},{2,18},{10... | collective-permute-start | bytes 2359304 | tf_op jit(solution)/shard_map/ppermute | solution.py:370
  158.1 35.1 %collective-permute-start.14 = (bf16[3,512,256]{2,1,0:T(8,128)(2,1)}, bf16[3,512,256]{2,1,0:T(8,128)(2,1)}, u32[]{:S(2)}, u32[]{:S(2)}) collective-permute-start(bf16[3,512,256]{2,1,0:T(8,128)(2,1)} %constant_dynamic-slice_fusion.2), channel_id=1, source_target_pairs={{0,24},{8,16},{16,8},{24,0},{1,25},{9,17},{17,9},{25,1},{2,26},{10... | collective-permute-start | bytes 2359304 | tf_op jit(solution)/shard_map/ppermute | solution.py:370
  290.9 202.4 %reduce-scatter.11.cloned.1.call-start = ((), (), s32[]{:S(2)}) async-start(), calls=%async_computation.16 | async-start | bytes 4718592 | tf_op jit(solution)/shard_map/reduce_scatter | solution.py:714
  300.4 192.9 %reduce-scatter.9.cloned.1.call-start = ((), (), s32[]{:S(2)}) async-start(), calls=%async_computation.15 | async-start | bytes 4718592 | tf_op jit(solution)/shard_map/reduce_scatter | solution.py:730
  336.4 26.0 %collective-permute-start.24 = (bf16[256,1024]{1,0:T(8,128)(2,1)S(1)}, bf16[256,1024]{1,0:T(8,128)(2,1)S(1)}, u32[]{:S(2)}, u32[]{:S(2)}) collective-permute-start(bf16[256,1024]{1,0:T(8,128)(2,1)S(1)} %get-tuple-element.185), channel_id=1, source_target_pairs={{0,8},{8,0},{16,24},{24,16},{1,9},{9,1},{17,25},{25,17},{2,10},{10... | collective-permute-start | bytes 1572872 | tf_op jit(solution)/shard_map/ppermute | solution.py:370
  383.5 31.6 %collective-permute-start.27 = (bf16[3,4,128,1024]{3,2,1,0:T(8,128)(2,1)}, bf16[3,4,128,1024]{3,2,1,0:T(8,128)(2,1)}, u32[]{:S(2)}, u32[]{:S(2)}) collective-permute-start(bf16[3,4,128,1024]{3,2,1,0:T(8,128)(2,1)} %get-tuple-element.279), channel_id=1, source_target_pairs={{0,1},{1,0},{2,3},{3,2},{4,5},{5,4},{6,7},{7,6},{8,9},{9,8},{10,11... | collective-permute-start | bytes 9437192 | tf_op jit(solution)/shard_map/ppermute | solution.py:370
  388.5 202.7 %reduce-scatter.7.cloned.1.call-start = ((), (), s32[]{:S(2)}) async-start(), calls=%async_computation.14 | async-start | bytes 4718592 | tf_op jit(solution)/shard_map/reduce_scatter | solution.py:778
  421.1 28.3 %collective-permute-start.31 = (bf16[3,4,32,1024]{3,2,1,0:T(8,128)(2,1)S(1)}, bf16[3,4,32,1024]{3,2,1,0:T(8,128)(2,1)}, u32[]{:S(2)}, u32[]{:S(2)}) collective-permute-start(bf16[3,4,32,1024]{3,2,1,0:T(8,128)(2,1)S(1)} %get-tuple-element.283), channel_id=1, source_target_pairs={{0,8},{8,0},{16,24},{24,16},{1,9},{9,1},{17,25},{25,17},{2,10},{10... | collective-permute-start | bytes 2359304 | tf_op jit(solution)/shard_map/ppermute | solution.py:370
  422.2 35.8 %collective-permute-start.32 = (bf16[3,4,32,1024]{3,2,1,0:T(8,128)(2,1)S(1)}, bf16[3,4,32,1024]{3,2,1,0:T(8,128)(2,1)}, u32[]{:S(2)}, u32[]{:S(2)}) collective-permute-start(bf16[3,4,32,1024]{3,2,1,0:T(8,128)(2,1)S(1)} %get-tuple-element.282), channel_id=1, source_target_pairs={{0,16},{8,24},{16,0},{24,8},{1,17},{9,25},{17,1},{25,9},{2,18},{10... | collective-permute-start | bytes 2359304 | tf_op jit(solution)/shard_map/ppermute | solution.py:370
  423.2 34.9 %collective-permute-start.33 = (bf16[3,4,32,1024]{3,2,1,0:T(8,128)(2,1)S(1)}, bf16[3,4,32,1024]{3,2,1,0:T(8,128)(2,1)}, u32[]{:S(2)}, u32[]{:S(2)}) collective-permute-start(bf16[3,4,32,1024]{3,2,1,0:T(8,128)(2,1)S(1)} %get-tuple-element.281), channel_id=1, source_target_pairs={{0,24},{8,16},{16,8},{24,0},{1,25},{9,17},{17,9},{25,1},{2,26},{10... | collective-permute-start | bytes 2359304 | tf_op jit(solution)/shard_map/ppermute | solution.py:370
  516.5 43.5 %collective-permute-start.40 = (bf16[128,2048]{1,0:T(8,128)(2,1)}, bf16[128,2048]{1,0:T(8,128)(2,1)}, u32[]{:S(2)}, u32[]{:S(2)}) collective-permute-start(bf16[128,2048]{1,0:T(8,128)(2,1)} %reduce-scatter.11.cloned.1.call-done.refs_0_), channel_id=1, source_target_pairs={{0,8},{8,0},{16,24},{24,16},{1,9},{9,1},{17,25},{25,17},{2,10},{10... | collective-permute-start | bytes 1572872 | tf_op jit(solution)/shard_map/ppermute | solution.py:370
  517.3 42.7 %collective-permute-start.41 = (bf16[128,2048]{1,0:T(8,128)(2,1)}, bf16[128,2048]{1,0:T(8,128)(2,1)}, u32[]{:S(2)}, u32[]{:S(2)}) collective-permute-start(bf16[128,2048]{1,0:T(8,128)(2,1)} %reduce-scatter.11.cloned.1.call-done.refs_0_), channel_id=1, source_target_pairs={{0,16},{8,24},{16,0},{24,8},{1,17},{9,25},{17,1},{25,9},{2,18},{10... | collective-permute-start | bytes 1572872 | tf_op jit(solution)/shard_map/ppermute | solution.py:370
  518.7 41.3 %collective-permute-start.42 = (bf16[128,2048]{1,0:T(8,128)(2,1)}, bf16[128,2048]{1,0:T(8,128)(2,1)}, u32[]{:S(2)}, u32[]{:S(2)}) collective-permute-start(bf16[128,2048]{1,0:T(8,128)(2,1)} %reduce-scatter.11.cloned.1.call-done.refs_0_), channel_id=1, source_target_pairs={{0,24},{8,16},{16,8},{24,0},{1,25},{9,17},{17,9},{25,1},{2,26},{10... | collective-permute-start | bytes 1572872 | tf_op jit(solution)/shard_map/ppermute | solution.py:370
  528.3 55.6 %all-to-all-start.3 = ((bf16[8,2,128,128]{2,3,1,0:T(8,128)(2,1)}), bf16[8,2,128,128]{2,3,1,0:T(8,128)(2,1)}, u32[]{:S(2)}, u32[]{:S(2)}) async-start(bf16[8,2,128,128]{2,3,1,0:T(8,128)(2,1)} %bitcast.238), calls=%async_computation.7 | async-start | bytes 1048576 | tf_op jit(solution)/shard_map/all_to_all | solution.py:790
  (139 other events, 1813.8 us)
Sparse Core Ops, SparseCore 0:
  14.7 54.0 all-gather.5
  73.4 22.2 all-gather.7
  97.9 53.4 all-gather.9
  153.5 45.8 all-gather.11
  201.4 45.8 all-gather.13
  291.0 47.6 reduce-scatter.4
  341.5 48.1 reduce-scatter.10
  392.6 49.7 reduce-scatter.8
  462.6 62.0 reduce-scatter.6

commit v3 on v2

--- a/solution.py
+++ b/solution.py
@@ -393,11 +393,9 @@
     return parts[0]
 
 
-def sum_everywhere(values):
-    for axis in ("core", "chip", "dp"):
-        count = lax.axis_size(axis)
-        values = tree_sum([values] + [swap(values, axis, k) for k in range(1, count)])
-    return values
+def sum_along(values, axis):
+    count = lax.axis_size(axis)
+    return tree_sum([values] + [swap(values, axis, k) for k in range(1, count)])
 
 
 def position():
@@ -483,12 +481,6 @@
 
 def share_columns(parts):
     return [swap(part, "core", 1) for part in parts]
-
-
-def send_rows(parts):
-    own, given = pick_blocks(parts, "core", 1)
-    both = jnp.stack([own, swap(given, "core", 1)], axis=1)
-    return swap_blocks(pick_blocks(both, "chip", 0), "chip")
 
 
 def join_rows(parts):
@@ -601,7 +593,7 @@
     bent = jnp.tanh(root * (values_in + 0.044715 * values_in * square))
     half = 0.5 * (1.0 + bent)
     slope = half + 0.5 * values_in * (1.0 - bent * bent) * root * (1.0 + 3.0 * 0.044715 * square)
-    return values_in * half, slope
+    return values_in * half, slope.astype(BF16)
 
 
 def on_device(
@@ -654,46 +646,55 @@
         cut = weights.reshape(weights.shape[0], shard_rows, groups, model // groups)
         return own_part(cut, 2).astype(BF16)
 
-    first = column_part(jnp.concatenate([attn_out[:1], attn_in[3:4]], axis=0))
-    second = column_part(jnp.concatenate([attn_in[4:], attn_out[1:]], axis=0))
     enc_rows = encoder.shape[0]
-    second = jnp.concatenate(
-        [second, encoder.reshape(enc_rows, groups, model // groups).transpose(1, 0, 2)], axis=0
-    )
+    keyed = jnp.concatenate(
+        [
+            column_part(attn_in[4:]),
+            encoder.reshape(enc_rows, groups, model // groups).transpose(1, 0, 2),
+        ],
+        axis=0,
+    )
+    outer = column_part(jnp.concatenate([attn_out[:1], attn_in[3:4], attn_out[1:]], axis=0))
     up = take_columns(ffn_in, shards, groups, unit_cut)
     down = own_part(ffn_out.reshape(groups, unit_cut, model), 0).astype(BF16)
     to_heads = join_parts(to_heads, 1).reshape(model, 3 * width)
-    normed_all, to_heads, grad_parts, first, second, up, down = meet(
-        normed_all, to_heads, grad_parts, first, second, up, down
-    )
-
-    first = lax.all_gather(first, SEQ, axis=1, tiled=True)
+    normed_all, to_heads, grad_parts, keyed, outer, up, down = meet(
+        normed_all, to_heads, grad_parts, keyed, outer, up, down
+    )
+
+    outer = lax.all_gather(outer, SEQ, axis=1, tiled=True)
     qkv = dot_f32(normed_all, to_heads).astype(BF16)
-    second = lax.all_gather(after(second, qkv), SEQ, axis=1, tiled=True)
+    keyed = lax.all_gather(after(keyed, qkv), SEQ, axis=1, tiled=True)
     query, key, value = [qkv[:, i * width : (i + 1) * width] for i in range(3)]
     out_heads, self_lse = self_forward(piece_starts, query, key, value, block)
-    out_heads, first = meet(out_heads, first)
     w_up = lax.all_gather(after(up, out_heads), SEQ, axis=0, tiled=True)
-    first_parts = fetch_columns(first)
     attended = lax.all_to_all(
         out_heads.reshape(shards, rows, width), SEQ, split_axis=0, concat_axis=0, tiled=True
     )
-    attended, first_parts = meet(attended, first_parts)
+    outer = after(outer, out_heads)
+    outer_parts = fetch_columns(outer[:2])
+    attended, outer_parts = meet(attended, outer_parts)
     w_down = lax.all_gather(after(down, attended), SEQ, axis=0, tiled=True)
-    first_shared = share_columns(first_parts)
+    outer_shared = share_columns(outer_parts)
+    cross_parts = fetch_columns(after(outer[2:], attended))
+    w_o, w_cq = join_fetched([outer[:2]] + outer_parts + outer_shared)
     attended = attended.transpose(1, 0, 2).reshape(rows, model)
-    attended, first_shared, second = meet(attended, first_shared, second)
-    second_parts = fetch_columns(second[:3])
-    encoder_all = second[3:].transpose(1, 0, 2).reshape(enc_rows * shards, model)
-    w_o, w_cq = join_fetched([first] + first_parts + first_shared)
     first_sum = resid_in + dot_f32(attended, w_o)
-
+    first_sum, cross_parts, keyed = meet(first_sum, cross_parts, keyed)
+
+    keyed_parts = fetch_columns(keyed[:2])
+    cross_shared = share_columns(cross_parts)
     normed_two, norm_two_back = jax.vjp(layer_norm, first_sum, gains[2], gains[3])
     normed_two = normed_two.astype(BF16)
     cross_queries = dot_f32(normed_two, w_cq).astype(BF16)
-    cross_queries, second_parts = meet(cross_queries, second_parts)
-    w_ck, w_cv, w_co = join_fetched([second[:3]] + second_parts + share_columns(second_parts))
+    encoder_all = keyed[2:].transpose(1, 0, 2).reshape(enc_rows * shards, model)
+    w_co = join_fetched([outer[2:]] + cross_parts + cross_shared)[0]
+    cross_queries, encoder_all, w_co, keyed_parts = meet(
+        cross_queries, encoder_all, w_co, keyed_parts
+    )
+    w_ck, w_cv = join_fetched([keyed[:2]] + keyed_parts + share_columns(keyed_parts))
     cross_kv = jnp.stack([dot_f32(encoder_all, w_ck), dot_f32(encoder_all, w_cv)]).astype(BF16)
+
     crossed, cross_lse = cross_forward(cross_queries, cross_kv)
     second_sum = first_sum + dot_f32(crossed, w_co)
 
@@ -703,30 +704,32 @@
     grad_tokens = jnp.concatenate(grad_parts, axis=0)
     activated, slope = gelu_both(dot_f32(ffn_tokens, w_up))
     activated = activated.astype(BF16)
+    grad_down = dot_tn(activated, grad_tokens).astype(BF16)
+    activated, slope = after((activated, slope), grad_down)
+    grad_down = lax.psum_scatter(grad_down, SEQ, scatter_dimension=0, tiled=True)
     grad_pre = (dot_nt(grad_tokens, w_down) * slope).astype(BF16)
     partial = dot_nt(grad_pre, w_up).astype(BF16)
     grad_three = swap_blocks([partial[k * rows : (k + 1) * rows] for k in range(groups)], "dp")
+
     activated, grad_pre = after((activated, grad_pre), partial)
-    grad_down = dot_tn(activated, grad_tokens).astype(BF16)
+    partial = dot_f32(activated, w_down)
     grad_up = dot_tn(ffn_tokens, grad_pre).astype(BF16)
-    grad_down = lax.psum_scatter(grad_down, SEQ, scatter_dimension=0, tiled=True)
-    activated, grad_three = after((activated, grad_three), grad_up)
+    grad_three, partial, grad_up = meet(grad_three, partial, grad_up)
     grad_up = lax.psum_scatter(grad_up, SEQ, scatter_dimension=0, tiled=True)
-    partial = dot_f32(activated, w_down)
     hidden_parts = [partial[:rows]] + [
         partial[k * rows : (k + 1) * rows].astype(BF16) for k in range(1, groups)
     ]
-    grad_three, hidden_parts = meet(grad_three, hidden_parts)
-    hidden_parts = swap_blocks(hidden_parts, "dp")
 
     norm_part, grad_gain_three, grad_shift_three = norm_three_back(tree_sum(grad_three))
     grad_second = grad_out.astype(F32) + norm_part
     grad_cross_branch = grad_second.astype(BF16)
+    grad_cross_branch, grad_down = meet(grad_cross_branch, grad_down)
+    down_parts = dp_gather(grad_down)
     grad_crossed = dot_nt(grad_cross_branch, w_co).astype(BF16)
     grad_cq, grad_ckv = cross_backward(
         cross_queries, cross_kv, crossed, grad_crossed, cross_lse, width
     )
-    grad_cq, hidden_parts, grad_ckv = meet(grad_cq, hidden_parts, grad_ckv)
+    grad_cq, down_parts, grad_ckv = meet(grad_cq, down_parts, grad_ckv)
     grad_ckv = lax.psum_scatter(grad_ckv, SEQ, scatter_dimension=0, tiled=True)
     grad_ckv = grad_ckv.reshape(2, enc_rows * shards, width)
     grad_normed_two = dot_nt(grad_cq, w_cq)
@@ -734,6 +737,12 @@
     grad_first = grad_second + norm_part
     grad_self_branch = grad_first.astype(BF16)
     grad_attended = dot_nt(grad_self_branch, w_o).astype(BF16)
+    grad_w_co = dot_tn(crossed, grad_cross_branch)
+    grad_w_cq = dot_tn(normed_two, grad_cq)
+    grad_w_o = dot_tn(attended, grad_self_branch)
+    local = jnp.stack([grad.astype(BF16) for grad in (grad_w_o, grad_w_co, grad_w_cq)])
+    local = pick_blocks(local.reshape(3, chips, 2, shard_rows, model), "core", 2)
+    grad_attended, local = meet(grad_attended, local)
     grad_heads = lax.all_to_all(
         grad_attended.reshape(rows, shards, width).transpose(1, 0, 2),
         SEQ,
@@ -742,71 +751,69 @@
         tiled=True,
     ).reshape(tokens, width)
 
-    crossed, attended, grad_down = after((crossed, attended, grad_down), grad_attended)
-    down_parts = dp_gather(grad_down)
-    grad_w_co = dot_tn(crossed, grad_cross_branch)
-    grad_w_cq = dot_tn(normed_two, grad_cq)
-    grad_w_o = dot_tn(attended, grad_self_branch)
-    local = jnp.stack([grad.astype(BF16) for grad in (grad_w_o, grad_w_co, grad_w_cq)])
-    local = swap_blocks(pick_blocks(local.reshape(3, chips, 2, shard_rows, model), "core", 2), "core")
-    grad_heads, local, down_parts = meet(grad_heads, local, down_parts)
+    scale = 1.0 / math.sqrt(tokens * groups)
+    local = swap_blocks(local, "core")
+    whole_down = join_parts(after(down_parts, grad_attended), 0)
+    local, whole_down = meet(local, whole_down)
+    local = tree_sum(local).astype(BF16).reshape(3, chips, groups, part_rows, model)
+    local = pick_blocks(local, "dp", 2)
+    sum_down, *upd_down = adam_call(whole_down, scale, ffn_out, first_ffn_out, second_ffn_out)
+    grad_heads, local, sum_down, grad_up = meet(grad_heads, local, sum_down, grad_up)
+
+    local = swap_blocks(local, "dp")
+    grad_flat = self_backward(
+        piece_starts, query, key, value, out_heads, grad_heads, self_lse, block
+    )
+    grad_flat, local = meet(grad_flat, local)
 
     def reduce_headed(inputs, grads):
         headed = dot_tn(inputs, grads).astype(BF16)
-        headed = headed.reshape(shards, groups, part_rows, grads.shape[1])
-        return swap_blocks(pick_blocks(headed, "dp", 1), "dp")
-
-    def send_headed(headed):
-        headed = tree_sum(headed).astype(BF16)
-        return send_rows(headed.reshape(chips, 2, part_rows, headed.shape[2]))
+        return headed.reshape(shards, groups, part_rows, grads.shape[1])
 
     def headed_rows(headed):
         count = headed[0].shape[2] // width
         headed = join_rows(headed).reshape(shards, part_rows, count, width)
         return headed.transpose(2, 1, 0, 3).reshape(count, part_rows, model)
 
-    local = tree_sum(local).astype(BF16).reshape(3, chips, groups, part_rows, model)
-    local = swap_blocks(pick_blocks(local, "dp", 2), "dp")
-    grad_flat = self_backward(
-        piece_starts, query, key, value, out_heads, grad_heads, self_lse, block
-    )
-    grad_flat, local = meet(grad_flat, local)
-
-    scale = 1.0 / math.sqrt(tokens * groups)
     partial = dot_nt(grad_flat, to_heads).astype(BF16)
-    grad_flat, local, down_parts = after((grad_flat, local, down_parts), partial)
     grad_normed_one = lax.psum_scatter(partial, SEQ, scatter_dimension=0, tiled=True)
+
+    grad_flat, local, grad_up, hidden_parts = after((grad_flat, local, grad_up, hidden_parts), partial)
+    up_parts = dp_gather(grad_up)
     self_part = reduce_headed(normed_all, grad_flat)
-    whole_down = join_parts(down_parts, 0)
     local = pick_blocks(tree_sum(local).astype(BF16), "chip", 1)
-    self_part, whole_down = meet(self_part, whole_down)
+    grad_ckv, local, self_part = meet(grad_ckv, local, self_part)
+    cross_part = reduce_headed(encoder_all, jnp.concatenate([grad_ckv[0], grad_ckv[1]], axis=1))
+    headed = jnp.concatenate([self_part, cross_part], axis=3).transpose(1, 0, 2, 3)
+    headed = lax.all_to_all(headed, "dp", split_axis=0, concat_axis=0, tiled=True)
     local = swap_blocks(local, "chip")
-    sum_down, *upd_down = adam_call(whole_down, scale, ffn_out, first_ffn_out, second_ffn_out)
-    local, sum_down, grad_ckv, grad_up = meet(local, sum_down, grad_ckv, grad_up)
-    cross_part = reduce_headed(encoder_all, jnp.concatenate([grad_ckv[0], grad_ckv[1]], axis=1))
-    headed = send_headed(
-        [jnp.concatenate([left, right], axis=2) for left, right in zip(self_part, cross_part)]
-    )
-    ckv_rows = lax.all_to_all(
-        grad_ckv.reshape(2, shards, enc_rows, width).transpose(1, 0, 2, 3),
-        SEQ,
-        split_axis=0,
-        concat_axis=0,
-        tiled=True,
-    )
-    up_parts = dp_gather(after(grad_up, cross_part[0]))
-    headed = headed_rows(headed)
-    local = tree_sum(local).astype(BF16)
-    up_parts, headed = meet(up_parts, headed)
-    attn_parts = dp_gather(jnp.concatenate([headed[:3], local[2:], headed[3:], local[:2]]))
+    seq = lax.axis_index("chip") * 2 + core
+    key_columns = lax.dynamic_slice_in_dim(w_ck, seq * width, width, 1)
+    value_columns = lax.dynamic_slice_in_dim(w_cv, seq * width, width, 1)
+    partial_enc = dot_nt(grad_ckv[0], key_columns) + dot_nt(grad_ckv[1], value_columns)
+    partial_enc, up_parts = meet(partial_enc.astype(BF16), up_parts)
+    grad_encoder = lax.psum_scatter(partial_enc, SEQ, scatter_dimension=0, tiled=True)
     whole_up = join_columns(up_parts, unit_cut)
     sum_up, *upd_up = adam_call(whole_up, scale, ffn_in, first_ffn_in, second_ffn_in)
-    attn_parts, sum_up, ckv_rows = meet(attn_parts, sum_up, ckv_rows)
-    whole_attn = join_parts(attn_parts, 1).reshape(8, shard_rows, model)
-    ckv_rows = ckv_rows.transpose(1, 2, 0, 3).reshape(2, enc_rows, model)
-    grad_encoder = dot_nt(ckv_rows[0], w_ck) + dot_nt(ckv_rows[1], w_cv)
-    grad_normed_one = after(grad_normed_one, whole_attn).astype(F32)
-    norm_part, grad_gain_one, grad_shift_one = norm_one_back(grad_normed_one)
+    headed, sum_up, local = meet(headed, sum_up, local)
+
+    headed = jnp.sum(headed.astype(F32), axis=0).astype(BF16)
+    own, given = pick_blocks(headed.reshape(chips, 2, part_rows, 5 * width), "core", 1)
+    given = swap(given, "core", 1)
+    local = tree_sum(local).astype(BF16)
+    given, own, local = meet(given, own, local)
+    hidden_parts = swap_blocks(after(hidden_parts, local), "dp")
+    headed = pick_blocks(jnp.stack([own, given], axis=1), "chip", 0)
+    headed = swap_blocks(headed, "chip")
+    headed, local, hidden_parts = meet(headed, local, hidden_parts)
+    local_parts = dp_gather(local)
+    out_hidden = second_sum + tree_sum(hidden_parts)
+    headed = headed_rows(headed)
+    headed, local_parts, out_hidden = meet(headed, local_parts, out_hidden)
+    headed_parts = dp_gather(headed)
+    local = join_parts(local_parts, 1).reshape(3, shard_rows, model)
+    grad_normed_one, local = meet(grad_normed_one, local)
+    norm_part, grad_gain_one, grad_shift_one = norm_one_back(grad_normed_one.astype(F32))
     grad_hidden = grad_first + norm_part
     sum_norms = jnp.stack(
         [
@@ -818,11 +825,18 @@
             grad_shift_three,
         ]
     )
-    norm_total = sum_everywhere(sum_norms * scale)
-    sum_in, *upd_in = adam_call(whole_attn[:6], scale, attn_in, first_attn_in, second_attn_in)
-    sum_out, *upd_out = adam_call(whole_attn[6:], scale, attn_out, first_attn_out, second_attn_out)
+    sum_norms = sum_along(sum_norms * scale, "core")
+    sum_norms, headed_parts = meet(sum_norms, headed_parts)
+    sum_norms = sum_along(sum_norms, "chip")
+    whole_in = join_parts(headed_parts, 1).reshape(5, shard_rows, model)
+    whole_in = jnp.concatenate([whole_in[:3], local[2:], whole_in[3:]])
+    sum_out, *upd_out = adam_call(local[:2], scale, attn_out, first_attn_out, second_attn_out)
+    sum_norms, sum_out, whole_in = meet(sum_norms, sum_out, whole_in)
+    norm_total = sum_along(sum_norms, "dp")
+    sum_in, *upd_in = adam_call(whole_in, scale, attn_in, first_attn_in, second_attn_in)
+    norm_total, sum_in, grad_encoder = meet(norm_total, sum_in, grad_encoder)
+    grad_encoder = grad_encoder.astype(F32)
     upd_norms = adam_update(norms, norm_total, first_norms, second_norms)
-    out_hidden = second_sum + tree_sum(hidden_parts)
     return (
         out_hidden,
         grad_hidden,

time: 645 us -> 576 us (0.89)
  waiting for transfers between devices: 176 us -> 150 us
  local copies, waits for them, and re-layouts: 79.9 us -> 61.5 us
  matrix products: 104 us -> 86.1 us
    ppermute x60 -> x63, waiting for transfers between devices: 153 us -> 109 us  [swap(): lax.ppermute(values, axis, [(index, index ^ offset) for index in range(co...]
    all_to_all x1, waiting for transfers between devices: 1.87 us -> 17.8 us  [on_device(): lax.all_to_all(out_heads.reshape(shards, rows, width), SEQ, split_axis=0,...]
    all_to_all x1, waiting for transfers between devices: 15.7 us -> 0.01 us  [on_device(): lax.all_to_all(grad_attended.reshape(rows, shards, width).transpose(1, 0,...]
    unnamed x192 -> x248, local copies, waits for them, and re-layouts: 33.1 us -> 21.8 us
    all_to_all x1, waiting for transfers between devices: 0.01 us -> 9.38 us  [on_device(): lax.all_to_all(to_heads, SEQ, split_axis=0, concat_axis=0, tiled=True)]
    dot_general x7, matrix products: 29.5 us -> 20.5 us  [dot_tn(): return lax.dot_general(left, right, TN, preferred_element_type=F32)]
    all_gather x1, waiting for transfers between devices: 0.02 us -> 8.07 us  [on_device(): normed_all = lax.all_gather(normed_one, SEQ, axis=0, tiled=True)]
    dot_general x8, matrix products: 36.6 us -> 29 us  [dot_nt(): return lax.dot_general(left, right, NT, preferred_element_type=F32)]
  transfers between devices with their start and end apart: 73 -> 77, of which waited for: 30 -> 31; matrix products, arithmetic and copies ran while one was open for 26% -> 27% of each run, Pallas kernels for 21% -> 23%
where the time goes in v3:
time: 576 us; the launch traced here: 567 us
  waiting for transfers between devices  150 us (26%)
  Pallas kernels  131 us (23%)
  starting transfers between devices  88 us (15%)
  matrix products  86.1 us (15%)
  local copies, waits for them, and re-layouts  61.5 us (11%)
  other arithmetic  33.9 us (6%)
  between operations  16.3 us (3%)
    ppermute x63, waiting for transfers between devices, swap(): lax.ppermute(values, axis, [(index, index ^ offset) for index in range(co...  109 us
    ppermute x63, starting transfers between devices, swap(): lax.ppermute(values, axis, [(index, index ^ offset) for index in range(co...  70.8 us
    pallas_call x4, Pallas kernels, adam_call(): pl.pallas_call(functools.partial(adam_kernel, scale), out_shape=(flat,) *...  37.9 us
    dot_general x8, matrix products, dot_f32(): return jnp.dot(left, right, preferred_element_type=F32)  36.6 us
    dot_general x8, matrix products, dot_nt(): return lax.dot_general(left, right, NT, preferred_element_type=F32)  29 us
    pallas_call x1, Pallas kernels, self_backward(): pl.pallas_call(functools.partial(self_bwd_kernel, heads, pieces, block),...  24.1 us
    unnamed x248, local copies, waits for them, and re-layouts  21.8 us
    dot_general x7, matrix products, dot_tn(): return lax.dot_general(left, right, TN, preferred_element_type=F32)  20.5 us
  transfers between devices with their start and end apart: 77, of which 31 were waited for; matrix products, arithmetic and copies ran while one was open for 27% of the time, Pallas kernels for 23%

profile of v3, /device:TPU:0, one launch (start us, length us, event | category | flops | bytes accessed | tf_op | source)
XLA Modules:
  0.0 567.0 jit_solution(15043666929356283776)
XLA Ops:
  30.9 9.4 %all-to-all-done.refs_0_ = bf16[8,32,384]{2,1,0:T(8,128)(2,1)S(1)} async-done(((bf16[8,32,384]{2,1,0:T(8,128)(2,1)}), bf16[8,32,384]{2,1,0:T(8,128)(2,1)S(1)}, u32[]{:S(2)}, u32[]{:S(2)}) %all-to-all-start) | async-done | bytes 196640 | tf_op jit(solution)/shard_map/all_to_all | solution.py:641
  53.2 6.1 %collective-permute-done.1.refs_2_ = bf16[8,32,384]{2,1,0:T(8,128)(2,1)S(1)} collective-permute-done((bf16[8,32,384]{2,1,0:T(8,128)(2,1)S(1)}, bf16[8,32,384]{2,1,0:T(8,128)(2,1)S(1)}, u32[]{:S(2)}, u32[]{:S(2)}) %collective-permute-start.1) | collective-permute-done | bytes 196640 | tf_op jit(solution)/shard_map/ppermute | solution.py:370
  60.1 8.1 %all-gather.6.cloned.1.call-done = bf16[2048,1024]{1,0:T(8,128)(2,1)} async-done(((bf16[256,1024]{1,0:T(8,128)(2,1)}), bf16[2048,1024]{1,0:T(8,128)(2,1)}) %all-gather.6.cloned.1.call-update) | async-done | bytes 4194320 | tf_op jit(solution)/shard_map/all_gather | solution.py:637
  73.4 20.0 %self_forward.1 = (bf16[2048,128]{1,0:T(8,128)(2,1)S(1)}, f32[2,8,2048]{2,1,0:T(8,128)S(1)}) custom-call(s32[1,2]{1,0:T(1,128)S(1)} %copy-done.36, bf16[2048,128]{1,0:T(8,128)(2,1)S(1)} %get-tuple-element.368.q_ref, bf16[2048,128]{1,0:T(8,128)(2,1)S(1)} %get-tuple-element.367.k_ref, bf16[2048,128]{1,0:T(8,128)(2,1)S(1)} %get-tuple-element.366.v_ref), custom_call_target="tpu_custom_call" | custom-call | flops 2147483648 | bytes 2097152 | tf_op jit(solution)/shard_map/self_forward/pallas_call | solution.py:137
  103.7 17.8 %all-to-all-done.1 = bf16[8,256,128]{1,2,0:T(8,128)(2,1)S(1)} async-done(((bf16[8,256,128]{1,2,0:T(8,128)(2,1)}), bf16[8,256,128]{1,2,0:T(8,128)(2,1)S(1)}, u32[]{:S(2)}, u32[]{:S(2)}) %all-to-all-start.1) | async-done | bytes 524320 | tf_op jit(solution)/shard_map/all_to_all | solution.py:671
  121.5 5.5 collective-permute-done.7.refs_2_
  166.8 9.5 %collective-permute-done.19.refs_2_ = bf16[2,512,256]{2,1,0:T(8,128)(2,1)} collective-permute-done((bf16[2,512,256]{2,1,0:T(8,128)(2,1)}, bf16[2,512,256]{2,1,0:T(8,128)(2,1)}, u32[]{:S(2)}, u32[]{:S(2)}) %collective-permute-start.19) | collective-permute-done | bytes 524320 | tf_op jit(solution)/shard_map/ppermute | solution.py:370
  190.9 11.0 %cross_forward.1 = (bf16[256,1024]{1,0:T(8,128)(2,1)S(1)}, f32[16,8,256]{2,1,0:T(8,128)S(1)}) custom-call(bf16[256,1024]{1,0:T(8,128)(2,1)S(1)} %fusion.16.q.q_ref, bf16[2,1024,1024]{2,1,0:T(8,128)(2,1)S(1)} %pad_maximum_fusion.1.k.v.k_ref.v_ref, bf16[2,1024,1024]{2,1,0:T(8,128)(2,1)S(1)} %pad_maximum_fusion.1.k.v.k_ref.v_ref), custom_call_target="tpu_custom_call" | custom-call | flops 1073741824 | bytes 5242880 | tf_op jit(solution)/shard_map/cross_forward/pallas_call | solution.py:282
  207.8 11.1 %collective-permute-done.24 = bf16[256,1024]{1,0:T(8,128)(2,1)S(1)} collective-permute-done((bf16[256,1024]{1,0:T(8,128)(2,1)S(1)}, bf16[256,1024]{1,0:T(8,128)(2,1)S(1)}, u32[]{:S(2)}, u32[]{:S(2)}) %collective-permute-start.24) | collective-permute-done | bytes 524320 | tf_op jit(solution)/shard_map/ppermute | solution.py:370
  218.9 11.6 %collective-permute-done.25 = bf16[256,1024]{1,0:T(8,128)(2,1)S(1)} collective-permute-done((bf16[256,1024]{1,0:T(8,128)(2,1)S(1)}, bf16[256,1024]{1,0:T(8,128)(2,1)S(1)}, u32[]{:S(2)}, u32[]{:S(2)}) %collective-permute-start.25) | collective-permute-done | bytes 524320 | tf_op jit(solution)/shard_map/ppermute | solution.py:370
  231.2 13.8 %add_convert_fusion = (bf16[1024,2048]{1,0:T(8,128)(2,1)}, bf16[1024,2048]{1,0:T(8,128)(2,1)S(1)}) fusion(bf16[1024,2048]{1,0:T(8,128)(2,1)} %all-gather.14.cloned.1.call-done, bf16[256,1024]{1,0:T(8,128)(2,1)} %collective-permute-done.26, bf16[256,1024]{1,0:T(8,128)(2,1)} %copy-done.114, bf16[256,1024]{1,0:T(8,128)(2,1)} %copy-done.112, ...), kind=kOutput, calls=%fused_computation.1 | convolution fusion | flops 4343201792 | bytes 14680064 | tf_op jit(solution)/shard_map/dot_general | solution.py:44
  247.1 6.2 %convolution_convert_fusion.2 = bf16[2048,1024]{1,0:T(8,128)(2,1)} fusion(bf16[1024,2048]{1,0:T(8,128)(2,1)S(1)} %get-tuple-element.211, bf16[1024,1024]{1,0:T(8,128)(2,1)S(1)} %copy-done.85), kind=kOutput, calls=%fused_computation.12 | convolution fusion | flops 4297064448 | bytes 10485760 | tf_op jit(solution)/shard_map/dot_general | solution.py:52
  253.4 8.7 %multiply_convert_fusion = bf16[1024,2048]{1,0:T(8,128)(2,1)S(1)} fusion(bf16[1024,2048]{1,0:T(8,128)(2,1)} %get-tuple-element.209, bf16[1024,1024]{1,0:T(8,128)(2,1)} %copy-done.84, bf16[2048,1024]{1,0:T(8,128)(2,1)} %all-gather.12.cloned.1.call-done), kind=kOutput, calls=%fused_computation | convolution fusion | flops 4301258752 | bytes 14680064 | tf_op jit(solution)/shard_map/dot_general | solution.py:48
  272.0 6.0 %fusion.69 = f32[1024,1024]{1,0:T(8,128)} fusion(bf16[1024,2048]{1,0:T(8,128)(2,1)S(1)} %copy-done.117, bf16[2048,1024]{1,0:T(8,128)(2,1)S(1)} %copy-done.111), kind=kOutput, calls=%fused_computation.179 | convolution fusion | flops 4294967296 | bytes 12582912 | tf_op jit(solution)/shard_map/dot_general | solution.py:44
  278.0 7.3 %convolution_convert_fusion.1 = bf16[1024,2048]{1,0:T(8,128)(2,1)} fusion(bf16[1024,2048]{1,0:T(8,128)(2,1)S(1)} %multiply_convert_fusion, bf16[256,1024]{1,0:T(8,128)(2,1)} %collective-permute-done.26, bf16[256,1024]{1,0:T(8,128)(2,1)S(1)} %copy-done.115, bf16[256,1024]{1,0:T(8,128)(2,1)S(1)} %copy-done.113, bf16[256,1024]{1,0:T(8,128)(2,1)S(1)} %copy-done.79), kind=kOutput, calls=%fused_computation.11 | convolution fusion | flops 4305453056 | bytes 10485760 | tf_op jit(solution)/shard_map/dot_general | solution.py:52
  285.3 7.3 %collective-permute-done.28 = bf16[256,1024]{1,0:T(8,128)(2,1)} collective-permute-done((bf16[256,1024]{1,0:T(8,128)(2,1)}, bf16[256,1024]{1,0:T(8,128)(2,1)}, u32[]{:S(2)}, u32[]{:S(2)}) %collective-permute-start.28) | collective-permute-done | bytes 524320 | tf_op jit(solution)/shard_map/ppermute | solution.py:370
  308.9 17.2 %cross_backward.1 = (bf16[256,1024]{1,0:T(8,128)(2,1)S(1)}, bf16[8,2,1024,128]{3,2,1,0:T(8,128)(2,1)}) custom-call(bf16[256,1024]{1,0:T(8,128)(2,1)S(1)} %copy-done.7, bf16[2,1024,1024]{2,1,0:T(8,128)(2,1)} %copy-done, bf16[2,1024,1024]{2,1,0:T(8,128)(2,1)} %copy-done, bf16[256,1024]{1,0:T(8,128)(2,1)S(1)} %get-tuple-element.199.o_ref, ...), custom_call_target="tpu_custom_call" | custom-call | flops 2684354560 | bytes 10485760 | tf_op jit(solution)/shard_map/cross_backward/pallas_call | solution.py:340
  347.7 12.7 %adam.4 = (f32[1024,1024]{1,0:T(8,128)}, f32[1024,1024]{1,0:T(8,128)}, f32[1024,1024]{1,0:T(8,128)}, f32[1024,1024]{1,0:T(8,128)}) custom-call(bf16[1024,1024]{1,0:T(8,128)(2,1)S(1)} %bitcast.192, f32[1024,1024]{1,0:T(8,128)} %w_ref.2, f32[1024,1024]{1,0:T(8,128)} %m1_ref.2, f32[1024,1024]{1,0:T(8,128)} %m2_ref.2), custom_call_target="tpu_custom_call" | custom-call | flops 20971520 | bytes 31457280 | tf_op jit(solution)/shard_map/adam/pallas_call | solution.py:573
  369.2 24.1 %self_backward.1 = bf16[2048,384]{1,0:T(8,128)(2,1)S(1)} custom-call(s32[1,2]{1,0:T(1,128)S(1)} %copy-done.36, bf16[2048,128]{1,0:T(8,128)(2,1)S(1)} %copy-done.27, bf16[2048,128]{1,0:T(8,128)(2,1)S(1)} %copy-done.25, bf16[2048,128]{1,0:T(8,128)(2,1)S(1)} %copy-done.23, bf16[2048,128]{1,0:T(8,128)(2,1)S(1)} %copy-done.21, bf16[2048,128]{1,0:T(8,128)(2,1)S(1)} %bitcast.206, ...), custom_call_target="tpu_custom_call" | custom-call | flops 5368709120 | bytes 4194304 | tf_op jit(solution)/shard_map/self_backward/pallas_call | solution.py:238
  393.3 8.8 %collective-permute-done.35 = bf16[3,4,32,1024]{3,2,1,0:T(8,128)(2,1)} collective-permute-done((bf16[3,4,32,1024]{3,2,1,0:T(8,128)(2,1)}, bf16[3,4,32,1024]{3,2,1,0:T(8,128)(2,1)}, u32[]{:S(2)}, u32[]{:S(2)}) %collective-permute-start.35) | collective-permute-done | bytes 786464 | tf_op jit(solution)/shard_map/ppermute | solution.py:370
  442.3 5.9 %collective-permute-start.40 = (bf16[3,32,1024]{2,1,0:T(8,128)(2,1)}, bf16[3,32,1024]{2,1,0:T(8,128)(2,1)S(1)}, u32[]{:S(2)}, u32[]{:S(2)}) collective-permute-start(bf16[3,32,1024]{2,1,0:T(8,128)(2,1)} %get-tuple-element.267), channel_id=1, source_target_pairs={{0,2},{2,0},{4,6},{6,4},{1,3},{3,1},{5,7},{7,5},{8,10},{10,8},{12,... | collective-permute-start | bytes 589832 | tf_op jit(solution)/shard_map/ppermute | solution.py:370
  451.5 13.0 %adam.5 = (f32[128,8192]{1,0:T(8,128)}, f32[128,8192]{1,0:T(8,128)}, f32[128,8192]{1,0:T(8,128)}, f32[128,8192]{1,0:T(8,128)}) custom-call(bf16[128,8192]{1,0:T(8,128)(2,1)S(1)} %place.14.g_ref, f32[128,8192]{1,0:T(8,128)} %w_ref.3, f32[128,8192]{1,0:T(8,128)} %m1_ref.3, f32[128,8192]{1,0:T(8,128)} %m2_ref.3), custom_call_target="tpu_custom_call" | custom-call | flops 20971520 | bytes 31457280 | tf_op jit(solution)/shard_map/adam/pallas_call | solution.py:573
  496.5 7.7 %collective-permute-done.49 = bf16[256,1024]{1,0:T(8,128)(2,1)S(1)} collective-permute-done((bf16[256,1024]{1,0:T(8,128)(2,1)}, bf16[256,1024]{1,0:T(8,128)(2,1)S(1)}, u32[]{:S(2)}, u32[]{:S(2)}) %collective-permute-start.49) | collective-permute-done | bytes 524320 | tf_op jit(solution)/shard_map/ppermute | solution.py:370
  547.9 9.3 %adam.7 = (f32[768,1024]{1,0:T(8,128)}, f32[768,1024]{1,0:T(8,128)}, f32[768,1024]{1,0:T(8,128)}, f32[768,1024]{1,0:T(8,128)}) custom-call(bf16[768,1024]{1,0:T(8,128)(2,1)S(1)} %bitcast.196, f32[768,1024]{1,0:T(8,128)S(1)} %bitcast.195, f32[768,1024]{1,0:T(8,128)} %bitcast.216, f32[768,1024]{1,0:T(8,128)} %bitcast.217), custom_call_target="tpu_custom_call" | custom-call | flops 15728640 | bytes 23592960 | tf_op jit(solution)/shard_map/adam/pallas_call | solution.py:573
  (519 shorter events, 292.6 us)
Async XLA Ops:
  7.2 60.9 %all-gather.6.cloned.1.call-start = ((), (), s32[]{:S(2)}) async-start(), calls=%async_computation.9 | async-start | bytes 4718592 | tf_op jit(solution)/shard_map/all_gather | solution.py:637
  14.0 46.0 %collective-permute-start.3 = (bf16[256,1024]{1,0:T(8,128)(2,1)}, bf16[256,1024]{1,0:T(8,128)(2,1)S(1)}, u32[]{:S(2)}, u32[]{:S(2)}) collective-permute-start(bf16[256,1024]{1,0:T(8,128)(2,1)} %param.22), channel_id=1, source_target_pairs={{0,8},{8,0},{16,24},{24,16},{1,9},{9,1},{17,25},{25,17},{2,10},{10... | collective-permute-start | bytes 1572872 | tf_op jit(solution)/shard_map/ppermute | solution.py:370
  17.0 43.1 %collective-permute-start.4 = (bf16[256,1024]{1,0:T(8,128)(2,1)}, bf16[256,1024]{1,0:T(8,128)(2,1)S(1)}, u32[]{:S(2)}, u32[]{:S(2)}) collective-permute-start(bf16[256,1024]{1,0:T(8,128)(2,1)} %param.22), channel_id=1, source_target_pairs={{0,16},{8,24},{16,0},{24,8},{1,17},{9,25},{17,1},{25,9},{2,18},{10... | collective-permute-start | bytes 1572872 | tf_op jit(solution)/shard_map/ppermute | solution.py:370
  18.5 41.6 %collective-permute-start.5 = (bf16[256,1024]{1,0:T(8,128)(2,1)}, bf16[256,1024]{1,0:T(8,128)(2,1)S(1)}, u32[]{:S(2)}, u32[]{:S(2)}) collective-permute-start(bf16[256,1024]{1,0:T(8,128)(2,1)} %param.22), channel_id=1, source_target_pairs={{0,24},{8,16},{16,8},{24,0},{1,25},{9,17},{17,9},{25,1},{2,26},{10... | collective-permute-start | bytes 1572872 | tf_op jit(solution)/shard_map/ppermute | solution.py:370
  26.6 71.5 %all-gather.8.cloned.1.call-start = ((), (), s32[]{:S(2)}) async-start(), calls=%async_computation.10 | async-start | bytes 1769472 | tf_op jit(solution)/shard_map/all_gather | solution.py:665
  68.2 77.6 %all-gather.10.cloned.1.call-start = ((), (), s32[]{:S(2)}) async-start(), calls=%async_computation.11 | async-start | bytes 3538944 | tf_op jit(solution)/shard_map/all_gather | solution.py:667
  72.8 158.4 %all-gather.14.cloned.1.call-start = ((), (), s32[]{:S(2)}) async-start(), calls=%async_computation.13 | async-start | bytes 4718592 | tf_op jit(solution)/shard_map/all_gather | solution.py:670
  94.5 27.0 %all-to-all-start.1 = ((bf16[8,256,128]{1,2,0:T(8,128)(2,1)}), bf16[8,256,128]{1,2,0:T(8,128)(2,1)S(1)}, u32[]{:S(2)}, u32[]{:S(2)}) async-start(bf16[8,256,128]{1,2,0:T(8,128)(2,1)} %copy.80), calls=%async_computation.1 | async-start | bytes 1048576 | tf_op jit(solution)/shard_map/all_to_all | solution.py:671
  98.0 155.3 %all-gather.12.cloned.1.call-start = ((), (), s32[]{:S(2)}) async-start(), calls=%async_computation.12 | async-start | bytes 4718592 | tf_op jit(solution)/shard_map/all_gather | solution.py:677
  101.7 25.3 %collective-permute-start.7 = (bf16[2,512,256]{2,1,0:T(8,128)(2,1)}, bf16[2,512,256]{2,1,0:T(8,128)(2,1)S(1)}, u32[]{:S(2)}, u32[]{:S(2)}) collective-permute-start(bf16[2,512,256]{2,1,0:T(8,128)(2,1)} %constant_dynamic-slice_fusion.2), channel_id=1, source_target_pairs={{0,16},{8,24},{16,0},{24,8},{1,17},{9,25},{17,1},{25,9},{2,18},{10... | collective-permute-start | bytes 1572872 | tf_op jit(solution)/shard_map/ppermute | solution.py:370
  132.3 171.3 %reduce-scatter.6.cloned.1.call-start = ((), (), s32[]{:S(2)}) async-start(), calls=%async_computation.14 | async-start | bytes 4718592 | tf_op jit(solution)/shard_map/reduce_scatter | solution.py:709
  151.8 24.5 %collective-permute-start.19 = (bf16[2,512,256]{2,1,0:T(8,128)(2,1)}, bf16[2,512,256]{2,1,0:T(8,128)(2,1)}, u32[]{:S(2)}, u32[]{:S(2)}) collective-permute-start(bf16[2,512,256]{2,1,0:T(8,128)(2,1)} %constant_dynamic-slice_fusion), channel_id=1, source_target_pairs={{0,16},{8,24},{16,0},{24,8},{1,17},{9,25},{17,1},{25,9},{2,18},{10... | collective-permute-start | bytes 1572872 | tf_op jit(solution)/shard_map/ppermute | solution.py:370
  205.5 24.9 %collective-permute-start.25 = (bf16[256,1024]{1,0:T(8,128)(2,1)S(1)}, bf16[256,1024]{1,0:T(8,128)(2,1)S(1)}, u32[]{:S(2)}, u32[]{:S(2)}) collective-permute-start(bf16[256,1024]{1,0:T(8,128)(2,1)S(1)} %add_convert_fusion.4), channel_id=1, source_target_pairs={{0,16},{8,24},{16,0},{24,8},{1,17},{9,25},{17,1},{25,9},{2,18},{10... | collective-permute-start | bytes 1572872 | tf_op jit(solution)/shard_map/ppermute | solution.py:370
  206.1 25.2 %collective-permute-start.26 = (bf16[256,1024]{1,0:T(8,128)(2,1)S(1)}, bf16[256,1024]{1,0:T(8,128)(2,1)}, u32[]{:S(2)}, u32[]{:S(2)}) collective-permute-start(bf16[256,1024]{1,0:T(8,128)(2,1)S(1)} %add_convert_fusion.4), channel_id=1, source_target_pairs={{0,24},{8,16},{16,8},{24,0},{1,25},{9,17},{17,9},{25,1},{2,26},{10... | collective-permute-start | bytes 1572872 | tf_op jit(solution)/shard_map/ppermute | solution.py:370
  253.3 112.4 %reduce-scatter.10.cloned.1.call-start = ((), (), s32[]{:S(2)}) async-start(), calls=%async_computation.16 | async-start | bytes 4718592 | tf_op jit(solution)/shard_map/reduce_scatter | solution.py:718
  292.7 131.8 %reduce-scatter.8.cloned.1.call-start = ((), (), s32[]{:S(2)}) async-start(), calls=%async_computation.15 | async-start | bytes 4718592 | tf_op jit(solution)/shard_map/reduce_scatter | solution.py:733
  346.9 175.9 %reduce-scatter.12.cloned.1.call-start = ((), (), s32[]{:S(2)}) async-start(), calls=%async_computation.17 | async-start | bytes 4718592 | tf_op jit(solution)/shard_map/reduce_scatter | solution.py:779
  365.7 27.7 %collective-permute-start.34 = (bf16[3,4,32,1024]{3,2,1,0:T(8,128)(2,1)}, bf16[3,4,32,1024]{3,2,1,0:T(8,128)(2,1)S(1)}, u32[]{:S(2)}, u32[]{:S(2)}) collective-permute-start(bf16[3,4,32,1024]{3,2,1,0:T(8,128)(2,1)} %get-tuple-element.243), channel_id=1, source_target_pairs={{0,8},{8,0},{16,24},{24,16},{1,9},{9,1},{17,25},{25,17},{2,10},{10... | collective-permute-start | bytes 2359304 | tf_op jit(solution)/shard_map/ppermute | solution.py:370
  366.5 35.6 %collective-permute-start.35 = (bf16[3,4,32,1024]{3,2,1,0:T(8,128)(2,1)}, bf16[3,4,32,1024]{3,2,1,0:T(8,128)(2,1)}, u32[]{:S(2)}, u32[]{:S(2)}) collective-permute-start(bf16[3,4,32,1024]{3,2,1,0:T(8,128)(2,1)} %get-tuple-element.244), channel_id=1, source_target_pairs={{0,16},{8,24},{16,0},{24,8},{1,17},{9,25},{17,1},{25,9},{2,18},{10... | collective-permute-start | bytes 2359304 | tf_op jit(solution)/shard_map/ppermute | solution.py:370
  368.0 35.7 %collective-permute-start.36 = (bf16[3,4,32,1024]{3,2,1,0:T(8,128)(2,1)}, bf16[3,4,32,1024]{3,2,1,0:T(8,128)(2,1)}, u32[]{:S(2)}, u32[]{:S(2)}) collective-permute-start(bf16[3,4,32,1024]{3,2,1,0:T(8,128)(2,1)} %get-tuple-element.245), channel_id=1, source_target_pairs={{0,24},{8,16},{16,8},{24,0},{1,25},{9,17},{17,9},{25,1},{2,26},{10... | collective-permute-start | bytes 2359304 | tf_op jit(solution)/shard_map/ppermute | solution.py:370
  418.0 24.2 %collective-permute-start.39 = (bf16[128,2048]{1,0:T(8,128)(2,1)S(1)}, bf16[128,2048]{1,0:T(8,128)(2,1)S(1)}, u32[]{:S(2)}, u32[]{:S(2)}) collective-permute-start(bf16[128,2048]{1,0:T(8,128)(2,1)S(1)} %copy-done.12), channel_id=1, source_target_pairs={{0,24},{8,16},{16,8},{24,0},{1,25},{9,17},{17,9},{25,1},{2,26},{10... | collective-permute-start | bytes 1572872 | tf_op jit(solution)/shard_map/ppermute | solution.py:370
  429.1 44.2 %all-to-all-start.3 = ((bf16[4,8,32,640]{3,2,1,0:T(8,128)(2,1)}), bf16[4,8,32,640]{3,2,1,0:T(8,128)(2,1)S(1)}, u32[]{:S(2)}, u32[]{:S(2)}) async-start(bf16[4,8,32,640]{3,2,1,0:T(8,128)(2,1)} %copy_bitcast_fusion), calls=%async_computation.6 | async-start | bytes 2621440 | tf_op jit(solution)/shard_map/all_to_all | solution.py:788
  432.7 124.6 %reduce-scatter.14.cloned.1.call-start = ((), (), s32[]{:S(2)}) async-start(), calls=%async_computation.18 | async-start | bytes 2359296 | tf_op jit(solution)/shard_map/reduce_scatter | solution.py:795
  479.0 25.1 %collective-permute-start.49 = (bf16[256,1024]{1,0:T(8,128)(2,1)}, bf16[256,1024]{1,0:T(8,128)(2,1)S(1)}, u32[]{:S(2)}, u32[]{:S(2)}) collective-permute-start(bf16[256,1024]{1,0:T(8,128)(2,1)} %get-tuple-element.285), channel_id=1, source_target_pairs={{0,24},{8,16},{16,8},{24,0},{1,25},{9,17},{17,9},{25,1},{2,26},{10... | collective-permute-start | bytes 1572872 | tf_op jit(solution)/shard_map/ppermute | solution.py:370
  (171 other events, 1626.6 us)
Sparse Core Ops, SparseCore 0:
  14.1 54.0 all-gather.5
  70.3 23.7 all-gather.7
  96.3 44.0 all-gather.9
  142.4 45.8 all-gather.13
  190.3 45.8 all-gather.11
  253.4 50.1 reduce-scatter.5
  306.5 49.5 reduce-scatter.9
  359.0 51.9 reduce-scatter.7
  413.2 59.9 reduce-scatter.11
  475.4 41.3 reduce-scatter.13

commit v4 on v3

--- a/solution.py
+++ b/solution.py
@@ -449,26 +449,6 @@
     return place(parts, store, full)
 
 
-def join_columns(parts, cut):
-    groups = len(parts)
-    rows, columns = parts[0].shape
-    if cut % 128:
-        joined = jnp.zeros((groups, rows, columns // cut, cut), parts[0].dtype)
-        for k, part in enumerate(parts):
-            part = part.reshape(rows, columns // cut, cut)
-            index = lax.axis_index("dp") ^ k
-            joined = lax.dynamic_update_index_in_dim(joined, part, index, 0)
-        return joined.transpose(1, 2, 0, 3).reshape(rows, columns * groups)
-
-    def store(dp_index, chip, core, refs, out):
-        for k, ref in enumerate(refs):
-            for s in range(columns // cut):
-                start = pl.multiple_of((s * groups + (dp_index ^ k)) * cut, 128)
-                out[:, pl.ds(start, cut)] = ref[:, s * cut : (s + 1) * cut]
-
-    return place(parts, store, (rows, columns * groups))
-
-
 def own_part(values, axis):
     return lax.dynamic_index_in_dim(values, lax.axis_index("dp"), axis, keepdims=False)
 
@@ -540,6 +520,68 @@
         ),
         name="take_columns",
     )(lax.axis_index("dp").astype(jnp.int32)[None], weights)
+
+
+def encoder_partial_kernel(at_ref, grad_ref, key_ref, value_ref, out_ref):
+    total = dot_nt(grad_ref[0], key_ref[...]) + dot_nt(grad_ref[1], value_ref[...])
+    out_ref[...] = total.astype(BF16)
+
+
+def encoder_partial(grad, w_keyed):
+    rows, width = grad.shape[1:]
+    model = w_keyed.shape[1]
+    seq = lax.axis_index("chip") * lax.axis_size("core") + lax.axis_index("core")
+    if width % 128:
+        own = lax.dynamic_slice_in_dim(w_keyed, seq * width, width, 2)
+        return (dot_nt(grad[0], own[0]) + dot_nt(grad[1], own[1])).astype(BF16)
+    step = min(rows, 256)
+    return pl.pallas_call(
+        encoder_partial_kernel,
+        out_shape=jax.ShapeDtypeStruct((rows, model), BF16),
+        grid_spec=pltpu.PrefetchScalarGridSpec(
+            num_scalar_prefetch=1,
+            grid=(rows // step,),
+            in_specs=[
+                pl.BlockSpec((2, step, width), lambda i, at: (0, i, 0)),
+                pl.BlockSpec((None, model, width), lambda i, at: (0, 0, at[0])),
+                pl.BlockSpec((None, model, width), lambda i, at: (1, 0, at[0])),
+            ],
+            out_specs=pl.BlockSpec((step, model), lambda i, at: (i, 0)),
+        ),
+        compiler_params=pltpu.CompilerParams(
+            dimension_semantics=("arbitrary",), vmem_limit_bytes=VMEM_LIMIT
+        ),
+        cost_estimate=pl.CostEstimate(
+            flops=4 * rows * model * width, bytes_accessed=4 * rows * model, transcendentals=0
+        ),
+        name="encoder_partial",
+    )(seq.astype(jnp.int32)[None], grad, w_keyed, w_keyed)
+
+
+def join_natural_kernel(cut, in_ref, out_ref):
+    groups = in_ref.shape[0]
+    for index in range(groups):
+        for s in range(in_ref.shape[2] // cut):
+            start = (s * groups + index) * cut
+            out_ref[:, start : start + cut] = in_ref[index, :, s * cut : (s + 1) * cut]
+
+
+def join_natural(stacked, cut):
+    groups, rows, columns = stacked.shape
+    return pl.pallas_call(
+        functools.partial(join_natural_kernel, cut),
+        out_shape=jax.ShapeDtypeStruct((rows, columns * groups), stacked.dtype),
+        compiler_params=pltpu.CompilerParams(vmem_limit_bytes=VMEM_LIMIT),
+        cost_estimate=pl.CostEstimate(
+            flops=0, bytes_accessed=4 * rows * columns * groups, transcendentals=0
+        ),
+        name="join_natural",
+    )(stacked)
+
+
+def dp_stack(values):
+    copies = jnp.broadcast_to(values[None], (lax.axis_size("dp"),) + values.shape)
+    return lax.all_to_all(copies, "dp", split_axis=0, concat_axis=0, tiled=True)
 
 
 def clip_units(grad):
@@ -658,8 +700,9 @@
     up = take_columns(ffn_in, shards, groups, unit_cut)
     down = own_part(ffn_out.reshape(groups, unit_cut, model), 0).astype(BF16)
     to_heads = join_parts(to_heads, 1).reshape(model, 3 * width)
-    normed_all, to_heads, grad_parts, keyed, outer, up, down = meet(
-        normed_all, to_heads, grad_parts, keyed, outer, up, down
+    grad_tokens = jnp.concatenate(grad_parts, axis=0)
+    normed_all, to_heads, grad_tokens, keyed, outer, up, down = meet(
+        normed_all, to_heads, grad_tokens, keyed, outer, up, down
     )
 
     outer = lax.all_gather(outer, SEQ, axis=1, tiled=True)
@@ -676,32 +719,29 @@
     attended, outer_parts = meet(attended, outer_parts)
     w_down = lax.all_gather(after(down, attended), SEQ, axis=0, tiled=True)
     outer_shared = share_columns(outer_parts)
-    cross_parts = fetch_columns(after(outer[2:], attended))
     w_o, w_cq = join_fetched([outer[:2]] + outer_parts + outer_shared)
     attended = attended.transpose(1, 0, 2).reshape(rows, model)
     first_sum = resid_in + dot_f32(attended, w_o)
-    first_sum, cross_parts, keyed = meet(first_sum, cross_parts, keyed)
+    first_sum, keyed = meet(first_sum, keyed)
 
     keyed_parts = fetch_columns(keyed[:2])
-    cross_shared = share_columns(cross_parts)
     normed_two, norm_two_back = jax.vjp(layer_norm, first_sum, gains[2], gains[3])
     normed_two = normed_two.astype(BF16)
     cross_queries = dot_f32(normed_two, w_cq).astype(BF16)
     encoder_all = keyed[2:].transpose(1, 0, 2).reshape(enc_rows * shards, model)
-    w_co = join_fetched([outer[2:]] + cross_parts + cross_shared)[0]
-    cross_queries, encoder_all, w_co, keyed_parts = meet(
-        cross_queries, encoder_all, w_co, keyed_parts
-    )
-    w_ck, w_cv = join_fetched([keyed[:2]] + keyed_parts + share_columns(keyed_parts))
-    cross_kv = jnp.stack([dot_f32(encoder_all, w_ck), dot_f32(encoder_all, w_cv)]).astype(BF16)
-
+    cross_queries, encoder_all, keyed_parts = meet(cross_queries, encoder_all, keyed_parts)
+    w_keyed = join_fetched([keyed[:2]] + keyed_parts + share_columns(keyed_parts))
+    cross_kv = jnp.stack([dot_f32(encoder_all, w_keyed[i]) for i in range(2)]).astype(BF16)
+
+    cross_parts = fetch_columns(after(outer[2:], cross_kv))
     crossed, cross_lse = cross_forward(cross_queries, cross_kv)
+    crossed, cross_parts = meet(crossed, cross_parts)
+    w_co = join_fetched([outer[2:]] + cross_parts + share_columns(cross_parts))[0]
     second_sum = first_sum + dot_f32(crossed, w_co)
 
     normed_three, norm_three_back = jax.vjp(layer_norm, second_sum, gains[4], gains[5])
     normed_three = normed_three.astype(BF16)
     ffn_tokens = jnp.concatenate(dp_gather(normed_three), axis=0)
-    grad_tokens = jnp.concatenate(grad_parts, axis=0)
     activated, slope = gelu_both(dot_f32(ffn_tokens, w_up))
     activated = activated.astype(BF16)
     grad_down = dot_tn(activated, grad_tokens).astype(BF16)
@@ -714,12 +754,8 @@
     activated, grad_pre = after((activated, grad_pre), partial)
     partial = dot_f32(activated, w_down)
     grad_up = dot_tn(ffn_tokens, grad_pre).astype(BF16)
-    grad_three, partial, grad_up = meet(grad_three, partial, grad_up)
+    grad_three, layer_out, grad_up = meet(grad_three, partial.astype(BF16), grad_up)
     grad_up = lax.psum_scatter(grad_up, SEQ, scatter_dimension=0, tiled=True)
-    hidden_parts = [partial[:rows]] + [
-        partial[k * rows : (k + 1) * rows].astype(BF16) for k in range(1, groups)
-    ]
-
     norm_part, grad_gain_three, grad_shift_three = norm_three_back(tree_sum(grad_three))
     grad_second = grad_out.astype(F32) + norm_part
     grad_cross_branch = grad_second.astype(BF16)
@@ -729,7 +765,9 @@
     grad_cq, grad_ckv = cross_backward(
         cross_queries, cross_kv, crossed, grad_crossed, cross_lse, width
     )
-    grad_cq, down_parts, grad_ckv = meet(grad_cq, down_parts, grad_ckv)
+    grad_cq, down_parts, grad_ckv, layer_out = meet(grad_cq, down_parts, grad_ckv, layer_out)
+    hidden_parts = [layer_out[k * rows : (k + 1) * rows] for k in range(groups)]
+    early_parts = swap_blocks(hidden_parts[:3], "dp")
     grad_ckv = lax.psum_scatter(grad_ckv, SEQ, scatter_dimension=0, tiled=True)
     grad_ckv = grad_ckv.reshape(2, enc_rows * shards, width)
     grad_normed_two = dot_nt(grad_cq, w_cq)
@@ -742,7 +780,7 @@
     grad_w_o = dot_tn(attended, grad_self_branch)
     local = jnp.stack([grad.astype(BF16) for grad in (grad_w_o, grad_w_co, grad_w_cq)])
     local = pick_blocks(local.reshape(3, chips, 2, shard_rows, model), "core", 2)
-    grad_attended, local = meet(grad_attended, local)
+    grad_attended, local, early_parts = meet(grad_attended, local, early_parts)
     grad_heads = lax.all_to_all(
         grad_attended.reshape(rows, shards, width).transpose(1, 0, 2),
         SEQ,
@@ -757,10 +795,11 @@
     local, whole_down = meet(local, whole_down)
     local = tree_sum(local).astype(BF16).reshape(3, chips, groups, part_rows, model)
     local = pick_blocks(local, "dp", 2)
+    local, whole_down = meet(local, whole_down)
+    local = swap_blocks(local, "dp")
     sum_down, *upd_down = adam_call(whole_down, scale, ffn_out, first_ffn_out, second_ffn_out)
-    grad_heads, local, sum_down, grad_up = meet(grad_heads, local, sum_down, grad_up)
-
-    local = swap_blocks(local, "dp")
+    grad_heads, local[1], sum_down, grad_up = meet(grad_heads, local[1], sum_down, grad_up)
+
     grad_flat = self_backward(
         piece_starts, query, key, value, out_heads, grad_heads, self_lse, block
     )
@@ -779,40 +818,38 @@
     grad_normed_one = lax.psum_scatter(partial, SEQ, scatter_dimension=0, tiled=True)
 
     grad_flat, local, grad_up, hidden_parts = after((grad_flat, local, grad_up, hidden_parts), partial)
-    up_parts = dp_gather(grad_up)
+    late_parts = [swap(hidden_parts[k], "dp", k) for k in range(3, groups)]
     self_part = reduce_headed(normed_all, grad_flat)
     local = pick_blocks(tree_sum(local).astype(BF16), "chip", 1)
-    grad_ckv, local, self_part = meet(grad_ckv, local, self_part)
+    grad_ckv, local, self_part, late_parts = meet(grad_ckv, local, self_part, late_parts)
     cross_part = reduce_headed(encoder_all, jnp.concatenate([grad_ckv[0], grad_ckv[1]], axis=1))
     headed = jnp.concatenate([self_part, cross_part], axis=3).transpose(1, 0, 2, 3)
     headed = lax.all_to_all(headed, "dp", split_axis=0, concat_axis=0, tiled=True)
     local = swap_blocks(local, "chip")
-    seq = lax.axis_index("chip") * 2 + core
-    key_columns = lax.dynamic_slice_in_dim(w_ck, seq * width, width, 1)
-    value_columns = lax.dynamic_slice_in_dim(w_cv, seq * width, width, 1)
-    partial_enc = dot_nt(grad_ckv[0], key_columns) + dot_nt(grad_ckv[1], value_columns)
-    partial_enc, up_parts = meet(partial_enc.astype(BF16), up_parts)
-    grad_encoder = lax.psum_scatter(partial_enc, SEQ, scatter_dimension=0, tiled=True)
-    whole_up = join_columns(up_parts, unit_cut)
-    sum_up, *upd_up = adam_call(whole_up, scale, ffn_in, first_ffn_in, second_ffn_in)
-    headed, sum_up, local = meet(headed, sum_up, local)
-
+    partial_enc = encoder_partial(grad_ckv, w_keyed)
+    out_hidden = second_sum + tree_sum(early_parts + late_parts)
+    headed, partial_enc, local[:3], out_hidden = meet(headed, partial_enc, local[:3], out_hidden)
+
+    whole_up = dp_stack(after(grad_up, headed))
     headed = jnp.sum(headed.astype(F32), axis=0).astype(BF16)
     own, given = pick_blocks(headed.reshape(chips, 2, part_rows, 5 * width), "core", 1)
     given = swap(given, "core", 1)
-    local = tree_sum(local).astype(BF16)
-    given, own, local = meet(given, own, local)
-    hidden_parts = swap_blocks(after(hidden_parts, local), "dp")
+    given, own = meet(given, own)
     headed = pick_blocks(jnp.stack([own, given], axis=1), "chip", 0)
     headed = swap_blocks(headed, "chip")
-    headed, local, hidden_parts = meet(headed, local, hidden_parts)
-    local_parts = dp_gather(local)
-    out_hidden = second_sum + tree_sum(hidden_parts)
+    headed, local, whole_up, partial_enc = meet(headed, local, whole_up, partial_enc)
+    grad_encoder = lax.psum_scatter(partial_enc, SEQ, scatter_dimension=0, tiled=True)
+    local = tree_sum(local).astype(BF16)
     headed = headed_rows(headed)
-    headed, local_parts, out_hidden = meet(headed, local_parts, out_hidden)
-    headed_parts = dp_gather(headed)
-    local = join_parts(local_parts, 1).reshape(3, shard_rows, model)
-    grad_normed_one, local = meet(grad_normed_one, local)
+    attn_parts = jnp.concatenate([headed[:3], local[2:], headed[3:], local[:2]])
+    attn_parts = dp_gather(attn_parts)
+    if unit_cut % 128:
+        whole_up = whole_up.reshape(groups, shard_rows, shards, unit_cut).transpose(1, 2, 0, 3)
+        whole_up = whole_up.reshape(shard_rows, hidden_units)
+    else:
+        whole_up = join_natural(whole_up, unit_cut)
+    sum_up, *upd_up = adam_call(whole_up, scale, ffn_in, first_ffn_in, second_ffn_in)
+    grad_normed_one, attn_parts, sum_up = meet(grad_normed_one, attn_parts, sum_up)
     norm_part, grad_gain_one, grad_shift_one = norm_one_back(grad_normed_one.astype(F32))
     grad_hidden = grad_first + norm_part
     sum_norms = jnp.stack(
@@ -826,15 +863,14 @@
         ]
     )
     sum_norms = sum_along(sum_norms * scale, "core")
-    sum_norms, headed_parts = meet(sum_norms, headed_parts)
+    whole_attn = join_parts(attn_parts, 1).reshape(8, shard_rows, model)
+    sum_norms, whole_attn = meet(sum_norms, whole_attn)
     sum_norms = sum_along(sum_norms, "chip")
-    whole_in = join_parts(headed_parts, 1).reshape(5, shard_rows, model)
-    whole_in = jnp.concatenate([whole_in[:3], local[2:], whole_in[3:]])
-    sum_out, *upd_out = adam_call(local[:2], scale, attn_out, first_attn_out, second_attn_out)
-    sum_norms, sum_out, whole_in = meet(sum_norms, sum_out, whole_in)
+    sum_in, *upd_in = adam_call(whole_attn[:6], scale, attn_in, first_attn_in, second_attn_in)
+    sum_norms, sum_in, grad_encoder = meet(sum_norms, sum_in, grad_encoder)
     norm_total = sum_along(sum_norms, "dp")
-    sum_in, *upd_in = adam_call(whole_in, scale, attn_in, first_attn_in, second_attn_in)
-    norm_total, sum_in, grad_encoder = meet(norm_total, sum_in, grad_encoder)
+    sum_out, *upd_out = adam_call(whole_attn[6:], scale, attn_out, first_attn_out, second_attn_out)
+    norm_total, sum_out = meet(norm_total, sum_out)
     grad_encoder = grad_encoder.astype(F32)
     upd_norms = adam_update(norms, norm_total, first_norms, second_norms)
     return (

time: 576 us -> 564 us (0.979)
    ppermute x63 -> x57, waiting for transfers between devices: 109 us -> 99 us  [swap(): lax.ppermute(values, axis, [(index, index ^ offset) for index in range(co...]
    ppermute x63 -> x57, starting transfers between devices: 70.8 us -> 62.5 us  [swap(): lax.ppermute(values, axis, [(index, index ^ offset) for index in range(co...]
    all_gather x1, waiting for transfers between devices: 8.07 us -> 14.9 us  [on_device(): normed_all = lax.all_gather(normed_one, SEQ, axis=0, tiled=True)]
    pallas_call x9 -> x7, Pallas kernels: 15.7 us -> 10.1 us  [place(): pl.pallas_call(functools.partial(place_kernel, store), out_shape=jax.Shap...]
    dot_general x8 -> x6, matrix products: 29 us -> 24.5 us  [dot_nt(): return lax.dot_general(left, right, NT, preferred_element_type=F32)]
    unnamed x248 -> x171, local copies, waits for them, and re-layouts: 21.8 us -> 17.7 us
  transfers between devices with their start and end apart: 77 -> 72, of which waited for: 31 -> 31; matrix products, arithmetic and copies ran while one was open for 27% -> 29% of each run, Pallas kernels for 23% -> 23%
where the time goes in v4:
time: 564 us; the launch traced here: 555 us
  waiting for transfers between devices  145 us (26%)
  Pallas kernels  128 us (23%)
  matrix products  85.3 us (15%)
  starting transfers between devices  83.6 us (15%)
  local copies, waits for them, and re-layouts  57.4 us (10%)
  other arithmetic  39 us (7%)
  between operations  16.2 us (3%)
    ppermute x57, waiting for transfers between devices, swap(): lax.ppermute(values, axis, [(index, index ^ offset) for index in range(co...  99 us
    ppermute x57, starting transfers between devices, swap(): lax.ppermute(values, axis, [(index, index ^ offset) for index in range(co...  62.5 us
    dot_general x8, matrix products, dot_f32(): return jnp.dot(left, right, preferred_element_type=F32)  38.5 us
    pallas_call x4, Pallas kernels, adam_call(): pl.pallas_call(functools.partial(adam_kernel, scale), out_shape=(flat,) *...  37.8 us
    dot_general x6, matrix products, dot_nt(): return lax.dot_general(left, right, NT, preferred_element_type=F32)  24.5 us
    pallas_call x1, Pallas kernels, self_backward(): pl.pallas_call(functools.partial(self_bwd_kernel, heads, pieces, block),...  23.8 us
    dot_general x7, matrix products, dot_tn(): return lax.dot_general(left, right, TN, preferred_element_type=F32)  22.3 us
    pallas_call x1, Pallas kernels, self_forward(): pl.pallas_call(functools.partial(self_fwd_kernel, heads, pieces, block),...  20.1 us
  transfers between devices with their start and end apart: 72, of which 31 were waited for; matrix products, arithmetic and copies ran while one was open for 29% of the time, Pallas kernels for 23%

profile of v4, /device:TPU:0, one launch (start us, length us, event | category | flops | bytes accessed | tf_op | source)
XLA Modules:
  0.0 554.9 jit_solution(12126978478034588431)
XLA Ops:
  32.4 6.8 %all-to-all-done.refs_0_ = bf16[8,32,384]{2,1,0:T(8,128)(2,1)S(1)} async-done(((bf16[8,32,384]{2,1,0:T(8,128)(2,1)}), bf16[8,32,384]{2,1,0:T(8,128)(2,1)S(1)}, u32[]{:S(2)}, u32[]{:S(2)}) %all-to-all-start) | async-done | bytes 196640 | tf_op jit(solution)/shard_map/all_to_all | solution.py:683
  52.1 14.9 %all-gather.6.cloned.1.call-done = bf16[2048,1024]{1,0:T(8,128)(2,1)} async-done(((bf16[256,1024]{1,0:T(8,128)(2,1)}), bf16[2048,1024]{1,0:T(8,128)(2,1)}) %all-gather.6.cloned.1.call-update) | async-done | bytes 4194320 | tf_op jit(solution)/shard_map/all_gather | solution.py:679
  67.1 5.7 %convolution_convert_fusion.3 = bf16[2048,384]{1,0:T(8,128)(2,1)} fusion(bf16[2048,1024]{1,0:T(8,128)(2,1)} %all-gather.6.cloned.1.call-done, bf16[1024,384]{1,0:T(8,128)(2,1)S(1)} %bitcast.204), kind=kOutput, calls=%fused_computation.14 | convolution fusion | flops 1611399168 | bytes 6553600 | tf_op jit(solution)/shard_map/dot_general | solution.py:44
  74.3 20.1 %self_forward.1 = (bf16[2048,128]{1,0:T(8,128)(2,1)S(1)}, f32[2,8,2048]{2,1,0:T(8,128)S(1)}) custom-call(s32[1,2]{1,0:T(1,128)S(1)} %copy-done.29, bf16[2048,128]{1,0:T(8,128)(2,1)S(1)} %get-tuple-element.341.q_ref, bf16[2048,128]{1,0:T(8,128)(2,1)S(1)} %get-tuple-element.340.k_ref, bf16[2048,128]{1,0:T(8,128)(2,1)S(1)} %get-tuple-element.339.v_ref), custom_call_target="tpu_custom_call" | custom-call | flops 2147483648 | bytes 2097152 | tf_op jit(solution)/shard_map/self_forward/pallas_call | solution.py:137
  104.7 19.8 %all-to-all-done.1 = bf16[8,256,128]{1,2,0:T(8,128)(2,1)S(1)} async-done(((bf16[8,256,128]{1,2,0:T(8,128)(2,1)}), bf16[8,256,128]{1,2,0:T(8,128)(2,1)S(1)}, u32[]{:S(2)}, u32[]{:S(2)}) %all-to-all-start.1) | async-done | bytes 524320 | tf_op jit(solution)/shard_map/all_to_all | solution.py:714
  161.4 11.7 %collective-permute-done.13.refs_2_ = bf16[2,512,256]{2,1,0:T(8,128)(2,1)S(1)} collective-permute-done((bf16[2,512,256]{2,1,0:T(8,128)(2,1)}, bf16[2,512,256]{2,1,0:T(8,128)(2,1)S(1)}, u32[]{:S(2)}, u32[]{:S(2)}) %collective-permute-start.13) | collective-permute-done | bytes 524320 | tf_op jit(solution)/shard_map/ppermute | solution.py:370
  190.3 11.0 %cross_forward.1 = (bf16[256,1024]{1,0:T(8,128)(2,1)S(1)}, f32[16,8,256]{2,1,0:T(8,128)S(1)}) custom-call(bf16[256,1024]{1,0:T(8,128)(2,1)S(1)} %fusion.17.q.q_ref, bf16[2,1024,1024]{2,1,0:T(8,128)(2,1)S(1)} %pad_maximum_fusion.1.k.v.k_ref.v_ref, bf16[2,1024,1024]{2,1,0:T(8,128)(2,1)S(1)} %pad_maximum_fusion.1.k.v.k_ref.v_ref), custom_call_target="tpu_custom_call" | custom-call | flops 1073741824 | bytes 5242880 | tf_op jit(solution)/shard_map/cross_forward/pallas_call | solution.py:282
  211.1 11.6 %collective-permute-done.24 = bf16[256,1024]{1,0:T(8,128)(2,1)} collective-permute-done((bf16[256,1024]{1,0:T(8,128)(2,1)}, bf16[256,1024]{1,0:T(8,128)(2,1)}, u32[]{:S(2)}, u32[]{:S(2)}) %collective-permute-start.24) | collective-permute-done | bytes 524320 | tf_op jit(solution)/shard_map/ppermute | solution.py:370
  222.7 10.1 %collective-permute-done.25 = bf16[256,1024]{1,0:T(8,128)(2,1)} collective-permute-done((bf16[256,1024]{1,0:T(8,128)(2,1)}, bf16[256,1024]{1,0:T(8,128)(2,1)}, u32[]{:S(2)}, u32[]{:S(2)}) %collective-permute-start.25) | collective-permute-done | bytes 524320 | tf_op jit(solution)/shard_map/ppermute | solution.py:370
  233.9 13.6 %add_convert_fusion = (bf16[1024,2048]{1,0:T(8,128)(2,1)}, bf16[1024,2048]{1,0:T(8,128)(2,1)S(1)}) fusion(bf16[1024,2048]{1,0:T(8,128)(2,1)} %all-gather.14.cloned.1.call-done, bf16[256,1024]{1,0:T(8,128)(2,1)} %collective-permute-done.26, bf16[256,1024]{1,0:T(8,128)(2,1)} %collective-permute-done.25, bf16[256,1024]{1,0:T(8,128)(2,1)} %collective-permute-done.24, ...), kind=kOutput, calls=%fused_computation.1 | convolution fusion | flops 4343201792 | bytes 14680064 | tf_op jit(solution)/shard_map/dot_general | solution.py:44
  249.5 6.2 %convolution_convert_fusion.2 = bf16[2048,1024]{1,0:T(8,128)(2,1)} fusion(bf16[1024,2048]{1,0:T(8,128)(2,1)S(1)} %get-tuple-element.195, bf16[1024,1024]{1,0:T(8,128)(2,1)S(1)} %copy-done.53), kind=kOutput, calls=%fused_computation.11 | convolution fusion | flops 4297064448 | bytes 10485760 | tf_op jit(solution)/shard_map/dot_general | solution.py:52
  255.8 9.0 %multiply_convert_fusion = bf16[1024,2048]{1,0:T(8,128)(2,1)S(1)} fusion(bf16[1024,2048]{1,0:T(8,128)(2,1)} %get-tuple-element.193, bf16[1024,1024]{1,0:T(8,128)(2,1)} %pad_maximum_fusion.2, bf16[2048,1024]{1,0:T(8,128)(2,1)} %all-gather.12.cloned.1.call-done), kind=kOutput, calls=%fused_computation | convolution fusion | flops 4301258752 | bytes 14680064 | tf_op jit(solution)/shard_map/dot_general | solution.py:48
  280.5 7.7 %convolution_convert_fusion.1 = bf16[1024,2048]{1,0:T(8,128)(2,1)} fusion(bf16[1024,2048]{1,0:T(8,128)(2,1)S(1)} %multiply_convert_fusion, bf16[256,1024]{1,0:T(8,128)(2,1)} %collective-permute-done.26, bf16[256,1024]{1,0:T(8,128)(2,1)} %collective-permute-done.25, bf16[256,1024]{1,0:T(8,128)(2,1)} %collective-permute-done.24, ...), kind=kOutput, calls=%fused_computation.10 | convolution fusion | flops 4305453056 | bytes 10485760 | tf_op jit(solution)/shard_map/dot_general | solution.py:52
  288.2 8.4 %collective-permute-done.28 = bf16[256,1024]{1,0:T(8,128)(2,1)} collective-permute-done((bf16[256,1024]{1,0:T(8,128)(2,1)}, bf16[256,1024]{1,0:T(8,128)(2,1)}, u32[]{:S(2)}, u32[]{:S(2)}) %collective-permute-start.28) | collective-permute-done | bytes 524320 | tf_op jit(solution)/shard_map/ppermute | solution.py:370
  309.1 17.3 %cross_backward.1 = (bf16[256,1024]{1,0:T(8,128)(2,1)S(1)}, bf16[8,2,1024,128]{3,2,1,0:T(8,128)(2,1)}) custom-call(bf16[256,1024]{1,0:T(8,128)(2,1)S(1)} %fusion.17.q.q_ref, bf16[2,1024,1024]{2,1,0:T(8,128)(2,1)} %copy-done, bf16[2,1024,1024]{2,1,0:T(8,128)(2,1)} %copy-done, bf16[256,1024]{1,0:T(8,128)(2,1)S(1)} %get-tuple-element.184.o_ref, ...), custom_call_target="tpu_custom_call" | custom-call | flops 2684354560 | bytes 10485760 | tf_op jit(solution)/shard_map/cross_backward/pallas_call | solution.py:340
  363.3 12.7 %adam.4 = (f32[1024,1024]{1,0:T(8,128)}, f32[1024,1024]{1,0:T(8,128)}, f32[1024,1024]{1,0:T(8,128)}, f32[1024,1024]{1,0:T(8,128)}) custom-call(bf16[1024,1024]{1,0:T(8,128)(2,1)S(1)} %bitcast.193, f32[1024,1024]{1,0:T(8,128)} %w_ref.2, f32[1024,1024]{1,0:T(8,128)} %m1_ref.2, f32[1024,1024]{1,0:T(8,128)} %m2_ref.2), custom_call_target="tpu_custom_call" | custom-call | flops 20971520 | bytes 31457280 | tf_op jit(solution)/shard_map/adam/pallas_call | solution.py:615
  380.5 23.8 %self_backward.1 = bf16[2048,384]{1,0:T(8,128)(2,1)S(1)} custom-call(s32[1,2]{1,0:T(1,128)S(1)} %copy-done.29, bf16[2048,128]{1,0:T(8,128)(2,1)S(1)} %copy-done.28, bf16[2048,128]{1,0:T(8,128)(2,1)S(1)} %copy-done.26, bf16[2048,128]{1,0:T(8,128)(2,1)S(1)} %copy-done.24, bf16[2048,128]{1,0:T(8,128)(2,1)S(1)} %copy-done.22, bf16[2048,128]{1,0:T(8,128)(2,1)S(1)} %bitcast.207, ...), custom_call_target="tpu_custom_call" | custom-call | flops 5368709120 | bytes 4194304 | tf_op jit(solution)/shard_map/self_backward/pallas_call | solution.py:238
  417.0 7.0 %collective-permute-done.39 = bf16[256,1024]{1,0:T(8,128)(2,1)} collective-permute-done((bf16[256,1024]{1,0:T(8,128)(2,1)}, bf16[256,1024]{1,0:T(8,128)(2,1)}, u32[]{:S(2)}, u32[]{:S(2)}) %collective-permute-start.39) | collective-permute-done | bytes 524320 | tf_op jit(solution)/shard_map/ppermute | solution.py:370
  443.4 6.0 %collective-permute-done.40 = bf16[3,32,1024]{2,1,0:T(8,128)(2,1)} collective-permute-done((bf16[3,32,1024]{2,1,0:T(8,128)(2,1)}, bf16[3,32,1024]{2,1,0:T(8,128)(2,1)}, u32[]{:S(2)}, u32[]{:S(2)}) %collective-permute-start.40) | collective-permute-done | bytes 196640 | tf_op jit(solution)/shard_map/ppermute | solution.py:370
  466.3 6.1 %collective-permute-done.46 = bf16[3,32,1024]{2,1,0:T(8,128)(2,1)S(1)} collective-permute-done((bf16[3,32,1024]{2,1,0:T(8,128)(2,1)}, bf16[3,32,1024]{2,1,0:T(8,128)(2,1)S(1)}, u32[]{:S(2)}, u32[]{:S(2)}) %collective-permute-start.46) | collective-permute-done | bytes 196640 | tf_op jit(solution)/shard_map/ppermute | solution.py:370
  472.7 8.7 %collective-permute-done.44.refs_2_ = bf16[2,32,640]{2,1,0:T(8,128)(2,1)S(1)} collective-permute-done((bf16[2,32,640]{2,1,0:T(8,128)(2,1)S(1)}, bf16[2,32,640]{2,1,0:T(8,128)(2,1)S(1)}, u32[]{:S(2)}, u32[]{:S(2)}) %collective-permute-start.44) | collective-permute-done | bytes 81952 | tf_op jit(solution)/shard_map/ppermute | solution.py:370
  489.9 12.8 %adam.5 = (f32[128,8192]{1,0:T(8,128)}, f32[128,8192]{1,0:T(8,128)}, f32[128,8192]{1,0:T(8,128)}, f32[128,8192]{1,0:T(8,128)}) custom-call(bf16[128,8192]{1,0:T(8,128)(2,1)S(1)} %join_natural.1.g_ref, f32[128,8192]{1,0:T(8,128)} %w_ref.3, f32[128,8192]{1,0:T(8,128)} %m1_ref.3, f32[128,8192]{1,0:T(8,128)} %m2_ref.3), custom_call_target="tpu_custom_call" | custom-call | flops 20971520 | bytes 31457280 | tf_op jit(solution)/shard_map/adam/pallas_call | solution.py:615
  502.7 9.7 %collective-permute-done.48.refs_2_ = bf16[8,32,1024]{2,1,0:T(8,128)(2,1)S(1)} collective-permute-done((bf16[8,32,1024]{2,1,0:T(8,128)(2,1)S(1)}, bf16[8,32,1024]{2,1,0:T(8,128)(2,1)S(1)}, u32[]{:S(2)}, u32[]{:S(2)}) %collective-permute-start.48) | collective-permute-done | bytes 524320 | tf_op jit(solution)/shard_map/ppermute | solution.py:370
  526.9 9.3 %adam.6 = (f32[768,1024]{1,0:T(8,128)}, f32[768,1024]{1,0:T(8,128)}, f32[768,1024]{1,0:T(8,128)}, f32[768,1024]{1,0:T(8,128)}) custom-call(bf16[768,1024]{1,0:T(8,128)(2,1)S(1)} %bitcast.197, f32[768,1024]{1,0:T(8,128)S(1)} %bitcast.196, f32[768,1024]{1,0:T(8,128)} %bitcast.216, f32[768,1024]{1,0:T(8,128)} %bitcast.217), custom_call_target="tpu_custom_call" | custom-call | flops 15728640 | bytes 23592960 | tf_op jit(solution)/shard_map/adam/pallas_call | solution.py:615
  (432 shorter events, 268.9 us)
Async XLA Ops:
  7.2 59.8 %all-gather.6.cloned.1.call-start = ((), (), s32[]{:S(2)}) async-start(), calls=%async_computation.10 | async-start | bytes 4718592 | tf_op jit(solution)/shard_map/all_gather | solution.py:679
  12.8 29.4 %collective-permute-start.3 = (bf16[256,1024]{1,0:T(8,128)(2,1)}, bf16[256,1024]{1,0:T(8,128)(2,1)S(1)}, u32[]{:S(2)}, u32[]{:S(2)}) collective-permute-start(bf16[256,1024]{1,0:T(8,128)(2,1)} %param.22), channel_id=1, source_target_pairs={{0,8},{8,0},{16,24},{24,16},{1,9},{9,1},{17,25},{25,17},{2,10},{10... | collective-permute-start | bytes 1572872 | tf_op jit(solution)/shard_map/ppermute | solution.py:370
  15.8 32.8 %collective-permute-start.4 = (bf16[256,1024]{1,0:T(8,128)(2,1)}, bf16[256,1024]{1,0:T(8,128)(2,1)}, u32[]{:S(2)}, u32[]{:S(2)}) collective-permute-start(bf16[256,1024]{1,0:T(8,128)(2,1)} %param.22), channel_id=1, source_target_pairs={{0,16},{8,24},{16,0},{24,8},{1,17},{9,25},{17,1},{25,9},{2,18},{10... | collective-permute-start | bytes 1572872 | tf_op jit(solution)/shard_map/ppermute | solution.py:370
  17.4 31.3 %collective-permute-start.5 = (bf16[256,1024]{1,0:T(8,128)(2,1)}, bf16[256,1024]{1,0:T(8,128)(2,1)}, u32[]{:S(2)}, u32[]{:S(2)}) collective-permute-start(bf16[256,1024]{1,0:T(8,128)(2,1)} %param.22), channel_id=1, source_target_pairs={{0,24},{8,16},{16,8},{24,0},{1,25},{9,17},{17,9},{25,1},{2,26},{10... | collective-permute-start | bytes 1572872 | tf_op jit(solution)/shard_map/ppermute | solution.py:370
  25.5 73.6 %all-gather.8.cloned.1.call-start = ((), (), s32[]{:S(2)}) async-start(), calls=%async_computation.11 | async-start | bytes 1769472 | tf_op jit(solution)/shard_map/all_gather | solution.py:708
  67.0 74.2 %all-gather.10.cloned.1.call-start = ((), (), s32[]{:S(2)}) async-start(), calls=%async_computation.12 | async-start | bytes 3538944 | tf_op jit(solution)/shard_map/all_gather | solution.py:710
  72.8 138.3 %all-gather.14.cloned.1.call-start = ((), (), s32[]{:S(2)}) async-start(), calls=%async_computation.14 | async-start | bytes 4718592 | tf_op jit(solution)/shard_map/all_gather | solution.py:713
  95.5 29.0 %all-to-all-start.1 = ((bf16[8,256,128]{1,2,0:T(8,128)(2,1)}), bf16[8,256,128]{1,2,0:T(8,128)(2,1)S(1)}, u32[]{:S(2)}, u32[]{:S(2)}) async-start(bf16[8,256,128]{1,2,0:T(8,128)(2,1)} %copy.82), calls=%async_computation.1 | async-start | bytes 1048576 | tf_op jit(solution)/shard_map/all_to_all | solution.py:714
  99.0 156.8 %all-gather.12.cloned.1.call-start = ((), (), s32[]{:S(2)}) async-start(), calls=%async_computation.13 | async-start | bytes 4718592 | tf_op jit(solution)/shard_map/all_gather | solution.py:720
  102.7 25.3 %collective-permute-start.7 = (bf16[2,512,256]{2,1,0:T(8,128)(2,1)}, bf16[2,512,256]{2,1,0:T(8,128)(2,1)S(1)}, u32[]{:S(2)}, u32[]{:S(2)}) collective-permute-start(bf16[2,512,256]{2,1,0:T(8,128)(2,1)} %constant_dynamic-slice_fusion.2), channel_id=1, source_target_pairs={{0,16},{8,24},{16,0},{24,8},{1,17},{9,25},{17,1},{25,9},{2,18},{10... | collective-permute-start | bytes 1572872 | tf_op jit(solution)/shard_map/ppermute | solution.py:370
  128.7 175.1 %reduce-scatter.6.cloned.1.call-start = ((), (), s32[]{:S(2)}) async-start(), calls=%async_computation.15 | async-start | bytes 4718592 | tf_op jit(solution)/shard_map/reduce_scatter | solution.py:749
  147.9 25.2 %collective-permute-start.13 = (bf16[2,512,256]{2,1,0:T(8,128)(2,1)}, bf16[2,512,256]{2,1,0:T(8,128)(2,1)S(1)}, u32[]{:S(2)}, u32[]{:S(2)}) collective-permute-start(bf16[2,512,256]{2,1,0:T(8,128)(2,1)} %constant_dynamic-slice_fusion.1), channel_id=1, source_target_pairs={{0,16},{8,24},{16,0},{24,8},{1,17},{9,25},{17,1},{25,9},{2,18},{10... | collective-permute-start | bytes 1572872 | tf_op jit(solution)/shard_map/ppermute | solution.py:370
  255.7 120.2 %reduce-scatter.10.cloned.1.call-start = ((), (), s32[]{:S(2)}) async-start(), calls=%async_computation.17 | async-start | bytes 4718592 | tf_op jit(solution)/shard_map/reduce_scatter | solution.py:758
  272.2 24.4 %collective-permute-start.28 = (bf16[256,1024]{1,0:T(8,128)(2,1)}, bf16[256,1024]{1,0:T(8,128)(2,1)}, u32[]{:S(2)}, u32[]{:S(2)}) collective-permute-start(bf16[256,1024]{1,0:T(8,128)(2,1)} %get-tuple-element.336), channel_id=1, source_target_pairs={{0,16},{8,24},{16,0},{24,8},{1,17},{9,25},{17,1},{25,9},{2,18},{10... | collective-permute-start | bytes 1572872 | tf_op jit(solution)/shard_map/ppermute | solution.py:370
  296.7 127.3 %reduce-scatter.8.cloned.1.call-start = ((), (), s32[]{:S(2)}) async-start(), calls=%async_computation.16 | async-start | bytes 4718592 | tf_op jit(solution)/shard_map/reduce_scatter | solution.py:771
  303.8 24.6 %collective-permute-start.30 = (bf16[256,1024]{1,0:T(8,128)(2,1)}, bf16[256,1024]{1,0:T(8,128)(2,1)S(1)}, u32[]{:S(2)}, u32[]{:S(2)}) collective-permute-start(bf16[256,1024]{1,0:T(8,128)(2,1)} %reduce-scatter.6.cloned.1.call-done.refs_0_), channel_id=1, source_target_pairs={{0,8},{8,0},{16,24},{24,16},{1,9},{9,1},{17,25},{25,17},{2,10},{10... | collective-permute-start | bytes 1572872 | tf_op jit(solution)/shard_map/ppermute | solution.py:370
  349.2 26.8 %all-to-all-start.2 = ((bf16[8,256,128]{2,1,0:T(8,128)(2,1)}), bf16[8,256,128]{2,1,0:T(8,128)(2,1)S(1)}, u32[]{:S(2)}, u32[]{:S(2)}) async-start(bf16[8,256,128]{2,1,0:T(8,128)(2,1)} %bitcast_bitcast_fusion), calls=%async_computation.4 | async-start | bytes 1048576 | tf_op jit(solution)/shard_map/all_to_all | solution.py:784
  352.7 161.2 %reduce-scatter.12.cloned.1.call-start = ((), (), s32[]{:S(2)}) async-start(), calls=%async_computation.18 | async-start | bytes 4718592 | tf_op jit(solution)/shard_map/reduce_scatter | solution.py:818
  360.6 43.6 %collective-permute-start.37 = (bf16[3,4,32,1024]{3,2,1,0:T(8,128)(2,1)}, bf16[3,4,32,1024]{3,2,1,0:T(8,128)(2,1)}, u32[]{:S(2)}, u32[]{:S(2)}) collective-permute-start(bf16[3,4,32,1024]{3,2,1,0:T(8,128)(2,1)} %get-tuple-element.232), channel_id=1, source_target_pairs={{0,16},{8,24},{16,0},{24,8},{1,17},{9,25},{17,1},{25,9},{2,18},{10... | collective-permute-start | bytes 2359304 | tf_op jit(solution)/shard_map/ppermute | solution.py:370
  362.0 42.3 %collective-permute-start.38 = (bf16[3,4,32,1024]{3,2,1,0:T(8,128)(2,1)}, bf16[3,4,32,1024]{3,2,1,0:T(8,128)(2,1)}, u32[]{:S(2)}, u32[]{:S(2)}) collective-permute-start(bf16[3,4,32,1024]{3,2,1,0:T(8,128)(2,1)} %get-tuple-element.233), channel_id=1, source_target_pairs={{0,24},{8,16},{16,8},{24,0},{1,25},{9,17},{17,9},{25,1},{2,26},{10... | collective-permute-start | bytes 2359304 | tf_op jit(solution)/shard_map/ppermute | solution.py:370
  452.0 29.4 %all-to-all-start.4 = ((bf16[4,128,2048]{2,1,0:T(8,128)(2,1)}), bf16[4,128,2048]{2,1,0:T(8,128)(2,1)S(1)}, u32[]{:S(2)}, u32[]{:S(2)}) async-start(bf16[4,128,2048]{2,1,0:T(8,128)(2,1)} %broadcast_in_dim.40), calls=%async_computation.8 | async-start | bytes 4194304 | tf_op jit(solution)/shard_map/all_to_all | solution.py:584
  456.3 80.0 %reduce-scatter.14.cloned.1.call-start = ((), (), s32[]{:S(2)}) async-start(), calls=%async_computation.19 | async-start | bytes 2359296 | tf_op jit(solution)/shard_map/reduce_scatter | solution.py:841
  487.5 24.9 %collective-permute-start.48 = (bf16[8,32,1024]{2,1,0:T(8,128)(2,1)S(1)}, bf16[8,32,1024]{2,1,0:T(8,128)(2,1)S(1)}, u32[]{:S(2)}, u32[]{:S(2)}) collective-permute-start(bf16[8,32,1024]{2,1,0:T(8,128)(2,1)S(1)} %pad_maximum_fusion.6.refs_0_), channel_id=1, source_target_pairs={{0,16},{8,24},{16,0},{24,8},{1,17},{9,25},{17,1},{25,9},{2,18},{10... | collective-permute-start | bytes 1572872 | tf_op jit(solution)/shard_map/ppermute | solution.py:370
  489.0 24.2 %collective-permute-start.49 = (bf16[8,32,1024]{2,1,0:T(8,128)(2,1)S(1)}, bf16[8,32,1024]{2,1,0:T(8,128)(2,1)S(1)}, u32[]{:S(2)}, u32[]{:S(2)}) collective-permute-start(bf16[8,32,1024]{2,1,0:T(8,128)(2,1)S(1)} %pad_maximum_fusion.6.refs_0_), channel_id=1, source_target_pairs={{0,24},{8,16},{16,8},{24,0},{1,25},{9,17},{17,9},{25,1},{2,26},{10... | collective-permute-start | bytes 1572872 | tf_op jit(solution)/shard_map/ppermute | solution.py:370
  (129 other events, 1432.0 us)
Sparse Core Ops, SparseCore 0:
  12.9 54.0 all-gather.5
  69.2 23.7 all-gather.7
  95.2 46.0 all-gather.9
  143.3 45.9 all-gather.13
  191.3 45.8 all-gather.11
  255.9 47.8 reduce-scatter.5
  306.6 48.1 reduce-scatter.9
  357.7 47.0 reduce-scatter.7
  409.9 63.1 reduce-scatter.11
  481.5 35.5 reduce-scatter.13

commit v5 on v4

--- a/solution.py
+++ b/solution.py
@@ -609,7 +609,7 @@
     shape = weight.shape
     columns = shape[-1]
     rows = math.prod(shape[:-1])
-    step = min(rows, 262144 // columns)
+    step = min(rows, 131072 // columns)
     spec = pl.BlockSpec((step, columns), lambda i: (i, 0))
     flat = jax.ShapeDtypeStruct((rows, columns), F32)
     outs = pl.pallas_call(

time: 564 us -> 564 us (level)
  transfers between devices with their start and end apart: 72 -> 72, of which waited for: 31 -> 31; matrix products, arithmetic and copies ran while one was open for 29% -> 29% of each run, Pallas kernels for 23% -> 24%
where the time goes in v5:
time: 564 us; the launch traced here: 555 us
  waiting for transfers between devices  143 us (25%)
  Pallas kernels  131 us (23%)
  matrix products  85.3 us (15%)
  starting transfers between devices  83.5 us (15%)
  local copies, waits for them, and re-layouts  57.4 us (10%)
  other arithmetic  39 us (7%)
  between operations  16.2 us (3%)
    ppermute x57, waiting for transfers between devices, swap(): lax.ppermute(values, axis, [(index, index ^ offset) for index in range(co...  96.7 us
    ppermute x57, starting transfers between devices, swap(): lax.ppermute(values, axis, [(index, index ^ offset) for index in range(co...  62.5 us
    pallas_call x4, Pallas kernels, adam_call(): pl.pallas_call(functools.partial(adam_kernel, scale), out_shape=(flat,) *...  40.2 us
    dot_general x8, matrix products, dot_f32(): return jnp.dot(left, right, preferred_element_type=F32)  38.5 us
    dot_general x6, matrix products, dot_nt(): return lax.dot_general(left, right, NT, preferred_element_type=F32)  24.5 us
    pallas_call x1, Pallas kernels, self_backward(): pl.pallas_call(functools.partial(self_bwd_kernel, heads, pieces, block),...  23.8 us
    dot_general x7, matrix products, dot_tn(): return lax.dot_general(left, right, TN, preferred_element_type=F32)  22.3 us
    pallas_call x1, Pallas kernels, self_forward(): pl.pallas_call(functools.partial(self_fwd_kernel, heads, pieces, block),...  20.1 us
  transfers between devices with their start and end apart: 72, of which 31 were waited for; matrix products, arithmetic and copies ran while one was open for 29% of the time, Pallas kernels for 24%

profile of v5, /device:TPU:0, one launch (start us, length us, event | category | flops | bytes accessed | tf_op | source)
XLA Modules:
  0.0 554.9 jit_solution(13286209631549627291)
XLA Ops:
  32.4 6.8 %all-to-all-done.refs_0_ = bf16[8,32,384]{2,1,0:T(8,128)(2,1)S(1)} async-done(((bf16[8,32,384]{2,1,0:T(8,128)(2,1)}), bf16[8,32,384]{2,1,0:T(8,128)(2,1)S(1)}, u32[]{:S(2)}, u32[]{:S(2)}) %all-to-all-start) | async-done | bytes 196640 | tf_op jit(solution)/shard_map/all_to_all | solution.py:683
  52.1 14.9 %all-gather.6.cloned.1.call-done = bf16[2048,1024]{1,0:T(8,128)(2,1)} async-done(((bf16[256,1024]{1,0:T(8,128)(2,1)}), bf16[2048,1024]{1,0:T(8,128)(2,1)}) %all-gather.6.cloned.1.call-update) | async-done | bytes 4194320 | tf_op jit(solution)/shard_map/all_gather | solution.py:679
  67.1 5.7 %convolution_convert_fusion.3 = bf16[2048,384]{1,0:T(8,128)(2,1)} fusion(bf16[2048,1024]{1,0:T(8,128)(2,1)} %all-gather.6.cloned.1.call-done, bf16[1024,384]{1,0:T(8,128)(2,1)S(1)} %bitcast.204), kind=kOutput, calls=%fused_computation.14 | convolution fusion | flops 1611399168 | bytes 6553600 | tf_op jit(solution)/shard_map/dot_general | solution.py:44
  74.3 20.1 %self_forward.1 = (bf16[2048,128]{1,0:T(8,128)(2,1)S(1)}, f32[2,8,2048]{2,1,0:T(8,128)S(1)}) custom-call(s32[1,2]{1,0:T(1,128)S(1)} %copy-done.29, bf16[2048,128]{1,0:T(8,128)(2,1)S(1)} %get-tuple-element.341.q_ref, bf16[2048,128]{1,0:T(8,128)(2,1)S(1)} %get-tuple-element.340.k_ref, bf16[2048,128]{1,0:T(8,128)(2,1)S(1)} %get-tuple-element.339.v_ref), custom_call_target="tpu_custom_call" | custom-call | flops 2147483648 | bytes 2097152 | tf_op jit(solution)/shard_map/self_forward/pallas_call | solution.py:137
  104.7 19.8 %all-to-all-done.1 = bf16[8,256,128]{1,2,0:T(8,128)(2,1)S(1)} async-done(((bf16[8,256,128]{1,2,0:T(8,128)(2,1)}), bf16[8,256,128]{1,2,0:T(8,128)(2,1)S(1)}, u32[]{:S(2)}, u32[]{:S(2)}) %all-to-all-start.1) | async-done | bytes 524320 | tf_op jit(solution)/shard_map/all_to_all | solution.py:714
  161.4 11.7 %collective-permute-done.13.refs_2_ = bf16[2,512,256]{2,1,0:T(8,128)(2,1)S(1)} collective-permute-done((bf16[2,512,256]{2,1,0:T(8,128)(2,1)}, bf16[2,512,256]{2,1,0:T(8,128)(2,1)S(1)}, u32[]{:S(2)}, u32[]{:S(2)}) %collective-permute-start.13) | collective-permute-done | bytes 524320 | tf_op jit(solution)/shard_map/ppermute | solution.py:370
  190.3 11.0 %cross_forward.1 = (bf16[256,1024]{1,0:T(8,128)(2,1)S(1)}, f32[16,8,256]{2,1,0:T(8,128)S(1)}) custom-call(bf16[256,1024]{1,0:T(8,128)(2,1)S(1)} %fusion.17.q.q_ref, bf16[2,1024,1024]{2,1,0:T(8,128)(2,1)S(1)} %pad_maximum_fusion.1.k.v.k_ref.v_ref, bf16[2,1024,1024]{2,1,0:T(8,128)(2,1)S(1)} %pad_maximum_fusion.1.k.v.k_ref.v_ref), custom_call_target="tpu_custom_call" | custom-call | flops 1073741824 | bytes 5242880 | tf_op jit(solution)/shard_map/cross_forward/pallas_call | solution.py:282
  211.1 11.6 %collective-permute-done.24 = bf16[256,1024]{1,0:T(8,128)(2,1)} collective-permute-done((bf16[256,1024]{1,0:T(8,128)(2,1)}, bf16[256,1024]{1,0:T(8,128)(2,1)}, u32[]{:S(2)}, u32[]{:S(2)}) %collective-permute-start.24) | collective-permute-done | bytes 524320 | tf_op jit(solution)/shard_map/ppermute | solution.py:370
  222.7 10.1 %collective-permute-done.25 = bf16[256,1024]{1,0:T(8,128)(2,1)} collective-permute-done((bf16[256,1024]{1,0:T(8,128)(2,1)}, bf16[256,1024]{1,0:T(8,128)(2,1)}, u32[]{:S(2)}, u32[]{:S(2)}) %collective-permute-start.25) | collective-permute-done | bytes 524320 | tf_op jit(solution)/shard_map/ppermute | solution.py:370
  233.9 13.6 %add_convert_fusion = (bf16[1024,2048]{1,0:T(8,128)(2,1)}, bf16[1024,2048]{1,0:T(8,128)(2,1)S(1)}) fusion(bf16[1024,2048]{1,0:T(8,128)(2,1)} %all-gather.14.cloned.1.call-done, bf16[256,1024]{1,0:T(8,128)(2,1)} %collective-permute-done.26, bf16[256,1024]{1,0:T(8,128)(2,1)} %collective-permute-done.25, bf16[256,1024]{1,0:T(8,128)(2,1)} %collective-permute-done.24, ...), kind=kOutput, calls=%fused_computation.1 | convolution fusion | flops 4343201792 | bytes 14680064 | tf_op jit(solution)/shard_map/dot_general | solution.py:44
  249.5 6.2 %convolution_convert_fusion.2 = bf16[2048,1024]{1,0:T(8,128)(2,1)} fusion(bf16[1024,2048]{1,0:T(8,128)(2,1)S(1)} %get-tuple-element.195, bf16[1024,1024]{1,0:T(8,128)(2,1)S(1)} %copy-done.53), kind=kOutput, calls=%fused_computation.11 | convolution fusion | flops 4297064448 | bytes 10485760 | tf_op jit(solution)/shard_map/dot_general | solution.py:52
  255.8 9.0 %multiply_convert_fusion = bf16[1024,2048]{1,0:T(8,128)(2,1)S(1)} fusion(bf16[1024,2048]{1,0:T(8,128)(2,1)} %get-tuple-element.193, bf16[1024,1024]{1,0:T(8,128)(2,1)} %pad_maximum_fusion.2, bf16[2048,1024]{1,0:T(8,128)(2,1)} %all-gather.12.cloned.1.call-done), kind=kOutput, calls=%fused_computation | convolution fusion | flops 4301258752 | bytes 14680064 | tf_op jit(solution)/shard_map/dot_general | solution.py:48
  280.5 7.7 %convolution_convert_fusion.1 = bf16[1024,2048]{1,0:T(8,128)(2,1)} fusion(bf16[1024,2048]{1,0:T(8,128)(2,1)S(1)} %multiply_convert_fusion, bf16[256,1024]{1,0:T(8,128)(2,1)} %collective-permute-done.26, bf16[256,1024]{1,0:T(8,128)(2,1)} %collective-permute-done.25, bf16[256,1024]{1,0:T(8,128)(2,1)} %collective-permute-done.24, ...), kind=kOutput, calls=%fused_computation.10 | convolution fusion | flops 4305453056 | bytes 10485760 | tf_op jit(solution)/shard_map/dot_general | solution.py:52
  288.2 8.4 %collective-permute-done.28 = bf16[256,1024]{1,0:T(8,128)(2,1)} collective-permute-done((bf16[256,1024]{1,0:T(8,128)(2,1)}, bf16[256,1024]{1,0:T(8,128)(2,1)}, u32[]{:S(2)}, u32[]{:S(2)}) %collective-permute-start.28) | collective-permute-done | bytes 524320 | tf_op jit(solution)/shard_map/ppermute | solution.py:370
  309.1 17.3 %cross_backward.1 = (bf16[256,1024]{1,0:T(8,128)(2,1)S(1)}, bf16[8,2,1024,128]{3,2,1,0:T(8,128)(2,1)}) custom-call(bf16[256,1024]{1,0:T(8,128)(2,1)S(1)} %fusion.17.q.q_ref, bf16[2,1024,1024]{2,1,0:T(8,128)(2,1)} %copy-done, bf16[2,1024,1024]{2,1,0:T(8,128)(2,1)} %copy-done, bf16[256,1024]{1,0:T(8,128)(2,1)S(1)} %get-tuple-element.184.o_ref, ...), custom_call_target="tpu_custom_call" | custom-call | flops 2684354560 | bytes 10485760 | tf_op jit(solution)/shard_map/cross_backward/pallas_call | solution.py:340
  363.3 14.1 %adam.4 = (f32[1024,1024]{1,0:T(8,128)}, f32[1024,1024]{1,0:T(8,128)}, f32[1024,1024]{1,0:T(8,128)}, f32[1024,1024]{1,0:T(8,128)}) custom-call(bf16[1024,1024]{1,0:T(8,128)(2,1)S(1)} %bitcast.193, f32[1024,1024]{1,0:T(8,128)} %w_ref.2, f32[1024,1024]{1,0:T(8,128)} %m1_ref.2, f32[1024,1024]{1,0:T(8,128)} %m2_ref.2), custom_call_target="tpu_custom_call" | custom-call | flops 20971520 | bytes 31457280 | tf_op jit(solution)/shard_map/adam/pallas_call | solution.py:615
  380.5 23.8 %self_backward.1 = bf16[2048,384]{1,0:T(8,128)(2,1)S(1)} custom-call(s32[1,2]{1,0:T(1,128)S(1)} %copy-done.29, bf16[2048,128]{1,0:T(8,128)(2,1)S(1)} %copy-done.28, bf16[2048,128]{1,0:T(8,128)(2,1)S(1)} %copy-done.26, bf16[2048,128]{1,0:T(8,128)(2,1)S(1)} %copy-done.24, bf16[2048,128]{1,0:T(8,128)(2,1)S(1)} %copy-done.22, bf16[2048,128]{1,0:T(8,128)(2,1)S(1)} %bitcast.207, ...), custom_call_target="tpu_custom_call" | custom-call | flops 5368709120 | bytes 4194304 | tf_op jit(solution)/shard_map/self_backward/pallas_call | solution.py:238
  417.0 7.0 %collective-permute-done.39 = bf16[256,1024]{1,0:T(8,128)(2,1)} collective-permute-done((bf16[256,1024]{1,0:T(8,128)(2,1)}, bf16[256,1024]{1,0:T(8,128)(2,1)}, u32[]{:S(2)}, u32[]{:S(2)}) %collective-permute-start.39) | collective-permute-done | bytes 524320 | tf_op jit(solution)/shard_map/ppermute | solution.py:370
  443.2 6.0 %collective-permute-done.40 = bf16[3,32,1024]{2,1,0:T(8,128)(2,1)} collective-permute-done((bf16[3,32,1024]{2,1,0:T(8,128)(2,1)}, bf16[3,32,1024]{2,1,0:T(8,128)(2,1)}, u32[]{:S(2)}, u32[]{:S(2)}) %collective-permute-start.40) | collective-permute-done | bytes 196640 | tf_op jit(solution)/shard_map/ppermute | solution.py:370
  466.2 6.1 %collective-permute-done.46 = bf16[3,32,1024]{2,1,0:T(8,128)(2,1)S(1)} collective-permute-done((bf16[3,32,1024]{2,1,0:T(8,128)(2,1)}, bf16[3,32,1024]{2,1,0:T(8,128)(2,1)S(1)}, u32[]{:S(2)}, u32[]{:S(2)}) %collective-permute-start.46) | collective-permute-done | bytes 196640 | tf_op jit(solution)/shard_map/ppermute | solution.py:370
  472.7 8.7 %collective-permute-done.44.refs_2_ = bf16[2,32,640]{2,1,0:T(8,128)(2,1)S(1)} collective-permute-done((bf16[2,32,640]{2,1,0:T(8,128)(2,1)S(1)}, bf16[2,32,640]{2,1,0:T(8,128)(2,1)S(1)}, u32[]{:S(2)}, u32[]{:S(2)}) %collective-permute-start.44) | collective-permute-done | bytes 81952 | tf_op jit(solution)/shard_map/ppermute | solution.py:370
  489.9 13.8 %adam.5 = (f32[128,8192]{1,0:T(8,128)}, f32[128,8192]{1,0:T(8,128)}, f32[128,8192]{1,0:T(8,128)}, f32[128,8192]{1,0:T(8,128)}) custom-call(bf16[128,8192]{1,0:T(8,128)(2,1)S(1)} %join_natural.1.g_ref, f32[128,8192]{1,0:T(8,128)} %w_ref.3, f32[128,8192]{1,0:T(8,128)} %m1_ref.3, f32[128,8192]{1,0:T(8,128)} %m2_ref.3), custom_call_target="tpu_custom_call" | custom-call | flops 20971520 | bytes 31457280 | tf_op jit(solution)/shard_map/adam/pallas_call | solution.py:615
  503.7 8.6 %collective-permute-done.48.refs_2_ = bf16[8,32,1024]{2,1,0:T(8,128)(2,1)S(1)} collective-permute-done((bf16[8,32,1024]{2,1,0:T(8,128)(2,1)S(1)}, bf16[8,32,1024]{2,1,0:T(8,128)(2,1)S(1)}, u32[]{:S(2)}, u32[]{:S(2)}) %collective-permute-start.48) | collective-permute-done | bytes 524320 | tf_op jit(solution)/shard_map/ppermute | solution.py:370
  526.9 9.6 %adam.6 = (f32[768,1024]{1,0:T(8,128)}, f32[768,1024]{1,0:T(8,128)}, f32[768,1024]{1,0:T(8,128)}, f32[768,1024]{1,0:T(8,128)}) custom-call(bf16[768,1024]{1,0:T(8,128)(2,1)S(1)} %bitcast.197, f32[768,1024]{1,0:T(8,128)S(1)} %bitcast.196, f32[768,1024]{1,0:T(8,128)} %bitcast.216, f32[768,1024]{1,0:T(8,128)} %bitcast.217), custom_call_target="tpu_custom_call" | custom-call | flops 15728640 | bytes 23592960 | tf_op jit(solution)/shard_map/adam/pallas_call | solution.py:615
  (432 shorter events, 267.2 us)
Async XLA Ops:
  7.2 59.8 %all-gather.6.cloned.1.call-start = ((), (), s32[]{:S(2)}) async-start(), calls=%async_computation.10 | async-start | bytes 4718592 | tf_op jit(solution)/shard_map/all_gather | solution.py:679
  12.8 29.4 %collective-permute-start.3 = (bf16[256,1024]{1,0:T(8,128)(2,1)}, bf16[256,1024]{1,0:T(8,128)(2,1)S(1)}, u32[]{:S(2)}, u32[]{:S(2)}) collective-permute-start(bf16[256,1024]{1,0:T(8,128)(2,1)} %param.22), channel_id=1, source_target_pairs={{0,8},{8,0},{16,24},{24,16},{1,9},{9,1},{17,25},{25,17},{2,10},{10... | collective-permute-start | bytes 1572872 | tf_op jit(solution)/shard_map/ppermute | solution.py:370
  15.8 32.8 %collective-permute-start.4 = (bf16[256,1024]{1,0:T(8,128)(2,1)}, bf16[256,1024]{1,0:T(8,128)(2,1)}, u32[]{:S(2)}, u32[]{:S(2)}) collective-permute-start(bf16[256,1024]{1,0:T(8,128)(2,1)} %param.22), channel_id=1, source_target_pairs={{0,16},{8,24},{16,0},{24,8},{1,17},{9,25},{17,1},{25,9},{2,18},{10... | collective-permute-start | bytes 1572872 | tf_op jit(solution)/shard_map/ppermute | solution.py:370
  17.4 31.3 %collective-permute-start.5 = (bf16[256,1024]{1,0:T(8,128)(2,1)}, bf16[256,1024]{1,0:T(8,128)(2,1)}, u32[]{:S(2)}, u32[]{:S(2)}) collective-permute-start(bf16[256,1024]{1,0:T(8,128)(2,1)} %param.22), channel_id=1, source_target_pairs={{0,24},{8,16},{16,8},{24,0},{1,25},{9,17},{17,9},{25,1},{2,26},{10... | collective-permute-start | bytes 1572872 | tf_op jit(solution)/shard_map/ppermute | solution.py:370
  25.5 73.6 %all-gather.8.cloned.1.call-start = ((), (), s32[]{:S(2)}) async-start(), calls=%async_computation.11 | async-start | bytes 1769472 | tf_op jit(solution)/shard_map/all_gather | solution.py:708
  67.0 74.2 %all-gather.10.cloned.1.call-start = ((), (), s32[]{:S(2)}) async-start(), calls=%async_computation.12 | async-start | bytes 3538944 | tf_op jit(solution)/shard_map/all_gather | solution.py:710
  72.8 138.3 %all-gather.14.cloned.1.call-start = ((), (), s32[]{:S(2)}) async-start(), calls=%async_computation.14 | async-start | bytes 4718592 | tf_op jit(solution)/shard_map/all_gather | solution.py:713
  95.5 29.0 %all-to-all-start.1 = ((bf16[8,256,128]{1,2,0:T(8,128)(2,1)}), bf16[8,256,128]{1,2,0:T(8,128)(2,1)S(1)}, u32[]{:S(2)}, u32[]{:S(2)}) async-start(bf16[8,256,128]{1,2,0:T(8,128)(2,1)} %copy.82), calls=%async_computation.1 | async-start | bytes 1048576 | tf_op jit(solution)/shard_map/all_to_all | solution.py:714
  99.0 156.8 %all-gather.12.cloned.1.call-start = ((), (), s32[]{:S(2)}) async-start(), calls=%async_computation.13 | async-start | bytes 4718592 | tf_op jit(solution)/shard_map/all_gather | solution.py:720
  102.7 25.3 %collective-permute-start.7 = (bf16[2,512,256]{2,1,0:T(8,128)(2,1)}, bf16[2,512,256]{2,1,0:T(8,128)(2,1)S(1)}, u32[]{:S(2)}, u32[]{:S(2)}) collective-permute-start(bf16[2,512,256]{2,1,0:T(8,128)(2,1)} %constant_dynamic-slice_fusion.2), channel_id=1, source_target_pairs={{0,16},{8,24},{16,0},{24,8},{1,17},{9,25},{17,1},{25,9},{2,18},{10... | collective-permute-start | bytes 1572872 | tf_op jit(solution)/shard_map/ppermute | solution.py:370
  128.7 175.1 %reduce-scatter.6.cloned.1.call-start = ((), (), s32[]{:S(2)}) async-start(), calls=%async_computation.15 | async-start | bytes 4718592 | tf_op jit(solution)/shard_map/reduce_scatter | solution.py:749
  147.9 25.2 %collective-permute-start.13 = (bf16[2,512,256]{2,1,0:T(8,128)(2,1)}, bf16[2,512,256]{2,1,0:T(8,128)(2,1)S(1)}, u32[]{:S(2)}, u32[]{:S(2)}) collective-permute-start(bf16[2,512,256]{2,1,0:T(8,128)(2,1)} %constant_dynamic-slice_fusion.1), channel_id=1, source_target_pairs={{0,16},{8,24},{16,0},{24,8},{1,17},{9,25},{17,1},{25,9},{2,18},{10... | collective-permute-start | bytes 1572872 | tf_op jit(solution)/shard_map/ppermute | solution.py:370
  255.7 121.6 %reduce-scatter.10.cloned.1.call-start = ((), (), s32[]{:S(2)}) async-start(), calls=%async_computation.17 | async-start | bytes 4718592 | tf_op jit(solution)/shard_map/reduce_scatter | solution.py:758
  272.2 24.4 %collective-permute-start.28 = (bf16[256,1024]{1,0:T(8,128)(2,1)}, bf16[256,1024]{1,0:T(8,128)(2,1)}, u32[]{:S(2)}, u32[]{:S(2)}) collective-permute-start(bf16[256,1024]{1,0:T(8,128)(2,1)} %get-tuple-element.336), channel_id=1, source_target_pairs={{0,16},{8,24},{16,0},{24,8},{1,17},{9,25},{17,1},{25,9},{2,18},{10... | collective-permute-start | bytes 1572872 | tf_op jit(solution)/shard_map/ppermute | solution.py:370
  296.7 127.3 %reduce-scatter.8.cloned.1.call-start = ((), (), s32[]{:S(2)}) async-start(), calls=%async_computation.16 | async-start | bytes 4718592 | tf_op jit(solution)/shard_map/reduce_scatter | solution.py:771
  303.8 24.6 %collective-permute-start.30 = (bf16[256,1024]{1,0:T(8,128)(2,1)}, bf16[256,1024]{1,0:T(8,128)(2,1)S(1)}, u32[]{:S(2)}, u32[]{:S(2)}) collective-permute-start(bf16[256,1024]{1,0:T(8,128)(2,1)} %reduce-scatter.6.cloned.1.call-done.refs_0_), channel_id=1, source_target_pairs={{0,8},{8,0},{16,24},{24,16},{1,9},{9,1},{17,25},{25,17},{2,10},{10... | collective-permute-start | bytes 1572872 | tf_op jit(solution)/shard_map/ppermute | solution.py:370
  349.2 28.1 %all-to-all-start.2 = ((bf16[8,256,128]{2,1,0:T(8,128)(2,1)}), bf16[8,256,128]{2,1,0:T(8,128)(2,1)S(1)}, u32[]{:S(2)}, u32[]{:S(2)}) async-start(bf16[8,256,128]{2,1,0:T(8,128)(2,1)} %bitcast_bitcast_fusion), calls=%async_computation.4 | async-start | bytes 1048576 | tf_op jit(solution)/shard_map/all_to_all | solution.py:784
  352.7 161.2 %reduce-scatter.12.cloned.1.call-start = ((), (), s32[]{:S(2)}) async-start(), calls=%async_computation.18 | async-start | bytes 4718592 | tf_op jit(solution)/shard_map/reduce_scatter | solution.py:818
  360.6 43.6 %collective-permute-start.37 = (bf16[3,4,32,1024]{3,2,1,0:T(8,128)(2,1)}, bf16[3,4,32,1024]{3,2,1,0:T(8,128)(2,1)}, u32[]{:S(2)}, u32[]{:S(2)}) collective-permute-start(bf16[3,4,32,1024]{3,2,1,0:T(8,128)(2,1)} %get-tuple-element.232), channel_id=1, source_target_pairs={{0,16},{8,24},{16,0},{24,8},{1,17},{9,25},{17,1},{25,9},{2,18},{10... | collective-permute-start | bytes 2359304 | tf_op jit(solution)/shard_map/ppermute | solution.py:370
  362.0 42.3 %collective-permute-start.38 = (bf16[3,4,32,1024]{3,2,1,0:T(8,128)(2,1)}, bf16[3,4,32,1024]{3,2,1,0:T(8,128)(2,1)}, u32[]{:S(2)}, u32[]{:S(2)}) collective-permute-start(bf16[3,4,32,1024]{3,2,1,0:T(8,128)(2,1)} %get-tuple-element.233), channel_id=1, source_target_pairs={{0,24},{8,16},{16,8},{24,0},{1,25},{9,17},{17,9},{25,1},{2,26},{10... | collective-permute-start | bytes 2359304 | tf_op jit(solution)/shard_map/ppermute | solution.py:370
  451.7 29.7 %all-to-all-start.4 = ((bf16[4,128,2048]{2,1,0:T(8,128)(2,1)}), bf16[4,128,2048]{2,1,0:T(8,128)(2,1)S(1)}, u32[]{:S(2)}, u32[]{:S(2)}) async-start(bf16[4,128,2048]{2,1,0:T(8,128)(2,1)} %broadcast_in_dim.40), calls=%async_computation.8 | async-start | bytes 4194304 | tf_op jit(solution)/shard_map/all_to_all | solution.py:584
  456.0 80.6 %reduce-scatter.14.cloned.1.call-start = ((), (), s32[]{:S(2)}) async-start(), calls=%async_computation.19 | async-start | bytes 2359296 | tf_op jit(solution)/shard_map/reduce_scatter | solution.py:841
  487.5 24.9 %collective-permute-start.48 = (bf16[8,32,1024]{2,1,0:T(8,128)(2,1)S(1)}, bf16[8,32,1024]{2,1,0:T(8,128)(2,1)S(1)}, u32[]{:S(2)}, u32[]{:S(2)}) collective-permute-start(bf16[8,32,1024]{2,1,0:T(8,128)(2,1)S(1)} %pad_maximum_fusion.6.refs_0_), channel_id=1, source_target_pairs={{0,16},{8,24},{16,0},{24,8},{1,17},{9,25},{17,1},{25,9},{2,18},{10... | collective-permute-start | bytes 1572872 | tf_op jit(solution)/shard_map/ppermute | solution.py:370
  489.0 24.2 %collective-permute-start.49 = (bf16[8,32,1024]{2,1,0:T(8,128)(2,1)S(1)}, bf16[8,32,1024]{2,1,0:T(8,128)(2,1)S(1)}, u32[]{:S(2)}, u32[]{:S(2)}) collective-permute-start(bf16[8,32,1024]{2,1,0:T(8,128)(2,1)S(1)} %pad_maximum_fusion.6.refs_0_), channel_id=1, source_target_pairs={{0,24},{8,16},{16,8},{24,0},{1,25},{9,17},{17,9},{25,1},{2,26},{10... | collective-permute-start | bytes 1572872 | tf_op jit(solution)/shard_map/ppermute | solution.py:370
  (129 other events, 1431.9 us)
Sparse Core Ops, SparseCore 0:
  12.9 54.0 all-gather.5
  69.2 23.7 all-gather.7
  95.2 46.0 all-gather.9
  143.3 45.9 all-gather.13
  191.3 45.8 all-gather.11
  255.9 47.8 reduce-scatter.5
  306.6 48.1 reduce-scatter.9
  357.7 47.0 reduce-scatter.7
  409.9 63.1 reduce-scatter.11
  481.5 35.5 reduce-scatter.13
